TPU v7x, 512 devices: a whole 4x4x16 slice. The times are simulated.
512 devices in a mesh: dp: 32 (over z_lo, x), mp: 16 (over y, z_hi, core).
Axes of the slice: x: 4, y: 4, z: 16 (z_hi: 2, z_lo: 8; z = z_hi * 8 + z_lo), core: 2. Of those that a mesh axis runs over, the one named last changes fastest.
Arguments:
- patches: bfloat16 [8192, 6144], P('dp', 'mp')
- destination: int32 [8192], P('dp'), may hold values from 0 to 8191, as said below
- segment: int32 [8192], P('dp'), may hold values from 0 to 8191, as said below
- ln_gain: float32 [6144], replicated
- w_query: bfloat16 [6144, 4096], P('dp', 'mp')
- w_key: bfloat16 [6144, 4096], P('dp', 'mp')
- w_value: bfloat16 [6144, 4096], P('dp', 'mp')
- query_gain: float32 [4096], P('mp')
- key_gain: float32 [4096], P('mp')
- attn_cotangent: bfloat16 [8192, 4096], P('dp', 'mp'), may hold values from -6 to 6
Outputs:
- attention: bfloat16 [8192, 4096], P('dp', 'mp')
- grad_packed: bfloat16 [8192, 6144], P('dp', 'mp')
Inputs may be any that keep to these rules, and one draw needn't show every extreme that they name: `destination`: each number appears once. The 256 loader rows of one index of dp place at most 16 rows into any one packed sequence, and exactly 16 into some sequence. `segment`: image ids never fall along the packed rows, and no image crosses the boundary between two packed sequences of 256 rows. Each image has 1 to min(64, 128) patches, and every packed sequence holds one image of exactly that most.
All inputs are finite; a program needn't handle non-finite values.
Results may differ from a plain program's by a relative error of at most 0.023.
The roundings to bfloat16 on the way count: a program that leaves them out, or rounds other values in their place, can miss the bound.
Values may be sent and summed in bfloat16 or wider, within the bound.
No kernel may reach another device: no remote copies, remote signals or barrier semaphores. Data moves between devices by JAX's collectives and lax.ppermute only.
A program may use at most 64 MiB of HBM per device.

v0:
```python
import math

import jax
import jax.numpy as jnp
from jax import lax
from jax.sharding import PartitionSpec as P

D = 6144
DH = 128


EPSILON = 1e-06
NEGATIVE = -1e30


def row_norm(values_in):
    row_mean = jnp.mean(values_in, axis=-1, keepdims=True)
    centred = values_in - row_mean
    row_var = jnp.mean(centred * centred, axis=-1, keepdims=True)
    inverse = lax.rsqrt(row_var + EPSILON)
    return (centred * inverse, inverse)


def norm_back(grad_hat, scaled, inverse):
    first = jnp.mean(grad_hat, axis=-1, keepdims=True)
    second = jnp.mean(grad_hat * scaled, axis=-1, keepdims=True)
    return (grad_hat - first - scaled * second) * inverse


def per_device(
    patches,
    destination,
    segment,
    ln_gain,
    w_query,
    w_key,
    w_value,
    query_gain,
    key_gain,
    attn_cotangent,
):
    seq_rows = patches.shape[0]
    n_groups = lax.axis_size("dp")
    slot_cap = 2 * seq_rows // n_groups
    owners = destination // seq_rows
    offsets = destination % seq_rows
    one_hot = (owners[:, None] == jnp.arange(n_groups)[None, :]).astype(jnp.bfloat16)
    row_index = jnp.arange(seq_rows)
    strict = (row_index[:, None] > row_index[None, :]).astype(jnp.bfloat16)
    earlier = jnp.dot(strict, one_hot, preferred_element_type=jnp.float32)
    slot_rank = jnp.sum(earlier * one_hot.astype(jnp.float32), axis=1).astype(jnp.int32)
    position = owners * slot_cap + slot_rank
    placing = jnp.arange(n_groups * slot_cap)[:, None] == position[None, :]
    send_rows = jnp.dot(
        placing.astype(jnp.bfloat16), patches, preferred_element_type=jnp.float32
    ).astype(jnp.bfloat16)
    send_rows = send_rows.reshape(n_groups, slot_cap, patches.shape[1])
    send_places = jnp.sum(jnp.where(placing, offsets[None, :] + 1, 0), axis=1) - 1
    send_places = send_places.reshape(n_groups, slot_cap)
    got_rows, got_places = (
        lax.all_to_all(send_rows, "dp", split_axis=0, concat_axis=0, tiled=True),
        lax.all_to_all(send_places, "dp", split_axis=0, concat_axis=0, tiled=True),
    )
    got_rows = got_rows.reshape(n_groups * slot_cap, patches.shape[1])
    got_places = got_places.reshape(n_groups * slot_cap)
    unpack = (row_index[:, None] == got_places[None, :]).astype(jnp.bfloat16)
    arrived = jnp.dot(unpack, got_rows, preferred_element_type=jnp.float32).astype(jnp.bfloat16)
    packed = lax.all_gather(arrived, "mp", axis=1, tiled=True)
    x_hat, inverse = row_norm(packed.astype(jnp.float32))
    normed = (x_hat * ln_gain).astype(jnp.bfloat16)
    columns = w_query.shape[1]
    full_query, full_key, full_value = (
        lax.all_gather(w_query, "dp", axis=0, tiled=True),
        lax.all_gather(w_key, "dp", axis=0, tiled=True),
        lax.all_gather(w_value, "dp", axis=0, tiled=True),
    )
    query_raw = jnp.dot(normed, full_query, preferred_element_type=jnp.float32)
    key_raw = jnp.dot(normed, full_key, preferred_element_type=jnp.float32)
    value_raw = jnp.dot(normed, full_value, preferred_element_type=jnp.float32)
    heads_here = columns // DH
    query_hat, query_inv = row_norm(query_raw.reshape(seq_rows, heads_here, DH))
    key_hat, key_inv = row_norm(key_raw.reshape(seq_rows, heads_here, DH))
    qgain = query_gain.reshape(heads_here, DH)
    kgain = key_gain.reshape(heads_here, DH)
    query_norm = (query_hat * qgain).astype(jnp.bfloat16)
    key_norm = (key_hat * kgain).astype(jnp.bfloat16)
    value_half = value_raw.astype(jnp.bfloat16).reshape(seq_rows, heads_here, DH)
    cotangent = attn_cotangent.reshape(seq_rows, heads_here, DH)
    factor = 1.0 / math.sqrt(DH)
    scores = (
        jnp.einsum("qhd,khd->hqk", query_norm, key_norm, preferred_element_type=jnp.float32)
        * factor
    )
    same_image = segment[:, None] == segment[None, :]
    scores = jnp.where(same_image[None, :, :], scores, NEGATIVE)
    row_peak = jnp.max(scores, axis=-1, keepdims=True)
    exp_scores = jnp.exp(scores - row_peak)
    prob_full = exp_scores / jnp.sum(exp_scores, axis=-1, keepdims=True)
    prob_half = prob_full.astype(jnp.bfloat16)
    context = jnp.einsum(
        "hqk,khd->qhd", prob_half, value_half, preferred_element_type=jnp.float32
    ).astype(jnp.bfloat16)
    grad_prob = jnp.einsum(
        "qhd,khd->hqk", cotangent, value_half, preferred_element_type=jnp.float32
    )
    row_delta = jnp.sum(prob_full * grad_prob, axis=-1, keepdims=True)
    grad_score = (prob_full * (grad_prob - row_delta) * factor).astype(jnp.bfloat16)
    query_side = jnp.einsum(
        "hqk,khd->qhd", grad_score, key_norm, preferred_element_type=jnp.float32
    )
    key_side = jnp.einsum(
        "hqk,qhd->khd", grad_score, query_norm, preferred_element_type=jnp.float32
    )
    value_grad = jnp.einsum(
        "hqk,qhd->khd", prob_half, cotangent, preferred_element_type=jnp.float32
    ).astype(jnp.bfloat16)
    query_grad = (
        norm_back(query_side * qgain, query_hat, query_inv)
        .astype(jnp.bfloat16)
        .reshape(seq_rows, columns)
    )
    key_grad = (
        norm_back(key_side * kgain, key_hat, key_inv)
        .astype(jnp.bfloat16)
        .reshape(seq_rows, columns)
    )
    value_grad = value_grad.reshape(seq_rows, columns)
    contract = (((1,), (1,)), ((), ()))
    partial_term = lax.dot_general(
        query_grad, full_query, contract, preferred_element_type=jnp.float32
    )
    partial_term = partial_term + lax.dot_general(
        key_grad, full_key, contract, preferred_element_type=jnp.float32
    )
    partial_term = partial_term + lax.dot_general(
        value_grad, full_value, contract, preferred_element_type=jnp.float32
    )
    shard = lax.psum_scatter(
        partial_term.astype(jnp.bfloat16), "mp", scatter_dimension=1, tiled=True
    ).astype(jnp.float32)
    width_here = shard.shape[1]
    start_here = lax.axis_index("mp") * width_here
    gain_here = lax.dynamic_slice_in_dim(ln_gain, start_here, width_here, 0)
    centred_here = lax.dynamic_slice_in_dim(x_hat, start_here, width_here, 1)
    scaled_here = shard * gain_here
    sums_first = jnp.sum(scaled_here, axis=1)
    sums_second = jnp.sum(scaled_here * centred_here, axis=1)
    total_first, total_second = lax.psum((sums_first, sums_second), "mp")
    mean_first = total_first[:, None] / D
    mean_second = total_second[:, None] / D
    grad_packed = ((shard * gain_here - mean_first - centred_here * mean_second) * inverse).astype(
        jnp.bfloat16
    )
    return (context.reshape(seq_rows, columns), grad_packed)


def solution(mesh):
    placed = (
        P("dp", "mp"),
        P("dp"),
        P("dp"),
        P(),
        P("dp", "mp"),
        P("dp", "mp"),
        P("dp", "mp"),
        P("mp"),
        P("mp"),
        P("dp", "mp"),
    )
    return jax.shard_map(
        per_device,
        mesh=mesh,
        in_specs=placed,
        out_specs=(P("dp", "mp"), P("dp", "mp")),
        check_vma=False,
    )
```

profile of v0, /device:TPU:1, one launch (start us, length us, event | category | flops | bytes accessed | tf_op | source)
XLA Modules:
  0.0 1074.9 jit_solution(15558009116337659157)
XLA Ops:
  7.2 0.7 fusion.31
  7.9 0.2 fusion.15
  8.1 0.1 select_reduce_fusion
  8.3 0.7 sub.87
  9.0 15.9 %all-to-all-start = ((s32[32,1,16]{2,1,0:T(1,128)}), s32[32,1,16]{2,1,0:T(1,128)S(1)}, u32[]{:S(2)}, u32[]{:S(2)}) async-start(s32[32,1,16]{2,1,0:T(1,128)} %bitcast), calls=%async_computation | async-start | bytes 32768 | tf_op jit(solution)/shard_map/all_to_all | solution.py:62
  24.9 1.1 convolution_convert_fusion
  26.0 10.3 all-to-all-done
  36.3 3.9 all-to-all-start.1
  40.2 0.0 all-gather.5.cloned.1.call-start
  40.2 0.5 broadcast.217
  40.7 0.7 reduce.3
  41.4 0.1 eq.67
  41.5 18.7 %all-to-all-done.1 = bf16[32,16,384]{2,1,0:T(8,128)(2,1)S(1)} async-done(((bf16[32,16,384]{2,1,0:T(8,128)(2,1)}), bf16[32,16,384]{2,1,0:T(8,128)(2,1)S(1)}, u32[]{:S(2)}, u32[]{:S(2)}) %all-to-all-start.1) | async-done | bytes 393248 | tf_op jit(solution)/shard_map/all_to_all | solution.py:61
  60.2 1.0 convolution_convert_fusion.1
  61.2 0.0 all-gather.11.cloned.1.call-start
  61.2 0.7 all-gather.11.cloned.1.call-update
  62.0 0.0 all-gather.9.cloned.1.call-start
  62.0 0.7 all-gather.9.cloned.1.call-update
  62.7 0.0 all-gather.7.cloned.1.call-start
  62.7 0.5 all-gather.7.cloned.1.call-update
  63.3 0.0 reduce-scatter.4.cloned.1.call-start
  63.3 1.7 copy.63
  65.0 0.9 broadcast_compare_fusion
  65.8 101.4 %all-gather.5.cloned.1.call-done = bf16[256,6144]{1,0:T(8,128)(2,1)} async-done(((bf16[256,384]{1,0:T(8,128)(2,1)}), bf16[256,6144]{1,0:T(8,128)(2,1)}) %all-gather.5.cloned.1.call-update) | async-done | bytes 3145744 | tf_op jit(solution)/shard_map/all_gather | solution.py:68
  167.3 2.5 convert_reduce_fusion
  169.8 0.3 copy-done.1
  170.1 1.0 fusion.5
  171.1 4.2 fusion.3
  175.3 190.1 %all-gather.11.cloned.1.call-done = bf16[6144,256]{1,0:T(8,128)(2,1)} async-done(((bf16[192,256]{1,0:T(8,128)(2,1)}), bf16[6144,256]{1,0:T(8,128)(2,1)}) %all-gather.11.cloned.1.call-update) | async-done | bytes 3145744 | tf_op jit(solution)/shard_map/all_gather | solution.py:74
  365.4 3.2 bitcast_reduce_fusion
  368.7 0.7 copy-done.5
  369.4 222.4 %all-gather.9.cloned.1.call-done = bf16[6144,256]{1,0:T(8,128)(2,1)} async-done(((bf16[192,256]{1,0:T(8,128)(2,1)}), bf16[6144,256]{1,0:T(8,128)(2,1)}) %all-gather.9.cloned.1.call-update) | async-done | bytes 3145744 | tf_op jit(solution)/shard_map/all_gather | solution.py:73
  591.8 3.2 bitcast_reduce_fusion.1
  595.1 0.7 copy-done.7
  595.8 222.2 %all-gather.7.cloned.1.call-done = bf16[6144,256]{1,0:T(8,128)(2,1)} async-done(((bf16[192,256]{1,0:T(8,128)(2,1)}), bf16[6144,256]{1,0:T(8,128)(2,1)}) %all-gather.7.cloned.1.call-update) | async-done | bytes 3145744 | tf_op jit(solution)/shard_map/all_gather | solution.py:75
  818.0 3.3 convolution_convert_fusion.4
  821.3 1.1 convolution_bitcast_fusion
  822.4 0.1 multiply_convert_fusion.4
  822.6 1.2 fusion.41
  823.7 2.1 convolution_convert_fusion.2
  825.9 3.4 fusion.40
  829.3 3.2 fusion.39
  832.6 0.7 broadcast_multiply_fusion.1
  833.2 0.7 broadcast_multiply_fusion.3
  833.9 0.7 broadcast_multiply_fusion.2
  834.6 0.7 broadcast_multiply_fusion
  835.2 1.1 multiply_convert_fusion.3
  836.3 1.1 multiply_convert_fusion.2
  837.5 1.0 fusion.46
  838.5 0.8 copy-done.4
  839.3 1.2 convolution_add_fusion.1
  840.5 0.7 copy-done.3
  841.2 1.0 fusion.2
  842.3 2.9 copy.61
  845.2 0.8 dynamic_slice.6
  846.0 0.0 copy-done.12
  846.0 0.1 copy-done.14
  846.1 0.6 convolution_convert_fusion.3
  846.7 0.8 copy.53
  847.5 153.3 %reduce-scatter.4.cloned.1.call-done = bf16[384,256]{1,0:T(8,128)(2,1)} async-done(((bf16[6144,256]{1,0:T(8,128)(2,1)}), bf16[384,256]{1,0:T(8,128)(2,1)}) %reduce-scatter.4.cloned.1.call-update) | async-done | bytes 196624
  1000.8 1.1 copy.62
  1001.8 1.2 fusion.20
  1003.0 63.5 %all-reduce = (f32[256]{0:T(256)S(1)}, f32[256]{0:T(256)S(1)}) all-reduce(f32[256]{0:T(256)S(1)} %get-tuple-element.15, f32[256]{0:T(256)S(1)} %get-tuple-element.14), channel_id=1, replica_groups=mesh['dp'=32,'mp'=16] {'mp'}, use_global_device_ids=true, to_apply=%region_19.20 | all-reduce | flops 512 | bytes 4096 | tf_op jit(solution)/shard_map/psum | solution.py:148
  1066.5 1.9 multiply_convert_fusion.1
  (51 shorter events, 0.3 us)
Async XLA Ops:
  7.2 17.7 %copy-start = (bf16[256,384]{1,0:T(8,128)(2,1)S(1)}, bf16[256,384]{1,0:T(8,128)(2,1)}, u32[]{:S(2)}) copy-start(bf16[256,384]{1,0:T(8,128)(2,1)} %param.10) | copy-start | bytes 589828
  9.0 27.3 %all-to-all-start = ((s32[32,1,16]{2,1,0:T(1,128)}), s32[32,1,16]{2,1,0:T(1,128)S(1)}, u32[]{:S(2)}, u32[]{:S(2)}) async-start(s32[32,1,16]{2,1,0:T(1,128)} %bitcast), calls=%async_computation | async-start | bytes 32768 | tf_op jit(solution)/shard_map/all_to_all | solution.py:62
  36.3 23.9 %all-to-all-start.1 = ((bf16[32,16,384]{2,1,0:T(8,128)(2,1)}), bf16[32,16,384]{2,1,0:T(8,128)(2,1)S(1)}, u32[]{:S(2)}, u32[]{:S(2)}) async-start(bf16[32,16,384]{2,1,0:T(8,128)(2,1)} %bitcast.1), calls=%async_computation.1 | async-start | bytes 786432 | tf_op jit(solution)/shard_map/all_to_all | solution.py:61
  40.2 127.1 %all-gather.5.cloned.1.call-start = ((), (), s32[]{:S(2)}) async-start(), calls=%async_computation.3 | async-start | bytes 3342336 | tf_op jit(solution)/shard_map/all_gather | solution.py:68
  61.2 304.2 %all-gather.11.cloned.1.call-start = ((), (), s32[]{:S(2)}) async-start(), calls=%async_computation.6 | async-start | bytes 3244032 | tf_op jit(solution)/shard_map/all_gather | solution.py:74
  62.0 529.8 %all-gather.9.cloned.1.call-start = ((), (), s32[]{:S(2)}) async-start(), calls=%async_computation.5 | async-start | bytes 3244032 | tf_op jit(solution)/shard_map/all_gather | solution.py:73
  62.7 755.3 %all-gather.7.cloned.1.call-start = ((), (), s32[]{:S(2)}) async-start(), calls=%async_computation.4 | async-start | bytes 3244032 | tf_op jit(solution)/shard_map/all_gather | solution.py:75
  63.3 937.5 %reduce-scatter.4.cloned.1.call-start = ((), (), s32[]{:S(2)}) async-start(), calls=%async_computation.7 | async-start | bytes 3342336
  167.3 2.8 copy-start.1
  167.3 3.8 copy-start.15
  171.1 4.2 copy-start.16
  368.7 0.7 copy-start.5
  595.0 0.7 copy-start.7
  818.0 3.3 copy-start.9
  818.0 4.4 copy-start.6
  818.0 4.4 copy-start.8
  818.0 4.4 copy-start.18
  818.0 4.4 copy-start.19
  822.5 3.3 copy-start.11
  822.6 3.3 copy-start.13
  823.7 2.2 copy-start.20
  825.9 11.6 %copy-start.2 = (bf16[6144,256]{1,0:T(8,128)(2,1)S(1)}, bf16[6144,256]{1,0:T(8,128)(2,1)}, u32[]{:S(2)}) copy-start(bf16[6144,256]{1,0:T(8,128)(2,1)} %all-gather.9.cloned.1.call-done) | copy-start | bytes 9437188
  837.4 1.9 copy-start.4
  839.3 1.9 copy-start.3
  839.3 1.9 copy-start.10
  845.1 0.9 copy-start.12
  845.1 1.0 copy-start.14
  845.1 1.0 copy-start.21
  845.1 221.3 %copy-start.17 = (f32[256]{0:T(256)S(1)}, f32[256]{0:T(256)}, u32[]{:S(2)}) copy-start(f32[256]{0:T(256)} %copy-done.16) | copy-start | bytes 3076
Sparse Core Ops, SparseCore 0:
  61.3 105.8 all-gather.4
  169.3 196.0 all-gather.10
  367.5 224.2 all-gather.8
  593.7 224.2 all-gather.6
  845.3 155.4 reduce-scatter.3
where the time goes:
time: 1080 us; the launch traced here: 1070 us
  waiting for transfers between devices  920 us (85%)
  blocking collectives  63.5 us (6%)
  matrix products  26.8 us (2%)
  starting transfers between devices  20 us (2%)
  other arithmetic  18.3 us (2%)
  between operations  14.1 us (1%)
  local copies, waits for them, and re-layouts  11.9 us (1%)
    all_gather x1, waiting for transfers between devices, per_device(): lax.all_gather(w_query, 'dp', axis=0, tiled=True)  222 us
    all_gather x1, waiting for transfers between devices, per_device(): lax.all_gather(w_value, 'dp', axis=0, tiled=True)  222 us
    all_gather x1, waiting for transfers between devices, per_device(): lax.all_gather(w_key, 'dp', axis=0, tiled=True)  190 us
    unnamed x6, waiting for transfers between devices  155 us
    all_gather x1, waiting for transfers between devices, per_device(): packed = lax.all_gather(arrived, 'mp', axis=1, tiled=True)  101 us
    psum x1, blocking collectives, per_device(): total_first, total_second = lax.psum((sums_first, sums_second), 'mp')  63.5 us
  transfers between devices with their start and end apart: 7, of which 7 were waited for; matrix products, arithmetic and copies ran while one was open for 2% of the time, Pallas kernels for 0%

commit v1 on v0

v1 whole, which is shorter than its diff:
```python
import functools
import math

import jax
import jax.numpy as jnp
from jax import lax
from jax.experimental import pallas as pl
from jax.experimental.pallas import tpu as pltpu
from jax.sharding import Mesh, PartitionSpec as P

D = 6144
DH = 128
LEN = 256
CAP = 16
NZ, NX, NY, NH, NC = 8, 4, 4, 2, 2
SHARD = D // (NY * NH * NC)
BLOCK = D // (NZ * NX)
EPSILON = 1e-06
NEGATIVE = -1e30
BF = jnp.bfloat16
F32 = jnp.float32
FOLD = [0, 2, 4, 6, 7, 5, 3, 1]
Z_RING = [(FOLD[i], FOLD[(i + 1) % NZ]) for i in range(NZ)]
Z_BACK = [(b, a) for a, b in Z_RING]
EARLY = (0, 1, -1, 2, -2)
LATE = (3, -3, 4)
TAIL = 16


def shift(n, k):
    return [(i, (i + k) % n) for i in range(n)]


def core_ring(n):
    return [(i * NC + k, (i + (1, n - 1)[k]) % n * NC + k) for i in range(n) for k in range(NC)]


def after(value, other):
    return value + other[(0,) * other.ndim] * 0


def contract(a, b, dim_a, dim_b):
    return lax.dot_general(
        a, b, (((dim_a,), (dim_b,)), ((), ())), preferred_element_type=F32
    )


def ring_source(place, core, steps, n):
    return lax.rem(place + jnp.where(core == 0, n - steps, steps), n)


def norm_kernel(where_ref, gain_ref, *rest):
    y, zh, c = where_ref[0], where_ref[1], where_ref[2]
    own, others = rest[:NY], rest[NY:NY + 2]
    normed_ref, packed_ref, stat_ref = rest[NY + 2:]
    blocks = []
    for steps in range(NY):
        for flip in range(NH):
            half = lax.rem(zh + flip, NH)
            there = ring_source(y, c, steps, NY) * NH + half
            blocks.append((own[steps], flip, there * NC + c))
            there = ring_source(y, 1 - c, steps, NY) * NH + half
            ref, i = (others[0], 2 * steps + flip) if steps < NY - 1 else (others[1], flip)
            blocks.append((ref, i, there * NC + (1 - c)))
    total = jnp.zeros((1, LEN), F32)
    for ref, i, _ in blocks:
        total = total + jnp.sum(ref[i].astype(F32), axis=0, keepdims=True)
    mean = total / D
    total = jnp.zeros((1, LEN), F32)
    for ref, i, _ in blocks:
        centred = ref[i].astype(F32) - mean
        total = total + jnp.sum(centred * centred, axis=0, keepdims=True)
    inverse = lax.rsqrt(total / D + EPSILON)
    stat_ref[0:1, :] = mean
    stat_ref[1:2, :] = inverse
    for ref, i, index in blocks:
        rows = pl.ds(pl.multiple_of(index * SHARD, SHARD), SHARD)
        value = ref[i]
        packed_ref[rows, :] = value
        normed_ref[rows, :] = (
            (value.astype(F32) - mean) * inverse * gain_ref[rows, :]
        ).astype(BF)


def row_norm(values_in):
    row_mean = jnp.mean(values_in, axis=-1, keepdims=True)
    centred = values_in - row_mean
    row_var = jnp.mean(centred * centred, axis=-1, keepdims=True)
    inverse = lax.rsqrt(row_var + EPSILON)
    return centred * inverse, inverse


def norm_back(grad_hat, scaled, inverse):
    first = jnp.mean(grad_hat, axis=-1, keepdims=True)
    second = jnp.mean(grad_hat * scaled, axis=-1, keepdims=True)
    return (grad_hat - first - scaled * second) * inverse


def weight_blocks(where_ref):
    c, zl, x = where_ref[2], where_ref[3], where_ref[4]
    position = jnp.where(lax.rem(zl, 2) == 0, zl // 2, 7 - zl // 2)
    found = []
    for early, steps in ((True, EARLY), (False, LATE)):
        for off in range(NX):
            x_from = off if early else ring_source(x, c, off, NX)
            for j, step in enumerate(steps):
                p = lax.rem(position - step + NZ, NZ)
                z_from = jnp.where(p < 4, 2 * p, 15 - 2 * p)
                found.append((early, off, j, z_from * NX + x_from))
    return found


def block_rows(block):
    return pl.ds(pl.multiple_of(block * BLOCK, BLOCK), BLOCK)


def first_kernel(where_ref, normed_ref, early_ref, late0_ref, late1_ref, late2_ref,
                 acc_ref, weight_ref, sems):
    late_refs = (late0_ref, late1_ref, late2_ref)
    blocks = weight_blocks(where_ref)
    count = NX * len(EARLY) + (NX - 1) * len(LATE)
    copies = []
    for n in range(2 * NX - 1):
        slot = n * len(EARLY) if n < NX else NX * len(EARLY) + (n - NX) * len(LATE)
        size = len(EARLY) if n < NX else len(LATE)
        source = early_ref.at[n] if n < NX else late_refs[n - NX]
        copy = pltpu.make_async_copy(source, weight_ref.at[slot:slot + size], sems.at[n])
        copy.start()
        copies.append((slot, copy))
    copies = dict(copies)
    for slot in range(count):
        if slot in copies:
            copies[slot].wait()
        part = contract(normed_ref[block_rows(blocks[slot][3]), :], weight_ref[slot], 0, 0)
        if slot == 0:
            acc_ref[...] = part
        else:
            acc_ref[...] += part


def main_kernel(where_ref, gain_ref, stat_ref, seg_row_ref, seg_col_ref, qgain_ref, kgain_ref,
                cot_ref, part_ref, normed_ref, packed_hbm, early_ref, *rest):
    late_refs, rest = rest[:NX], rest[NX:]
    attn_ref, keep_a, keep_b, give_a, give_b = rest[:5]
    weight_ref, rows_ref, packed_ref, acc_ref, grad_ref, sems = rest[5:]
    y, zh, c = where_ref[0], where_ref[1], where_ref[2]
    blocks = weight_blocks(where_ref)
    first_late = NX * len(EARLY)
    final = first_late + (NX - 1) * len(LATE)

    arrived = []
    order = [2 * NX - 1] + list(range(2 * NX - 1))
    for n in order:
        slot = n * len(EARLY) if n < NX else first_late + (n - NX) * len(LATE)
        size = len(EARLY) if n < NX else len(LATE)
        source = early_ref.at[n] if n < NX else late_refs[n - NX]
        copy = pltpu.make_async_copy(source, weight_ref.at[slot:slot + size], sems.at[n])
        copy.start()
        arrived.append((slot, copy))
        if n == 2 * NX - 1:
            for j in range(len(LATE)):
                copy = pltpu.make_async_copy(
                    normed_ref.at[block_rows(blocks[final + j][3]), :],
                    rows_ref.at[j], sems.at[2 * NX + j])
                copy.start()
                arrived.append((-1 - j, copy))
    arrived = dict(arrived)
    packed_copy = pltpu.make_async_copy(packed_hbm, packed_ref, sems.at[2 * NX + len(LATE)])
    packed_copy.start()

    arrived.pop(final).wait()
    for j in range(len(LATE)):
        arrived.pop(-1 - j).wait()
        part = contract(rows_ref[j], weight_ref[final + j], 0, 0)
        if j == 0:
            acc_ref[...] = part_ref[...] + part
        else:
            acc_ref[...] += part

    factor = 1.0 / math.sqrt(DH)
    same = seg_col_ref[...] == seg_row_ref[...]
    width = qgain_ref.shape[1]
    for h in range(width // DH):
        cols = slice(h * DH, (h + 1) * DH)
        qgain, kgain = qgain_ref[:, cols], kgain_ref[:, cols]
        query_hat, query_inv = row_norm(acc_ref[:, h * DH:(h + 1) * DH])
        key_hat, key_inv = row_norm(acc_ref[:, width + h * DH:width + (h + 1) * DH])
        value = acc_ref[:, 2 * width + h * DH:2 * width + (h + 1) * DH].astype(BF)
        query = (query_hat * qgain).astype(BF)
        key = (key_hat * kgain).astype(BF)
        cot = cot_ref[:, cols]
        scores = jnp.where(same, contract(query, key, 1, 1) * factor, NEGATIVE)
        exp_scores = jnp.exp(scores - jnp.max(scores, axis=-1, keepdims=True))
        prob = exp_scores / jnp.sum(exp_scores, axis=-1, keepdims=True)
        prob_half = prob.astype(BF)
        attn_ref[:, cols] = contract(prob_half, value, 1, 0).astype(BF)
        grad_prob = contract(cot, value, 1, 1)
        delta = jnp.sum(prob * grad_prob, axis=-1, keepdims=True)
        grad_score = (prob * (grad_prob - delta) * factor).astype(BF)
        query_side = contract(grad_score, key, 1, 0)
        key_side = contract(grad_score, query, 0, 0)
        grad_ref[:, h * DH:(h + 1) * DH] = norm_back(
            query_side * qgain, query_hat, query_inv).astype(BF)
        grad_ref[:, width + h * DH:width + (h + 1) * DH] = norm_back(
            key_side * kgain, key_hat, key_inv).astype(BF)
        grad_ref[:, 2 * width + h * DH:2 * width + (h + 1) * DH] = contract(
            prob_half, cot, 0, 0).astype(BF)

    mean, inverse = stat_ref[0:1, :], stat_ref[1:2, :]
    first = jnp.zeros((1, LEN), F32)
    second = jnp.zeros((1, LEN), F32)
    packed_copy.wait()
    for slot, (_, _, _, block) in enumerate(blocks):
        if slot in arrived:
            arrived[slot].wait()
        rows = block_rows(block)
        term = contract(weight_ref[slot], grad_ref[...], 1, 1).astype(BF)
        scaled = term.astype(F32) * gain_ref[rows, :]
        first = first + jnp.sum(scaled, axis=0, keepdims=True)
        second = second + jnp.sum(
            scaled * (packed_ref[rows, :].astype(F32) - mean), axis=0, keepdims=True)
        same_core = lax.rem(block // 2, NC) == c
        same_half = lax.rem(block // 4, NH) == zh
        target = (block // 8) * SHARD + lax.rem(block, 2) * BLOCK
        out = pl.ds(pl.multiple_of(target, BLOCK), BLOCK)
        for core_flag, half_flag, ref in (
            (True, True, keep_a), (True, False, keep_b),
            (False, True, give_a), (False, False, give_b),
        ):
            @pl.when(jnp.logical_and(same_core == core_flag, same_half == half_flag))
            def _(ref=ref):
                ref[out, :] = term

    sums = split_sums(first, second * inverse)
    keep_b[NY * SHARD:, :] = sums
    give_b[NY * SHARD:, :] = sums


def split_sums(first, second):
    rows = []
    for value in (first, second):
        for _ in range(3):
            piece = value.astype(BF)
            rows.append(piece.astype(F32))
            value = value - piece.astype(F32)
    rows.append(jnp.zeros((TAIL - len(rows), LEN), F32))
    return jnp.concatenate(rows, axis=0).astype(BF)


def join_sums(tail):
    tail = tail.astype(F32)
    return (
        tail[..., 0:1, :] + tail[..., 1:2, :] + tail[..., 2:3, :],
        tail[..., 3:4, :] + tail[..., 4:5, :] + tail[..., 5:6, :],
    )


def send_packets(patches, destination):
    rows = patches.shape[0]
    n_groups = NZ * NX
    owners = destination // LEN
    offsets = destination % LEN
    one_hot = (owners[:, None] == jnp.arange(n_groups)[None, :]).astype(BF)
    index = jnp.arange(rows)
    strict = (index[:, None] > index[None, :]).astype(BF)
    earlier = jnp.dot(strict, one_hot, preferred_element_type=F32)
    rank = jnp.sum(earlier * one_hot.astype(F32), axis=1).astype(jnp.int32)
    position = owners * CAP + rank
    placing = jnp.arange(n_groups * CAP)[:, None] == position[None, :]
    sent = jnp.dot(placing.astype(BF), patches, preferred_element_type=F32).astype(BF)
    places = jnp.sum(jnp.where(placing, offsets[None, :] + 1, 0), axis=1)
    places = places.reshape(n_groups, 1, CAP).astype(BF)
    places = jnp.pad(places, ((0, 0), (0, 7), (0, 128 - CAP)))
    blocks = [
        sent[:, i:i + 128].reshape(n_groups, CAP, 128) for i in range(0, sent.shape[1], 128)
    ]
    return jnp.concatenate(blocks + [places], axis=1)


def unpack(got):
    n_groups = got.shape[0]
    n_blocks = (got.shape[1] - 8) // CAP
    places = got[:, n_blocks * CAP, :CAP].astype(jnp.int32).reshape(n_groups * CAP) - 1
    chosen = (places[:, None] == jnp.arange(LEN)[None, :]).astype(BF)
    out = [
        contract(
            got[:, i * CAP:(i + 1) * CAP].reshape(n_groups * CAP, 128), chosen, 0, 0
        ).astype(BF)
        for i in range(n_blocks)
    ]
    return jnp.concatenate(out, axis=0)


def per_device(patches, destination, segment, ln_gain, w_query, w_key, w_value,
               query_gain, key_gain, attn_cotangent):
    y, zh, c = lax.axis_index("y"), lax.axis_index("zh"), lax.axis_index("c")
    zl, x = lax.axis_index("zl"), lax.axis_index("x")
    where = jnp.stack([y, zh, c, zl, x]).astype(jnp.int32)
    gain_column = ln_gain[:, None]

    weight = jnp.concatenate([w_query, w_key, w_value], axis=1)
    packets = send_packets(patches, destination)

    x_ring = functools.partial(lax.ppermute, axis_name=("x", "c"), perm=core_ring(NX))
    y_ring = functools.partial(lax.ppermute, axis_name=("y", "c"), perm=core_ring(NY))
    got = lax.all_to_all(packets, ("zl", "x"), split_axis=0, concat_axis=0, tiled=True)
    z = {0: weight}
    for step in (1, 2, 3, 4):
        block = z[step - 1]
        z[step] = lax.ppermute(after(block, got) if step == 2 else block, "zl", Z_RING)
        if step < 4:
            z[-step] = lax.ppermute(z[1 - step], "zl", Z_BACK)
    early = lax.all_gather(jnp.concatenate([z[n] for n in EARLY]), "x", axis=0, tiled=True)
    early = early.reshape((NX, len(EARLY)) + weight.shape)
    late = [jnp.stack([z[n] for n in LATE])]
    for _ in range(NX - 1):
        late.append(x_ring(late[-1]))

    mine = unpack(got)
    g = [jnp.stack([mine, lax.ppermute(mine, "zh", shift(NH, 1))])]
    for _ in range(NY - 1):
        g.append(y_ring(g[-1]))
    most = lax.ppermute(jnp.concatenate(g[:3]), "c", shift(NC, 1))
    last = lax.ppermute(g[3], "c", shift(NC, 1))

    vmem = pl.BlockSpec(memory_space=pltpu.VMEM)
    smem = pl.BlockSpec(memory_space=pltpu.SMEM)
    normed, packed, stat = pl.pallas_call(
        norm_kernel,
        out_shape=(
            jax.ShapeDtypeStruct((D, LEN), BF),
            jax.ShapeDtypeStruct((D, LEN), BF),
            jax.ShapeDtypeStruct((2, LEN), F32),
        ),
        in_specs=[smem] + [vmem] * 7,
        out_specs=(vmem, vmem, vmem),
        compiler_params=pltpu.CompilerParams(vmem_limit_bytes=32 << 20),
        cost_estimate=pl.CostEstimate(flops=20_000_000, bytes_accessed=10_000_000, transcendentals=0),
        name="norm",
    )(where, gain_column, *g, most, last)

    width = w_query.shape[1]
    hbm = pl.BlockSpec(memory_space=pl.ANY)
    n_first = NX * len(EARLY) + (NX - 1) * len(LATE)
    part = pl.pallas_call(
        first_kernel,
        out_shape=jax.ShapeDtypeStruct((LEN, 3 * width), F32),
        in_specs=[smem, vmem] + [hbm] * NX,
        out_specs=vmem,
        scratch_shapes=[
            pltpu.VMEM((n_first,) + weight.shape, BF),
            pltpu.SemaphoreType.DMA((2 * NX - 1,)),
        ],
        compiler_params=pltpu.CompilerParams(vmem_limit_bytes=24 << 20),
        cost_estimate=pl.CostEstimate(
            flops=2_200_000_000, bytes_accessed=12_000_000, transcendentals=0),
        name="first",
    )(where, normed, early, *late[:NX - 1])

    half = jax.ShapeDtypeStruct((NY * SHARD, LEN), BF)
    half_tail = jax.ShapeDtypeStruct((NY * SHARD + TAIL, LEN), BF)
    context, keep_a, keep_b, give_a, give_b = pl.pallas_call(
        main_kernel,
        out_shape=(jax.ShapeDtypeStruct((LEN, width), BF), half, half_tail, half, half_tail),
        in_specs=[smem] + [vmem] * 8 + [hbm] * (3 + NX),
        out_specs=(vmem,) * 5,
        scratch_shapes=[
            pltpu.VMEM((NZ * NX,) + weight.shape, BF),
            pltpu.VMEM((len(LATE), BLOCK, LEN), BF),
            pltpu.VMEM((D, LEN), BF),
            pltpu.VMEM((LEN, 3 * width), F32),
            pltpu.VMEM((LEN, 3 * width), BF),
            pltpu.SemaphoreType.DMA((2 * NX + len(LATE) + 1,)),
        ],
        compiler_params=pltpu.CompilerParams(vmem_limit_bytes=36 << 20),
        cost_estimate=pl.CostEstimate(
            flops=3_000_000_000, bytes_accessed=20_000_000, transcendentals=131072),
        name="core",
    )(where, gain_column, stat, segment[None, :], segment[:, None], query_gain[None, :],
      key_gain[None, :], attn_cotangent, part, normed, packed, early, *late)

    rows = NY * SHARD
    y_swap = functools.partial(
        lax.all_to_all, axis_name="y", split_axis=0, concat_axis=0, tiled=True)
    taken = lax.ppermute(give_b, "c", shift(NC, 1))
    tails = [a + b for a, b in zip(join_sums(keep_b[rows:]), join_sums(taken[rows:]))]
    both = (keep_b[:rows].astype(F32) + taken[:rows].astype(F32)).astype(BF)
    tail = jnp.broadcast_to(split_sums(*tails)[None], (NY, TAIL, LEN))
    got_b = y_swap(jnp.concatenate([both.reshape(NY, SHARD, LEN), tail], axis=1))
    taken = lax.ppermute(give_a, "c", shift(NC, 1))
    both = (keep_a.astype(F32) + taken.astype(F32)).astype(BF)
    got_a = y_swap(both.reshape(NY, SHARD, LEN))
    leave = jnp.sum(got_b[:, :SHARD].astype(F32), axis=0).astype(BF)
    sums = [jnp.sum(a, axis=0) for a in join_sums(got_b[:, SHARD:])]
    came = lax.ppermute(
        jnp.concatenate([leave, split_sums(*sums)], axis=0), "zh", shift(NH, 1))
    shard = jnp.sum(got_a.astype(F32), axis=0) + came[:SHARD].astype(F32)
    first, second = [a + b for a, b in zip(sums, join_sums(came[SHARD:]))]

    index = (y * NH + zh) * NC + c
    gain_here = lax.dynamic_slice_in_dim(ln_gain, index * SHARD, SHARD, 0)[:, None]
    mean, inverse = stat[0:1], stat[1:2]
    x_hat = (mine.astype(F32) - mean) * inverse
    grad = (shard * gain_here - first / D - x_hat * (second / D)) * inverse
    return context, grad.T.astype(BF)


def solution(mesh):
    fine = Mesh(mesh.devices.reshape(NZ, NX, NY, NH, NC), ("zl", "x", "y", "zh", "c"))
    dp, mp = ("zl", "x"), ("y", "zh", "c")
    placed = (
        P(dp, mp), P(dp), P(dp), P(), P(dp, mp), P(dp, mp), P(dp, mp), P(mp), P(mp), P(dp, mp),
    )
    return jax.shard_map(
        per_device,
        mesh=fine,
        in_specs=placed,
        out_specs=(P(dp, mp), P(dp, mp)),
        check_vma=False,
    )
```

time: 1080 us -> 290 us (0.27)
  the two profiles are of different devices: /device:TPU:1 before, /device:TPU:41 now
where the time goes in v1:
time: 290 us; the launch traced here: 288 us
  waiting for transfers between devices  110 us (38%)
  starting transfers between devices  101 us (35%)
  Pallas kernels  29.8 us (10%)
  local copies, waits for them, and re-layouts  22.9 us (8%)
  between operations  15.5 us (5%)
  other arithmetic  7.12 us (2%)
    ppermute x4, waiting for transfers between devices, per_device(): lax.ppermute(after(block, got) if step == 2 else block, 'zl', Z_RING)  25.4 us
    ppermute x1, waiting for transfers between devices, per_device(): g = [jnp.stack([mine, lax.ppermute(mine, 'zh', shift(NH, 1))])]  21.2 us
    ppermute x3, starting transfers between devices, per_device(): z[-step] = lax.ppermute(z[1 - step], 'zl', Z_BACK)  21 us
    all_to_all x1, waiting for transfers between devices, per_device(): lax.all_to_all(packets, ('zl', 'x'), split_axis=0, concat_axis=0, tiled=T...  20.9 us
    unnamed x75, local copies, waits for them, and re-layouts  19.6 us
    pallas_call x1, Pallas kernels, per_device(): pl.pallas_call(main_kernel, out_shape=(jax.ShapeDtypeStruct((LEN, width),...  18.4 us
    ppermute x1, waiting for transfers between devices, per_device(): lax.ppermute(jnp.concatenate([leave, split_sums(*sums)], axis=0), 'zh', s...  16.3 us
    all_to_all x1, starting transfers between devices, per_device(): lax.all_to_all(packets, ('zl', 'x'), split_axis=0, concat_axis=0, tiled=T...  14.7 us
  transfers between devices with their start and end apart: 23, of which 13 were waited for; matrix products, arithmetic and copies ran while one was open for 3% of the time, Pallas kernels for 4%

profile of v1, /device:TPU:41, one launch (start us, length us, event | category | flops | bytes accessed | tf_op | source)
XLA Modules:
  0.0 288.4 jit_solution(17538934847217885931)
XLA Ops:
  7.2 0.7 and_select_fusion.1
  8.8 0.8 fusion.2
  9.6 14.7 %all-to-all-start = ((bf16[32,56,128]{2,1,0:T(8,128)(2,1)}), bf16[32,56,128]{2,1,0:T(8,128)(2,1)S(1)}, u32[]{:S(2)}, u32[]{:S(2)}) async-start(bf16[32,56,128]{2,1,0:T(8,128)(2,1)} %fusion.2), calls=%async_computation | async-start | bytes 917504 | tf_op jit(solution)/shard_map/all_to_all | solution.py:306
  24.5 2.1 collective-permute-start.6
  26.6 4.0 %collective-permute-start.7 = (bf16[192,768]{1,0:T(8,128)(2,1)S(1)}, bf16[192,768]{1,0:T(8,128)(2,1)S(1)}, u32[]{:S(2)}, u32[]{:S(2)}) collective-permute-start(bf16[192,768]{1,0:T(8,128)(2,1)S(1)} %get-tuple-element.42), channel_id=1, source_target_pairs={{128,0},{256,128},{384,256},{448,384},{320,448},{192,320},{64,192}... | collective-permute-start | bytes 884744 | tf_op jit(solution)/shard_map/ppermute | solution.py:312
  30.7 20.9 %all-to-all-done = bf16[32,56,128]{2,1,0:T(8,128)(2,1)S(1)} async-done(((bf16[32,56,128]{2,1,0:T(8,128)(2,1)}), bf16[32,56,128]{2,1,0:T(8,128)(2,1)S(1)}, u32[]{:S(2)}, u32[]{:S(2)}) %all-to-all-start) | async-done | bytes 458784 | tf_op jit(solution)/shard_map/all_to_all | solution.py:306
  51.6 0.5 slice.175
  52.9 3.2 %collective-permute-start.8 = (bf16[192,768]{1,0:T(8,128)(2,1)S(1)}, bf16[192,768]{1,0:T(8,128)(2,1)S(1)}, u32[]{:S(2)}, u32[]{:S(2)}) collective-permute-start(bf16[192,768]{1,0:T(8,128)(2,1)S(1)} %get-tuple-element.38), channel_id=1, source_target_pairs={{0,128},{128,256},{256,384},{384,448},{448,320},{320,192},{192,64}... | collective-permute-start | bytes 884744 | tf_op jit(solution)/shard_map/ppermute | solution.py:310
  56.1 8.8 %collective-permute-start.9 = (bf16[192,768]{1,0:T(8,128)(2,1)S(1)}, bf16[192,768]{1,0:T(8,128)(2,1)S(1)}, u32[]{:S(2)}, u32[]{:S(2)}) collective-permute-start(bf16[192,768]{1,0:T(8,128)(2,1)S(1)} %collective-permute-done.7), channel_id=1, source_target_pairs={{128,0},{256,128},{384,256},{448,384},{320,448},{192,320},{64,192}... | collective-permute-start | bytes 884744 | tf_op jit(solution)/shard_map/ppermute | solution.py:312
  64.9 3.7 %collective-permute-done.8 = bf16[192,768]{1,0:T(8,128)(2,1)S(1)} collective-permute-done((bf16[192,768]{1,0:T(8,128)(2,1)S(1)}, bf16[192,768]{1,0:T(8,128)(2,1)S(1)}, u32[]{:S(2)}, u32[]{:S(2)}) %collective-permute-start.8) | collective-permute-done | bytes 294944 | tf_op jit(solution)/shard_map/ppermute | solution.py:310
  68.6 3.4 %collective-permute-done.9 = bf16[192,768]{1,0:T(8,128)(2,1)S(1)} collective-permute-done((bf16[192,768]{1,0:T(8,128)(2,1)S(1)}, bf16[192,768]{1,0:T(8,128)(2,1)S(1)}, u32[]{:S(2)}, u32[]{:S(2)}) %collective-permute-start.9) | collective-permute-done | bytes 294944 | tf_op jit(solution)/shard_map/ppermute | solution.py:312
  72.1 1.1 copy-done.26
  73.2 8.2 %collective-permute-start.11 = (bf16[192,768]{1,0:T(8,128)(2,1)S(1)}, bf16[192,768]{1,0:T(8,128)(2,1)S(1)}, u32[]{:S(2)}, u32[]{:S(2)}) collective-permute-start(bf16[192,768]{1,0:T(8,128)(2,1)S(1)} %collective-permute-done.9), channel_id=1, source_target_pairs={{128,0},{256,128},{384,256},{448,384},{320,448},{192,320},{64,192}... | collective-permute-start | bytes 884744 | tf_op jit(solution)/shard_map/ppermute | solution.py:312
  81.4 1.9 collective-permute-start.10
  83.5 0.3 convolution_convert_fusion.3
  83.8 13.3 %collective-permute-done.10 = bf16[192,768]{1,0:T(8,128)(2,1)S(1)} collective-permute-done((bf16[192,768]{1,0:T(8,128)(2,1)S(1)}, bf16[192,768]{1,0:T(8,128)(2,1)S(1)}, u32[]{:S(2)}, u32[]{:S(2)}) %collective-permute-start.10) | collective-permute-done | bytes 294944 | tf_op jit(solution)/shard_map/ppermute | solution.py:310
  97.1 1.9 collective-permute-start.12
  99.1 0.3 convolution_convert_fusion.2
  99.7 8.4 %collective-permute-done.12 = bf16[192,768]{1,0:T(8,128)(2,1)S(1)} collective-permute-done((bf16[192,768]{1,0:T(8,128)(2,1)S(1)}, bf16[192,768]{1,0:T(8,128)(2,1)S(1)}, u32[]{:S(2)}, u32[]{:S(2)}) %collective-permute-start.12) | collective-permute-done | bytes 294944 | tf_op jit(solution)/shard_map/ppermute | solution.py:310
  108.2 4.7 %collective-permute-start.13 = (bf16[3,192,768]{2,1,0:T(8,128)(2,1)S(1)}, bf16[3,192,768]{2,1,0:T(8,128)(2,1)S(1)}, u32[]{:S(2)}, u32[]{:S(2)}) collective-permute-start(bf16[3,192,768]{2,1,0:T(8,128)(2,1)S(1)} %pad_maximum_fusion.1.late0_ref.rest_0_), channel_id=1, source_target_pairs={{0,16},{1,49},{16,32},{17,1},{32,48},{33,17},{48,0},{49,33},{2,18}... | collective-permute-start | bytes 2654216 | tf_op jit(solution)/shard_map/ppermute | solution.py:317
  112.9 0.9 copy-done.5
  113.8 7.9 %collective-permute-start = (bf16[384,256]{1,0:T(8,128)(2,1)S(1)}, bf16[384,256]{1,0:T(8,128)(2,1)S(1)}, u32[]{:S(2)}, u32[]{:S(2)}) collective-permute-start(bf16[384,256]{1,0:T(8,128)(2,1)S(1)} %get-tuple-element.41), channel_id=1, source_target_pairs={{0,2},{2,0},{1,3},{3,1},{4,6},{6,4},{5,7},{7,5},{8,10},{10,8},{9,1... | collective-permute-start | bytes 589832 | tf_op jit(solution)/shard_map/ppermute | solution.py:320
  121.8 21.2 %collective-permute-done = bf16[384,256]{1,0:T(8,128)(2,1)S(1)} collective-permute-done((bf16[384,256]{1,0:T(8,128)(2,1)S(1)}, bf16[384,256]{1,0:T(8,128)(2,1)S(1)}, u32[]{:S(2)}, u32[]{:S(2)}) %collective-permute-start) | collective-permute-done | bytes 196640 | tf_op jit(solution)/shard_map/ppermute | solution.py:320
  143.0 2.1 collective-permute-start.1
  145.1 0.8 copy-done.17
  145.9 6.1 %collective-permute-done.1.rest_1_ = bf16[2,384,256]{2,1,0:T(8,128)(2,1)S(1)} collective-permute-done((bf16[2,384,256]{2,1,0:T(8,128)(2,1)S(1)}, bf16[2,384,256]{2,1,0:T(8,128)(2,1)S(1)}, u32[]{:S(2)}, u32[]{:S(2)}) %collective-permute-start.1) | collective-permute-done | bytes 393248 | tf_op jit(solution)/shard_map/ppermute | solution.py:322
  151.9 2.5 collective-permute-start.2
  154.5 1.9 collective-permute-start.14
  156.4 0.9 copy-done.8
  157.3 3.4 %collective-permute-done.2.rest_2_ = bf16[2,384,256]{2,1,0:T(8,128)(2,1)S(1)} collective-permute-done((bf16[2,384,256]{2,1,0:T(8,128)(2,1)S(1)}, bf16[2,384,256]{2,1,0:T(8,128)(2,1)S(1)}, u32[]{:S(2)}, u32[]{:S(2)}) %collective-permute-start.2) | collective-permute-done | bytes 393248 | tf_op jit(solution)/shard_map/ppermute | solution.py:322
  160.7 1.2 pad_maximum_fusion
  162.0 0.8 copy-done.13
  162.7 3.9 %collective-permute-start.4 = (bf16[6,384,256]{2,1,0:T(8,128)(2,1)}, bf16[6,384,256]{2,1,0:T(8,128)(2,1)}, u32[]{:S(2)}, u32[]{:S(2)}) collective-permute-start(bf16[6,384,256]{2,1,0:T(8,128)(2,1)} %pad_maximum_fusion), channel_id=1, source_target_pairs={{0,1},{1,0},{2,3},{3,2},{4,5},{5,4},{6,7},{7,6},{8,9},{9,8},{10,11... | collective-permute-start | bytes 3538952 | tf_op jit(solution)/shard_map/ppermute | solution.py:323
  166.7 4.5 %collective-permute-start.3 = (bf16[2,384,256]{2,1,0:T(8,128)(2,1)S(1)}, bf16[2,384,256]{2,1,0:T(8,128)(2,1)}, u32[]{:S(2)}, u32[]{:S(2)}) collective-permute-start(bf16[2,384,256]{2,1,0:T(8,128)(2,1)S(1)} %collective-permute-done.2.rest_2_), channel_id=1, source_target_pairs={{0,4},{1,13},{4,8},{5,1},{8,12},{9,5},{12,0},{13,9},{2,6},{3,15},{... | collective-permute-start | bytes 1179656 | tf_op jit(solution)/shard_map/ppermute | solution.py:322
  171.2 1.9 collective-permute-start.15
  173.1 2.7 collective-permute-done.3.rest_3_
  175.9 3.5 %collective-permute-start.5 = (bf16[2,384,256]{2,1,0:T(8,128)(2,1)}, bf16[2,384,256]{2,1,0:T(8,128)(2,1)}, u32[]{:S(2)}, u32[]{:S(2)}) collective-permute-start(bf16[2,384,256]{2,1,0:T(8,128)(2,1)} %collective-permute-done.3.rest_3_), channel_id=1, source_target_pairs={{0,1},{1,0},{2,3},{3,2},{4,5},{5,4},{6,7},{7,6},{8,9},{9,8},{10,11... | collective-permute-start | bytes 1179656 | tf_op jit(solution)/shard_map/ppermute | solution.py:324
  179.4 1.1 copy.27.gain_ref
  180.9 1.0 copy-done.14
  181.9 1.0 copy-done.16
  182.9 1.0 copy-done.18
  183.9 4.2 %norm.1 = (bf16[6144,256]{1,0:T(8,128)(2,1)S(1)}, bf16[6144,256]{1,0:T(8,128)(2,1)S(1)}, f32[2,256]{1,0:T(2,128)S(1)}) custom-call(s32[5]{0:T(128)S(1)} %stack.44.where_ref, f32[6144,1]{1,0:T(8,128)S(1)} %copy.27.gain_ref, bf16[2,384,256]{2,1,0:T(8,128)(2,1)S(1)} %copy-done.18, bf16[2,384,256]{2,1,0:T(8,128)(2,1)S(1)} %copy-done.14, ...), custom_call_target="tpu_custom_call" | custom-call | flops 20000000 | bytes 10000000 | tf_op jit(solution)/shard_map/norm/pallas_call | solution.py:328
  188.1 1.7 copy-done.2
  189.8 1.7 copy-done.11
  191.5 2.7 copy-done.1
  194.2 1.9 copy-done.3
  196.1 1.2 copy-done.6
  197.3 1.2 copy-done.9
  198.5 7.1 %first.1.part_ref = f32[256,768]{1,0:T(8,128)S(1)} custom-call(s32[5]{0:T(128)S(1)} %stack.44.where_ref, bf16[6144,256]{1,0:T(8,128)(2,1)S(1)} %copy-done.3, bf16[4,5,192,768]{3,2,1,0:T(8,128)(2,1)S(1)} %bitcast.39, bf16[3,192,768]{2,1,0:T(8,128)(2,1)S(1)} %copy-done.6, bf16[3,192,768]{2,1,0:T(8,128)(2,1)S(1)} %copy-done.9, ...), custom_call_target="tpu_custom_call" | custom-call | flops 2200000000 | bytes 12000000 | tf_op jit(solution)/shard_map/first/pallas_call | solution.py:345
  205.7 18.4 %core.1 = (bf16[256,256]{1,0:T(8,128)(2,1)}, bf16[1536,256]{1,0:T(8,128)(2,1)S(1)}, bf16[1552,256]{1,0:T(8,128)(2,1)S(1)}, bf16[1536,256]{1,0:T(8,128)(2,1)}, bf16[1552,256]{1,0:T(8,128)(2,1)S(1)}) custom-call(s32[5]{0:T(128)S(1)} %stack.44.where_ref, f32[6144,1]{1,0:T(8,128)S(1)} %copy.27.gain_ref, f32[2,256]{1,0:T(2,128)S(1)} %get-tuple-element.10.stat_ref, ...), custom_call_target="tpu_custom_call" | custom-call | flops 3000000000 | bytes 20000000 | tf_op jit(solution)/shard_map/core/pallas_call | solution.py:362
  224.1 0.9 copy-done.20
  225.0 2.3 collective-permute-start.17
  227.3 2.1 collective-permute-start.16
  229.6 1.3 add_convert_fusion
  231.0 1.0 pad_maximum_fusion.2
  231.9 6.4 %all-to-all-start.2 = ((bf16[4,400,256]{2,1,0:T(8,128)(2,1)}), bf16[4,400,256]{2,1,0:T(8,128)(2,1)S(1)}, u32[]{:S(2)}, u32[]{:S(2)}) async-start(bf16[4,400,256]{2,1,0:T(8,128)(2,1)} %pad_maximum_fusion.2), calls=%async_computation.2 | async-start | bytes 1638400 | tf_op jit(solution)/shard_map/all_to_all | solution.py:389
  238.4 0.8 dynamic_slice.3
  239.1 1.1 add_convert_fusion.1
  240.2 9.3 %all-to-all-done.2 = bf16[4,400,256]{2,1,0:T(8,128)(2,1)S(1)} async-done(((bf16[4,400,256]{2,1,0:T(8,128)(2,1)}), bf16[4,400,256]{2,1,0:T(8,128)(2,1)S(1)}, u32[]{:S(2)}, u32[]{:S(2)}) %all-to-all-start.2) | async-done | bytes 819232 | tf_op jit(solution)/shard_map/all_to_all | solution.py:389
  249.6 4.6 %all-to-all-start.1 = ((bf16[4,384,256]{2,1,0:T(8,128)(2,1)}), bf16[4,384,256]{2,1,0:T(8,128)(2,1)S(1)}, u32[]{:S(2)}, u32[]{:S(2)}) async-start(bf16[4,384,256]{2,1,0:T(8,128)(2,1)} %bitcast.23), calls=%async_computation.1 | async-start | bytes 1572864 | tf_op jit(solution)/shard_map/all_to_all | solution.py:392
  254.7 7.9 %collective-permute-start.18 = (bf16[400,256]{1,0:T(8,128)(2,1)S(1)}, bf16[400,256]{1,0:T(8,128)(2,1)S(1)}, u32[]{:S(2)}, u32[]{:S(2)}) collective-permute-start(bf16[400,256]{1,0:T(8,128)(2,1)S(1)} %concatenate.43), channel_id=1, source_target_pairs={{0,2},{2,0},{1,3},{3,1},{4,6},{6,4},{5,7},{7,5},{8,10},{10,8},{9,1... | collective-permute-start | bytes 614408 | tf_op jit(solution)/shard_map/ppermute | solution.py:395
  262.6 1.5 all-to-all-done.1
  264.3 16.3 %collective-permute-done.18 = bf16[400,256]{1,0:T(8,128)(2,1)S(1)} collective-permute-done((bf16[400,256]{1,0:T(8,128)(2,1)S(1)}, bf16[400,256]{1,0:T(8,128)(2,1)S(1)}, u32[]{:S(2)}, u32[]{:S(2)}) %collective-permute-start.18) | collective-permute-done | bytes 204832 | tf_op jit(solution)/shard_map/ppermute | solution.py:395
  280.7 0.8 copy.29
  (111 shorter events, 3.1 us)
Async XLA Ops:
  7.2 1.0 copy-start
  8.1 16.3 %copy-start.31 = (bf16[192,256]{1,0:T(8,128)(2,1)S(1)}, bf16[192,256]{1,0:T(8,128)(2,1)}, u32[]{:S(2)}) copy-start(bf16[192,256]{1,0:T(8,128)(2,1)} %param.14) | copy-start | bytes 294916
  8.5 16.0 %copy-start.32 = (bf16[192,256]{1,0:T(8,128)(2,1)S(1)}, bf16[192,256]{1,0:T(8,128)(2,1)}, u32[]{:S(2)}) copy-start(bf16[192,256]{1,0:T(8,128)(2,1)} %param.15) | copy-start | bytes 294916
  8.5 16.0 %copy-start.33 = (bf16[192,256]{1,0:T(8,128)(2,1)S(1)}, bf16[192,256]{1,0:T(8,128)(2,1)}, u32[]{:S(2)}) copy-start(bf16[192,256]{1,0:T(8,128)(2,1)} %param.16) | copy-start | bytes 294916
  9.6 42.0 %all-to-all-start = ((bf16[32,56,128]{2,1,0:T(8,128)(2,1)}), bf16[32,56,128]{2,1,0:T(8,128)(2,1)S(1)}, u32[]{:S(2)}, u32[]{:S(2)}) async-start(bf16[32,56,128]{2,1,0:T(8,128)(2,1)} %fusion.2), calls=%async_computation | async-start | bytes 917504 | tf_op jit(solution)/shard_map/all_to_all | solution.py:306
  24.3 167.2 %all-gather.2.cloned.1.call-start = ((), (), s32[]{:S(2)}) async-start(), calls=%async_computation.3 | async-start | bytes 7372800 | tf_op jit(solution)/shard_map/all_gather | solution.py:313
  24.5 28.3 %collective-permute-start.6 = (bf16[192,768]{1,0:T(8,128)(2,1)S(1)}, bf16[192,768]{1,0:T(8,128)(2,1)S(1)}, u32[]{:S(2)}, u32[]{:S(2)}) collective-permute-start(bf16[192,768]{1,0:T(8,128)(2,1)S(1)} %get-tuple-element.42), channel_id=1, source_target_pairs={{0,128},{128,256},{256,384},{384,448},{448,320},{320,192},{192,64}... | collective-permute-start | bytes 884744 | tf_op jit(solution)/shard_map/ppermute | solution.py:310
  26.6 29.4 %collective-permute-start.7 = (bf16[192,768]{1,0:T(8,128)(2,1)S(1)}, bf16[192,768]{1,0:T(8,128)(2,1)S(1)}, u32[]{:S(2)}, u32[]{:S(2)}) collective-permute-start(bf16[192,768]{1,0:T(8,128)(2,1)S(1)} %get-tuple-element.42), channel_id=1, source_target_pairs={{128,0},{256,128},{384,256},{448,384},{320,448},{192,320},{64,192}... | collective-permute-start | bytes 884744 | tf_op jit(solution)/shard_map/ppermute | solution.py:312
  52.9 15.7 %collective-permute-start.8 = (bf16[192,768]{1,0:T(8,128)(2,1)S(1)}, bf16[192,768]{1,0:T(8,128)(2,1)S(1)}, u32[]{:S(2)}, u32[]{:S(2)}) collective-permute-start(bf16[192,768]{1,0:T(8,128)(2,1)S(1)} %get-tuple-element.38), channel_id=1, source_target_pairs={{0,128},{128,256},{256,384},{384,448},{448,320},{320,192},{192,64}... | collective-permute-start | bytes 884744 | tf_op jit(solution)/shard_map/ppermute | solution.py:310
  56.1 16.0 %collective-permute-start.9 = (bf16[192,768]{1,0:T(8,128)(2,1)S(1)}, bf16[192,768]{1,0:T(8,128)(2,1)S(1)}, u32[]{:S(2)}, u32[]{:S(2)}) collective-permute-start(bf16[192,768]{1,0:T(8,128)(2,1)S(1)} %collective-permute-done.7), channel_id=1, source_target_pairs={{128,0},{256,128},{384,256},{448,384},{320,448},{192,320},{64,192}... | collective-permute-start | bytes 884744 | tf_op jit(solution)/shard_map/ppermute | solution.py:312
  72.1 1.1 copy-start.26
  73.2 26.5 %collective-permute-start.11 = (bf16[192,768]{1,0:T(8,128)(2,1)S(1)}, bf16[192,768]{1,0:T(8,128)(2,1)S(1)}, u32[]{:S(2)}, u32[]{:S(2)}) collective-permute-start(bf16[192,768]{1,0:T(8,128)(2,1)S(1)} %collective-permute-done.9), channel_id=1, source_target_pairs={{128,0},{256,128},{384,256},{448,384},{320,448},{192,320},{64,192}... | collective-permute-start | bytes 884744 | tf_op jit(solution)/shard_map/ppermute | solution.py:312
  81.4 15.7 %collective-permute-start.10 = (bf16[192,768]{1,0:T(8,128)(2,1)S(1)}, bf16[192,768]{1,0:T(8,128)(2,1)S(1)}, u32[]{:S(2)}, u32[]{:S(2)}) collective-permute-start(bf16[192,768]{1,0:T(8,128)(2,1)S(1)} %collective-permute-done.8), channel_id=1, source_target_pairs={{0,128},{128,256},{256,384},{384,448},{448,320},{320,192},{192,64}... | collective-permute-start | bytes 884744 | tf_op jit(solution)/shard_map/ppermute | solution.py:310
  97.1 11.0 %collective-permute-start.12 = (bf16[192,768]{1,0:T(8,128)(2,1)S(1)}, bf16[192,768]{1,0:T(8,128)(2,1)S(1)}, u32[]{:S(2)}, u32[]{:S(2)}) collective-permute-start(bf16[192,768]{1,0:T(8,128)(2,1)S(1)} %collective-permute-done.10), channel_id=1, source_target_pairs={{0,128},{128,256},{256,384},{384,448},{448,320},{320,192},{192,64}... | collective-permute-start | bytes 884744 | tf_op jit(solution)/shard_map/ppermute | solution.py:310
  99.4 43.6 %copy-start.27 = (bf16[128,256]{1,0:T(8,128)(2,1)}, bf16[128,256]{1,0:T(8,128)(2,1)S(1)}, u32[]{:S(2)}) copy-start(bf16[128,256]{1,0:T(8,128)(2,1)S(1)} %convolution_convert_fusion.2) | copy-start | bytes 196612
  99.7 43.3 %copy-start.29 = (bf16[128,256]{1,0:T(8,128)(2,1)}, bf16[128,256]{1,0:T(8,128)(2,1)S(1)}, u32[]{:S(2)}) copy-start(bf16[128,256]{1,0:T(8,128)(2,1)S(1)} %convolution_convert_fusion.1) | copy-start | bytes 196612
  108.2 46.2 %collective-permute-start.13 = (bf16[3,192,768]{2,1,0:T(8,128)(2,1)S(1)}, bf16[3,192,768]{2,1,0:T(8,128)(2,1)S(1)}, u32[]{:S(2)}, u32[]{:S(2)}) collective-permute-start(bf16[3,192,768]{2,1,0:T(8,128)(2,1)S(1)} %pad_maximum_fusion.1.late0_ref.rest_0_), channel_id=1, source_target_pairs={{0,16},{1,49},{16,32},{17,1},{32,48},{33,17},{48,0},{49,33},{2,18}... | collective-permute-start | bytes 2654216 | tf_op jit(solution)/shard_map/ppermute | solution.py:317
  112.9 0.9 copy-start.5
  113.8 29.1 %collective-permute-start = (bf16[384,256]{1,0:T(8,128)(2,1)S(1)}, bf16[384,256]{1,0:T(8,128)(2,1)S(1)}, u32[]{:S(2)}, u32[]{:S(2)}) collective-permute-start(bf16[384,256]{1,0:T(8,128)(2,1)S(1)} %get-tuple-element.41), channel_id=1, source_target_pairs={{0,2},{2,0},{1,3},{3,1},{4,6},{6,4},{5,7},{7,5},{8,10},{10,8},{9,1... | collective-permute-start | bytes 589832 | tf_op jit(solution)/shard_map/ppermute | solution.py:320
  143.0 36.4 %copy-start.34 = (f32[6144]{0:T(1024)S(1)}, f32[6144]{0:T(1024)}, u32[]{:S(2)}) copy-start(f32[6144]{0:T(1024)} %param.13) | copy-start | bytes 73732
  143.0 8.9 %collective-permute-start.1 = (bf16[2,384,256]{2,1,0:T(8,128)(2,1)S(1)}, bf16[2,384,256]{2,1,0:T(8,128)(2,1)S(1)}, u32[]{:S(2)}, u32[]{:S(2)}) collective-permute-start(bf16[2,384,256]{2,1,0:T(8,128)(2,1)S(1)} %pad_maximum_fusion.3.rest_0_), channel_id=1, source_target_pairs={{0,4},{1,13},{4,8},{5,1},{8,12},{9,5},{12,0},{13,9},{2,6},{3,15},{... | collective-permute-start | bytes 1179656 | tf_op jit(solution)/shard_map/ppermute | solution.py:322
  145.1 0.8 copy-start.17
  151.9 8.8 %collective-permute-start.2 = (bf16[2,384,256]{2,1,0:T(8,128)(2,1)S(1)}, bf16[2,384,256]{2,1,0:T(8,128)(2,1)S(1)}, u32[]{:S(2)}, u32[]{:S(2)}) collective-permute-start(bf16[2,384,256]{2,1,0:T(8,128)(2,1)S(1)} %collective-permute-done.1.rest_1_), channel_id=1, source_target_pairs={{0,4},{1,13},{4,8},{5,1},{8,12},{9,5},{12,0},{13,9},{2,6},{3,15},{... | collective-permute-start | bytes 1179656 | tf_op jit(solution)/shard_map/ppermute | solution.py:322
  154.5 16.7 %collective-permute-start.14 = (bf16[3,192,768]{2,1,0:T(8,128)(2,1)S(1)}, bf16[3,192,768]{2,1,0:T(8,128)(2,1)}, u32[]{:S(2)}, u32[]{:S(2)}) collective-permute-start(bf16[3,192,768]{2,1,0:T(8,128)(2,1)S(1)} %collective-permute-done.13.late1_ref.rest_1_), channel_id=1, source_target_pairs={{0,16},{1,49},{16,32},{17,1},{32,48},{33,17},{48,0},{49,33},{2,18}... | collective-permute-start | bytes 2654216 | tf_op jit(solution)/shard_map/ppermute | solution.py:317
  156.4 0.9 copy-start.8
  160.7 10.4 %copy-start.15 = (bf16[2,384,256]{2,1,0:T(8,128)(2,1)}, bf16[2,384,256]{2,1,0:T(8,128)(2,1)S(1)}, u32[]{:S(2)}) copy-start(bf16[2,384,256]{2,1,0:T(8,128)(2,1)S(1)} %collective-permute-done.2.rest_2_) | copy-start | bytes 1179652
  162.0 0.8 copy-start.13
  162.7 18.2 %collective-permute-start.4 = (bf16[6,384,256]{2,1,0:T(8,128)(2,1)}, bf16[6,384,256]{2,1,0:T(8,128)(2,1)}, u32[]{:S(2)}, u32[]{:S(2)}) collective-permute-start(bf16[6,384,256]{2,1,0:T(8,128)(2,1)} %pad_maximum_fusion), channel_id=1, source_target_pairs={{0,1},{1,0},{2,3},{3,2},{4,5},{5,4},{6,7},{7,6},{8,9},{9,8},{10,11... | collective-permute-start | bytes 3538952 | tf_op jit(solution)/shard_map/ppermute | solution.py:323
  166.7 9.2 %collective-permute-start.3 = (bf16[2,384,256]{2,1,0:T(8,128)(2,1)S(1)}, bf16[2,384,256]{2,1,0:T(8,128)(2,1)}, u32[]{:S(2)}, u32[]{:S(2)}) collective-permute-start(bf16[2,384,256]{2,1,0:T(8,128)(2,1)S(1)} %collective-permute-done.2.rest_2_), channel_id=1, source_target_pairs={{0,4},{1,13},{4,8},{5,1},{8,12},{9,5},{12,0},{13,9},{2,6},{3,15},{... | collective-permute-start | bytes 1179656 | tf_op jit(solution)/shard_map/ppermute | solution.py:322
  171.2 34.4 %collective-permute-start.15 = (bf16[3,192,768]{2,1,0:T(8,128)(2,1)}, bf16[3,192,768]{2,1,0:T(8,128)(2,1)}, u32[]{:S(2)}, u32[]{:S(2)}) collective-permute-start(bf16[3,192,768]{2,1,0:T(8,128)(2,1)} %collective-permute-done.14.late2_ref.rest_2_), channel_id=1, source_target_pairs={{0,16},{1,49},{16,32},{17,1},{32,48},{33,17},{48,0},{49,33},{2,18}... | collective-permute-start | bytes 2654216 | tf_op jit(solution)/shard_map/ppermute | solution.py:317
  175.9 5.0 %collective-permute-start.5 = (bf16[2,384,256]{2,1,0:T(8,128)(2,1)}, bf16[2,384,256]{2,1,0:T(8,128)(2,1)}, u32[]{:S(2)}, u32[]{:S(2)}) collective-permute-start(bf16[2,384,256]{2,1,0:T(8,128)(2,1)} %collective-permute-done.3.rest_3_), channel_id=1, source_target_pairs={{0,1},{1,0},{2,3},{3,2},{4,5},{5,4},{6,7},{7,6},{8,9},{9,8},{10,11... | collective-permute-start | bytes 1179656 | tf_op jit(solution)/shard_map/ppermute | solution.py:324
  179.4 1.1 copy-start.23
  180.9 1.0 copy-start.14
  181.9 1.0 copy-start.16
  182.9 1.0 copy-start.18
  188.1 1.7 copy-start.2
  189.8 1.7 copy-start.11
  191.5 2.7 copy-start.1
  194.2 1.9 copy-start.3
  196.1 1.2 copy-start.6
  197.3 1.2 copy-start.9
  198.4 7.2 %copy-start.4 = (bf16[6144,256]{1,0:T(8,128)(2,1)S(1)}, bf16[6144,256]{1,0:T(8,128)(2,1)}, u32[]{:S(2)}) copy-start(bf16[6144,256]{1,0:T(8,128)(2,1)} %copy-done.2) | copy-start | bytes 9437188
  198.4 7.2 %copy-start.7 = (bf16[3,192,768]{2,1,0:T(8,128)(2,1)S(1)}, bf16[3,192,768]{2,1,0:T(8,128)(2,1)}, u32[]{:S(2)}) copy-start(bf16[3,192,768]{2,1,0:T(8,128)(2,1)} %copy-done.5) | copy-start | bytes 2654212
  198.5 7.2 %copy-start.10 = (bf16[3,192,768]{2,1,0:T(8,128)(2,1)S(1)}, bf16[3,192,768]{2,1,0:T(8,128)(2,1)}, u32[]{:S(2)}) copy-start(bf16[3,192,768]{2,1,0:T(8,128)(2,1)} %copy-done.8) | copy-start | bytes 2654212
  198.5 7.2 %copy-start.12 = (bf16[6144,256]{1,0:T(8,128)(2,1)S(1)}, bf16[6144,256]{1,0:T(8,128)(2,1)}, u32[]{:S(2)}) copy-start(bf16[6144,256]{1,0:T(8,128)(2,1)} %copy-done.11) | copy-start | bytes 9437188
  198.5 7.2 %copy-start.22 = (bf16[256,256]{1,0:T(8,128)(2,1)S(1)}, bf16[256,256]{1,0:T(8,128)(2,1)}, u32[]{:S(2)}) copy-start(bf16[256,256]{1,0:T(8,128)(2,1)} %cot_ref.1) | copy-start | bytes 393220
  198.5 7.2 %copy-start.24 = (f32[256]{0:T(256)S(1)}, f32[256]{0:T(256)}, u32[]{:S(2)}) copy-start(f32[256]{0:T(256)} %param.17) | copy-start | bytes 3076
  198.5 7.2 %copy-start.25 = (f32[256]{0:T(256)S(1)}, f32[256]{0:T(256)}, u32[]{:S(2)}) copy-start(f32[256]{0:T(256)} %param.18) | copy-start | bytes 3076
  224.1 0.9 copy-start.20
  225.0 4.3 %copy-start.19 = (bf16[1552,256]{1,0:T(8,128)(2,1)}, bf16[1552,256]{1,0:T(8,128)(2,1)S(1)}, u32[]{:S(2)}) copy-start(bf16[1552,256]{1,0:T(8,128)(2,1)S(1)} %get-tuple-element.16) | copy-start | bytes 2383876
  225.0 4.4 %collective-permute-start.17 = (bf16[1552,256]{1,0:T(8,128)(2,1)S(1)}, bf16[1552,256]{1,0:T(8,128)(2,1)S(1)}, u32[]{:S(2)}, u32[]{:S(2)}) collective-permute-start(bf16[1552,256]{1,0:T(8,128)(2,1)S(1)} %get-tuple-element.17), channel_id=1, source_target_pairs={{0,1},{1,0},{2,3},{3,2},{4,5},{5,4},{6,7},{7,6},{8,9},{9,8},{10,11... | collective-permute-start | bytes 2383880 | tf_op jit(solution)/shard_map/ppermute | solution.py:385
  227.3 11.8 %collective-permute-start.16 = (bf16[1536,256]{1,0:T(8,128)(2,1)}, bf16[1536,256]{1,0:T(8,128)(2,1)S(1)}, u32[]{:S(2)}, u32[]{:S(2)}) collective-permute-start(bf16[1536,256]{1,0:T(8,128)(2,1)} %get-tuple-element.15), channel_id=1, source_target_pairs={{0,1},{1,0},{2,3},{3,2},{4,5},{5,4},{6,7},{7,6},{8,9},{9,8},{10,11... | collective-permute-start | bytes 2359304 | tf_op jit(solution)/shard_map/ppermute | solution.py:390
  230.9 8.2 %copy-start.21 = (bf16[1536,256]{1,0:T(8,128)(2,1)S(1)}, bf16[1536,256]{1,0:T(8,128)(2,1)}, u32[]{:S(2)}) copy-start(bf16[1536,256]{1,0:T(8,128)(2,1)} %copy-done.20) | copy-start | bytes 2359300
  231.9 17.6 %all-to-all-start.2 = ((bf16[4,400,256]{2,1,0:T(8,128)(2,1)}), bf16[4,400,256]{2,1,0:T(8,128)(2,1)S(1)}, u32[]{:S(2)}, u32[]{:S(2)}) async-start(bf16[4,400,256]{2,1,0:T(8,128)(2,1)} %pad_maximum_fusion.2), calls=%async_computation.2 | async-start | bytes 1638400 | tf_op jit(solution)/shard_map/all_to_all | solution.py:389
  249.6 14.6 %all-to-all-start.1 = ((bf16[4,384,256]{2,1,0:T(8,128)(2,1)}), bf16[4,384,256]{2,1,0:T(8,128)(2,1)S(1)}, u32[]{:S(2)}, u32[]{:S(2)}) async-start(bf16[4,384,256]{2,1,0:T(8,128)(2,1)} %bitcast.23), calls=%async_computation.1 | async-start | bytes 1572864 | tf_op jit(solution)/shard_map/all_to_all | solution.py:392
  254.2 26.3 %copy-start.28 = (bf16[128,256]{1,0:T(8,128)(2,1)S(1)}, bf16[128,256]{1,0:T(8,128)(2,1)}, u32[]{:S(2)}) copy-start(bf16[128,256]{1,0:T(8,128)(2,1)} %copy-done.27) | copy-start | bytes 196612
  254.2 26.4 %copy-start.30 = (bf16[128,256]{1,0:T(8,128)(2,1)S(1)}, bf16[128,256]{1,0:T(8,128)(2,1)}, u32[]{:S(2)}) copy-start(bf16[128,256]{1,0:T(8,128)(2,1)} %copy-done.29) | copy-start | bytes 196612
  254.7 25.9 %collective-permute-start.18 = (bf16[400,256]{1,0:T(8,128)(2,1)S(1)}, bf16[400,256]{1,0:T(8,128)(2,1)S(1)}, u32[]{:S(2)}, u32[]{:S(2)}) collective-permute-start(bf16[400,256]{1,0:T(8,128)(2,1)S(1)} %concatenate.43), channel_id=1, source_target_pairs={{0,2},{2,0},{1,3},{3,1},{4,6},{6,4},{5,7},{7,5},{8,10},{10,8},{9,1... | collective-permute-start | bytes 614408 | tf_op jit(solution)/shard_map/ppermute | solution.py:395
Sparse Core Ops, SparseCore 0:
  73.3 83.4 all-gather.1

commit v2 on v1

--- a/solution.py
+++ b/solution.py
@@ -22,7 +22,9 @@
 FOLD = [0, 2, 4, 6, 7, 5, 3, 1]
 Z_RING = [(FOLD[i], FOLD[(i + 1) % NZ]) for i in range(NZ)]
 Z_BACK = [(b, a) for a, b in Z_RING]
+Z_TWO = [(FOLD[i], FOLD[(i + 2) % NZ]) for i in range(NZ)]
 EARLY = (0, 1, -1, 2, -2)
+FIRST = 1
 LATE = (3, -3, 4)
 TAIL = 16
 
@@ -100,13 +102,13 @@
     c, zl, x = where_ref[2], where_ref[3], where_ref[4]
     position = jnp.where(lax.rem(zl, 2) == 0, zl // 2, 7 - zl // 2)
     found = []
-    for early, steps in ((True, EARLY), (False, LATE)):
+    for steps in (EARLY[:FIRST], EARLY[FIRST:], LATE):
         for off in range(NX):
-            x_from = off if early else ring_source(x, c, off, NX)
-            for j, step in enumerate(steps):
+            x_from = ring_source(x, c, off, NX) if steps is LATE else off
+            for step in steps:
                 p = lax.rem(position - step + NZ, NZ)
                 z_from = jnp.where(p < 4, 2 * p, 15 - 2 * p)
-                found.append((early, off, j, z_from * NX + x_from))
+                found.append(z_from * NX + x_from)
     return found
 
 
@@ -114,24 +116,31 @@
     return pl.ds(pl.multiple_of(block * BLOCK, BLOCK), BLOCK)
 
 
-def first_kernel(where_ref, normed_ref, early_ref, late0_ref, late1_ref, late2_ref,
+def load_weights(early_refs, late_refs, weight_ref, sems):
+    sources = []
+    for ref in early_refs:
+        sources.extend((ref.at[off], ref.shape[1]) for off in range(NX))
+    sources.extend((ref, ref.shape[0]) for ref in late_refs)
+    copies = {}
+    slot = 0
+    for n, (source, size) in enumerate(sources):
+        copies[slot] = pltpu.make_async_copy(
+            source, weight_ref.at[slot:slot + size], sems.at[n])
+        slot += size
+    return copies
+
+
+def first_kernel(where_ref, normed_ref, early0_ref, early1_ref, late0_ref, late1_ref, late2_ref,
                  acc_ref, weight_ref, sems):
-    late_refs = (late0_ref, late1_ref, late2_ref)
     blocks = weight_blocks(where_ref)
-    count = NX * len(EARLY) + (NX - 1) * len(LATE)
-    copies = []
-    for n in range(2 * NX - 1):
-        slot = n * len(EARLY) if n < NX else NX * len(EARLY) + (n - NX) * len(LATE)
-        size = len(EARLY) if n < NX else len(LATE)
-        source = early_ref.at[n] if n < NX else late_refs[n - NX]
-        copy = pltpu.make_async_copy(source, weight_ref.at[slot:slot + size], sems.at[n])
+    copies = load_weights(
+        (early0_ref, early1_ref), (late0_ref, late1_ref, late2_ref), weight_ref, sems)
+    for copy in copies.values():
         copy.start()
-        copies.append((slot, copy))
-    copies = dict(copies)
-    for slot in range(count):
+    for slot in range(weight_ref.shape[0]):
         if slot in copies:
             copies[slot].wait()
-        part = contract(normed_ref[block_rows(blocks[slot][3]), :], weight_ref[slot], 0, 0)
+        part = contract(normed_ref[block_rows(blocks[slot]), :], weight_ref[slot], 0, 0)
         if slot == 0:
             acc_ref[...] = part
         else:
@@ -139,38 +148,29 @@
 
 
 def main_kernel(where_ref, gain_ref, stat_ref, seg_row_ref, seg_col_ref, qgain_ref, kgain_ref,
-                cot_ref, part_ref, normed_ref, packed_hbm, early_ref, *rest):
-    late_refs, rest = rest[:NX], rest[NX:]
+                cot_ref, part_ref, normed_ref, packed_hbm, *rest):
+    early_refs, late_refs, rest = rest[:2], rest[2:2 + NX], rest[2 + NX:]
     attn_ref, keep_a, keep_b, give_a, give_b = rest[:5]
     weight_ref, rows_ref, packed_ref, acc_ref, grad_ref, sems = rest[5:]
-    y, zh, c = where_ref[0], where_ref[1], where_ref[2]
+    zh, c = where_ref[1], where_ref[2]
     blocks = weight_blocks(where_ref)
-    first_late = NX * len(EARLY)
-    final = first_late + (NX - 1) * len(LATE)
-
-    arrived = []
-    order = [2 * NX - 1] + list(range(2 * NX - 1))
-    for n in order:
-        slot = n * len(EARLY) if n < NX else first_late + (n - NX) * len(LATE)
-        size = len(EARLY) if n < NX else len(LATE)
-        source = early_ref.at[n] if n < NX else late_refs[n - NX]
-        copy = pltpu.make_async_copy(source, weight_ref.at[slot:slot + size], sems.at[n])
+    final = NZ * NX - len(LATE)
+
+    arrived = load_weights(early_refs, late_refs, weight_ref, sems)
+    last_copy = arrived.pop(final)
+    last_copy.start()
+    row_copies = [
+        pltpu.make_async_copy(
+            normed_ref.at[block_rows(blocks[final + j]), :], rows_ref.at[j], sems.at[3 * NX + j])
+        for j in range(len(LATE))
+    ]
+    packed_copy = pltpu.make_async_copy(packed_hbm, packed_ref, sems.at[3 * NX + len(LATE)])
+    for copy in row_copies + list(arrived.values()) + [packed_copy]:
         copy.start()
-        arrived.append((slot, copy))
-        if n == 2 * NX - 1:
-            for j in range(len(LATE)):
-                copy = pltpu.make_async_copy(
-                    normed_ref.at[block_rows(blocks[final + j][3]), :],
-                    rows_ref.at[j], sems.at[2 * NX + j])
-                copy.start()
-                arrived.append((-1 - j, copy))
-    arrived = dict(arrived)
-    packed_copy = pltpu.make_async_copy(packed_hbm, packed_ref, sems.at[2 * NX + len(LATE)])
-    packed_copy.start()
-
-    arrived.pop(final).wait()
-    for j in range(len(LATE)):
-        arrived.pop(-1 - j).wait()
+
+    last_copy.wait()
+    for j, copy in enumerate(row_copies):
+        copy.wait()
         part = contract(rows_ref[j], weight_ref[final + j], 0, 0)
         if j == 0:
             acc_ref[...] = part_ref[...] + part
@@ -210,7 +210,7 @@
     first = jnp.zeros((1, LEN), F32)
     second = jnp.zeros((1, LEN), F32)
     packed_copy.wait()
-    for slot, (_, _, _, block) in enumerate(blocks):
+    for slot, block in enumerate(blocks):
         if slot in arrived:
             arrived[slot].wait()
         rows = block_rows(block)
@@ -304,20 +304,27 @@
     x_ring = functools.partial(lax.ppermute, axis_name=("x", "c"), perm=core_ring(NX))
     y_ring = functools.partial(lax.ppermute, axis_name=("y", "c"), perm=core_ring(NY))
     got = lax.all_to_all(packets, ("zl", "x"), split_axis=0, concat_axis=0, tiled=True)
+    mine = unpack(got)
+    partner = lax.ppermute(mine, "zh", shift(NH, 1))
     z = {0: weight}
-    for step in (1, 2, 3, 4):
-        block = z[step - 1]
-        z[step] = lax.ppermute(after(block, got) if step == 2 else block, "zl", Z_RING)
-        if step < 4:
-            z[-step] = lax.ppermute(z[1 - step], "zl", Z_BACK)
-    early = lax.all_gather(jnp.concatenate([z[n] for n in EARLY]), "x", axis=0, tiled=True)
-    early = early.reshape((NX, len(EARLY)) + weight.shape)
+    z[1] = lax.ppermute(weight, "zl", Z_RING)
+    z[-1] = lax.ppermute(weight, "zl", Z_BACK)
+    z[2] = lax.ppermute(weight, "zl", Z_TWO)
+    z[-2] = lax.ppermute(weight, "zl", [(b, a) for a, b in Z_TWO])
+    z[3] = lax.ppermute(after(z[2], got), "zl", Z_RING)
+    z[-3] = lax.ppermute(z[-2], "zl", Z_BACK)
+    z[4] = lax.ppermute(after(z[3], partner), "zl", Z_RING)
+    early = []
+    for steps in (EARLY[:FIRST], EARLY[FIRST:]):
+        joined = lax.all_gather(
+            jnp.concatenate([after(z[n], got) if n == 1 else z[n] for n in steps]),
+            "x", axis=0, tiled=True)
+        early.append(joined.reshape((NX, len(steps)) + weight.shape))
     late = [jnp.stack([z[n] for n in LATE])]
     for _ in range(NX - 1):
         late.append(x_ring(late[-1]))
 
-    mine = unpack(got)
-    g = [jnp.stack([mine, lax.ppermute(mine, "zh", shift(NH, 1))])]
+    g = [jnp.stack([mine, partner])]
     for _ in range(NY - 1):
         g.append(y_ring(g[-1]))
     most = lax.ppermute(jnp.concatenate(g[:3]), "c", shift(NC, 1))
@@ -345,24 +352,24 @@
     part = pl.pallas_call(
         first_kernel,
         out_shape=jax.ShapeDtypeStruct((LEN, 3 * width), F32),
-        in_specs=[smem, vmem] + [hbm] * NX,
+        in_specs=[smem, vmem] + [hbm] * (NX + 1),
         out_specs=vmem,
         scratch_shapes=[
             pltpu.VMEM((n_first,) + weight.shape, BF),
-            pltpu.SemaphoreType.DMA((2 * NX - 1,)),
+            pltpu.SemaphoreType.DMA((3 * NX - 1,)),
         ],
-        compiler_params=pltpu.CompilerParams(vmem_limit_bytes=24 << 20),
+        compiler_params=pltpu.CompilerParams(vmem_limit_bytes=54 << 20),
         cost_estimate=pl.CostEstimate(
             flops=2_200_000_000, bytes_accessed=12_000_000, transcendentals=0),
         name="first",
-    )(where, normed, early, *late[:NX - 1])
+    )(where, normed, *early, *late[:NX - 1])
 
     half = jax.ShapeDtypeStruct((NY * SHARD, LEN), BF)
     half_tail = jax.ShapeDtypeStruct((NY * SHARD + TAIL, LEN), BF)
     context, keep_a, keep_b, give_a, give_b = pl.pallas_call(
         main_kernel,
         out_shape=(jax.ShapeDtypeStruct((LEN, width), BF), half, half_tail, half, half_tail),
-        in_specs=[smem] + [vmem] * 8 + [hbm] * (3 + NX),
+        in_specs=[smem] + [vmem] * 8 + [hbm] * (4 + NX),
         out_specs=(vmem,) * 5,
         scratch_shapes=[
             pltpu.VMEM((NZ * NX,) + weight.shape, BF),
@@ -370,14 +377,14 @@
             pltpu.VMEM((D, LEN), BF),
             pltpu.VMEM((LEN, 3 * width), F32),
             pltpu.VMEM((LEN, 3 * width), BF),
-            pltpu.SemaphoreType.DMA((2 * NX + len(LATE) + 1,)),
+            pltpu.SemaphoreType.DMA((3 * NX + len(LATE) + 1,)),
         ],
-        compiler_params=pltpu.CompilerParams(vmem_limit_bytes=36 << 20),
+        compiler_params=pltpu.CompilerParams(vmem_limit_bytes=54 << 20),
         cost_estimate=pl.CostEstimate(
             flops=3_000_000_000, bytes_accessed=20_000_000, transcendentals=131072),
         name="core",
     )(where, gain_column, stat, segment[None, :], segment[:, None], query_gain[None, :],
-      key_gain[None, :], attn_cotangent, part, normed, packed, early, *late)
+      key_gain[None, :], attn_cotangent, part, normed, packed, *early, *late)
 
     rows = NY * SHARD
     y_swap = functools.partial(

time: 290 us -> 296 us (1.021)
  the two profiles are of different devices: /device:TPU:41 before, /device:TPU:40 now
where the time goes in v2:
time: 296 us; the launch traced here: 294 us
  waiting for transfers between devices  117 us (40%)
  starting transfers between devices  99.9 us (34%)
  Pallas kernels  35.6 us (12%)
  between operations  16 us (5%)
  local copies, waits for them, and re-layouts  15.4 us (5%)
  other arithmetic  8.89 us (3%)
    all_to_all x1, waiting for transfers between devices, per_device(): lax.all_to_all(packets, ('zl', 'x'), split_axis=0, concat_axis=0, tiled=T...  24.3 us
    pallas_call x1, Pallas kernels, per_device(): pl.pallas_call(main_kernel, out_shape=(jax.ShapeDtypeStruct((LEN, width),...  22.2 us
    ppermute x1, waiting for transfers between devices, per_device(): lax.ppermute(jnp.concatenate([leave, split_sums(*sums)], axis=0), 'zh', s...  19.5 us
    ppermute x1, waiting for transfers between devices, per_device(): z[2] = lax.ppermute(weight, 'zl', Z_TWO)  19.2 us
    ppermute x1, waiting for transfers between devices, per_device(): z[4] = lax.ppermute(after(z[3], partner), 'zl', Z_RING)  17.8 us
    all_to_all x1, starting transfers between devices, per_device(): lax.all_to_all(packets, ('zl', 'x'), split_axis=0, concat_axis=0, tiled=T...  15.3 us
    ppermute x3, waiting for transfers between devices, per_device(): g.append(y_ring(g[-1]))  10.9 us
    ppermute x3, starting transfers between devices, per_device(): g.append(y_ring(g[-1]))  10.4 us
  transfers between devices with their start and end apart: 24, of which 11 were waited for; matrix products, arithmetic and copies ran while one was open for 4% of the time, Pallas kernels for 5%

profile of v2, /device:TPU:40, one launch (start us, length us, event | category | flops | bytes accessed | tf_op | source)
XLA Modules:
  0.0 294.3 jit_solution(9803538120710369594)
XLA Ops:
  7.2 0.7 and_select_fusion.1
  8.2 0.3 convolution_convert_fusion
  8.8 0.8 fusion.2
  9.6 15.3 %all-to-all-start = ((bf16[32,56,128]{2,1,0:T(8,128)(2,1)}), bf16[32,56,128]{2,1,0:T(8,128)(2,1)S(1)}, u32[]{:S(2)}, u32[]{:S(2)}) async-start(bf16[32,56,128]{2,1,0:T(8,128)(2,1)} %fusion.2), calls=%async_computation | async-start | bytes 917504 | tf_op jit(solution)/shard_map/all_to_all | solution.py:306
  25.0 0.7 copy-done.16
  25.8 2.1 collective-permute-start.6
  28.0 6.7 %collective-permute-start.8 = (bf16[192,768]{1,0:T(8,128)(2,1)}, bf16[192,768]{1,0:T(8,128)(2,1)S(1)}, u32[]{:S(2)}, u32[]{:S(2)}) collective-permute-start(bf16[192,768]{1,0:T(8,128)(2,1)} %copy-done.16), channel_id=1, source_target_pairs={{0,256},{128,384},{256,448},{384,320},{448,192},{320,64},{192,0},{... | collective-permute-start | bytes 884744 | tf_op jit(solution)/shard_map/ppermute | solution.py:312
  34.7 3.0 %collective-permute-start.9 = (bf16[192,768]{1,0:T(8,128)(2,1)}, bf16[192,768]{1,0:T(8,128)(2,1)S(1)}, u32[]{:S(2)}, u32[]{:S(2)}) collective-permute-start(bf16[192,768]{1,0:T(8,128)(2,1)} %copy-done.16), channel_id=1, source_target_pairs={{256,0},{384,128},{448,256},{320,384},{192,448},{64,320},{0,192},{... | collective-permute-start | bytes 884744 | tf_op jit(solution)/shard_map/ppermute | solution.py:313
  37.7 4.6 %collective-permute-start.7 = (bf16[192,768]{1,0:T(8,128)(2,1)}, bf16[192,768]{1,0:T(8,128)(2,1)S(1)}, u32[]{:S(2)}, u32[]{:S(2)}) collective-permute-start(bf16[192,768]{1,0:T(8,128)(2,1)} %copy-done.16), channel_id=1, source_target_pairs={{128,0},{256,128},{384,256},{448,384},{320,448},{192,320},{64,192}... | collective-permute-start | bytes 884744 | tf_op jit(solution)/shard_map/ppermute | solution.py:311
  42.3 24.3 %all-to-all-done = bf16[32,56,128]{2,1,0:T(8,128)(2,1)S(1)} async-done(((bf16[32,56,128]{2,1,0:T(8,128)(2,1)}), bf16[32,56,128]{2,1,0:T(8,128)(2,1)S(1)}, u32[]{:S(2)}, u32[]{:S(2)}) %all-to-all-start) | async-done | bytes 458784 | tf_op jit(solution)/shard_map/all_to_all | solution.py:306
  66.7 0.5 slice.180
  67.9 19.2 %collective-permute-done.8 = bf16[192,768]{1,0:T(8,128)(2,1)S(1)} collective-permute-done((bf16[192,768]{1,0:T(8,128)(2,1)}, bf16[192,768]{1,0:T(8,128)(2,1)S(1)}, u32[]{:S(2)}, u32[]{:S(2)}) %collective-permute-start.8) | collective-permute-done | bytes 294944 | tf_op jit(solution)/shard_map/ppermute | solution.py:312
  87.0 1.1 pad_maximum_fusion.1
  88.4 1.9 collective-permute-start.10
  90.3 0.3 convolution_convert_fusion.3
  90.6 0.3 convolution_convert_fusion.2
  91.0 0.3 convolution_convert_fusion.1
  91.3 8.2 %collective-permute-start = (bf16[384,256]{1,0:T(8,128)(2,1)S(1)}, bf16[384,256]{1,0:T(8,128)(2,1)S(1)}, u32[]{:S(2)}, u32[]{:S(2)}) collective-permute-start(bf16[384,256]{1,0:T(8,128)(2,1)S(1)} %get-tuple-element.39), channel_id=1, source_target_pairs={{0,2},{2,0},{1,3},{3,1},{4,6},{6,4},{5,7},{7,5},{8,10},{10,8},{9,1... | collective-permute-start | bytes 589832 | tf_op jit(solution)/shard_map/ppermute | solution.py:308
  99.5 4.8 %collective-permute-start.11 = (bf16[192,768]{1,0:T(8,128)(2,1)S(1)}, bf16[192,768]{1,0:T(8,128)(2,1)S(1)}, u32[]{:S(2)}, u32[]{:S(2)}) collective-permute-start(bf16[192,768]{1,0:T(8,128)(2,1)S(1)} %collective-permute-done.9), channel_id=1, source_target_pairs={{128,0},{256,128},{384,256},{448,384},{320,448},{192,320},{64,192}... | collective-permute-start | bytes 884744 | tf_op jit(solution)/shard_map/ppermute | solution.py:315
  104.4 10.0 %collective-permute-done = bf16[384,256]{1,0:T(8,128)(2,1)S(1)} collective-permute-done((bf16[384,256]{1,0:T(8,128)(2,1)S(1)}, bf16[384,256]{1,0:T(8,128)(2,1)S(1)}, u32[]{:S(2)}, u32[]{:S(2)}) %collective-permute-start) | collective-permute-done | bytes 196640 | tf_op jit(solution)/shard_map/ppermute | solution.py:308
  114.4 0.5 slice.181
  115.6 5.7 %collective-permute-start.12 = (bf16[192,768]{1,0:T(8,128)(2,1)S(1)}, bf16[192,768]{1,0:T(8,128)(2,1)S(1)}, u32[]{:S(2)}, u32[]{:S(2)}) collective-permute-start(bf16[192,768]{1,0:T(8,128)(2,1)S(1)} %broadcast_add_fusion), channel_id=1, source_target_pairs={{0,128},{128,256},{256,384},{384,448},{448,320},{320,192},{192,64}... | collective-permute-start | bytes 884744 | tf_op jit(solution)/shard_map/ppermute | solution.py:316
  121.4 17.8 %collective-permute-done.12 = bf16[192,768]{1,0:T(8,128)(2,1)S(1)} collective-permute-done((bf16[192,768]{1,0:T(8,128)(2,1)S(1)}, bf16[192,768]{1,0:T(8,128)(2,1)S(1)}, u32[]{:S(2)}, u32[]{:S(2)}) %collective-permute-start.12) | collective-permute-done | bytes 294944 | tf_op jit(solution)/shard_map/ppermute | solution.py:316
  139.3 3.7 %collective-permute-start.13 = (bf16[3,192,768]{2,1,0:T(8,128)(2,1)S(1)}, bf16[3,192,768]{2,1,0:T(8,128)(2,1)S(1)}, u32[]{:S(2)}, u32[]{:S(2)}) collective-permute-start(bf16[3,192,768]{2,1,0:T(8,128)(2,1)S(1)} %pad_maximum_fusion.2.late0_ref.rest_2_), channel_id=1, source_target_pairs={{0,16},{1,49},{16,32},{17,1},{32,48},{33,17},{48,0},{49,33},{2,18}... | collective-permute-start | bytes 2654216 | tf_op jit(solution)/shard_map/ppermute | solution.py:325
  143.0 3.5 %collective-permute-start.1 = (bf16[2,384,256]{2,1,0:T(8,128)(2,1)S(1)}, bf16[2,384,256]{2,1,0:T(8,128)(2,1)S(1)}, u32[]{:S(2)}, u32[]{:S(2)}) collective-permute-start(bf16[2,384,256]{2,1,0:T(8,128)(2,1)S(1)} %pad_maximum_fusion.4.rest_0_), channel_id=1, source_target_pairs={{0,4},{1,13},{4,8},{5,1},{8,12},{9,5},{12,0},{13,9},{2,6},{3,15},{... | collective-permute-start | bytes 1179656 | tf_op jit(solution)/shard_map/ppermute | solution.py:329
  146.5 0.7 copy-done.8
  147.2 5.4 %collective-permute-done.1.rest_1_ = bf16[2,384,256]{2,1,0:T(8,128)(2,1)S(1)} collective-permute-done((bf16[2,384,256]{2,1,0:T(8,128)(2,1)S(1)}, bf16[2,384,256]{2,1,0:T(8,128)(2,1)S(1)}, u32[]{:S(2)}, u32[]{:S(2)}) %collective-permute-start.1) | collective-permute-done | bytes 393248 | tf_op jit(solution)/shard_map/ppermute | solution.py:329
  152.7 3.5 %collective-permute-start.2 = (bf16[2,384,256]{2,1,0:T(8,128)(2,1)S(1)}, bf16[2,384,256]{2,1,0:T(8,128)(2,1)S(1)}, u32[]{:S(2)}, u32[]{:S(2)}) collective-permute-start(bf16[2,384,256]{2,1,0:T(8,128)(2,1)S(1)} %collective-permute-done.1.rest_1_), channel_id=1, source_target_pairs={{0,4},{1,13},{4,8},{5,1},{8,12},{9,5},{12,0},{13,9},{2,6},{3,15},{... | collective-permute-start | bytes 1179656 | tf_op jit(solution)/shard_map/ppermute | solution.py:329
  156.2 3.2 %collective-permute-start.14 = (bf16[3,192,768]{2,1,0:T(8,128)(2,1)S(1)}, bf16[3,192,768]{2,1,0:T(8,128)(2,1)}, u32[]{:S(2)}, u32[]{:S(2)}) collective-permute-start(bf16[3,192,768]{2,1,0:T(8,128)(2,1)S(1)} %collective-permute-done.13.late1_ref.rest_3_), channel_id=1, source_target_pairs={{0,16},{1,49},{16,32},{17,1},{32,48},{33,17},{48,0},{49,33},{2,18}... | collective-permute-start | bytes 2654216 | tf_op jit(solution)/shard_map/ppermute | solution.py:325
  159.3 3.0 %collective-permute-done.2.rest_2_ = bf16[2,384,256]{2,1,0:T(8,128)(2,1)S(1)} collective-permute-done((bf16[2,384,256]{2,1,0:T(8,128)(2,1)S(1)}, bf16[2,384,256]{2,1,0:T(8,128)(2,1)S(1)}, u32[]{:S(2)}, u32[]{:S(2)}) %collective-permute-start.2) | collective-permute-done | bytes 393248 | tf_op jit(solution)/shard_map/ppermute | solution.py:329
  162.3 1.2 pad_maximum_fusion
  163.5 0.8 copy-done.4
  164.3 1.9 collective-permute-start.4
  166.2 3.5 %collective-permute-start.3 = (bf16[2,384,256]{2,1,0:T(8,128)(2,1)S(1)}, bf16[2,384,256]{2,1,0:T(8,128)(2,1)}, u32[]{:S(2)}, u32[]{:S(2)}) collective-permute-start(bf16[2,384,256]{2,1,0:T(8,128)(2,1)S(1)} %collective-permute-done.2.rest_2_), channel_id=1, source_target_pairs={{0,4},{1,13},{4,8},{5,1},{8,12},{9,5},{12,0},{13,9},{2,6},{3,15},{... | collective-permute-start | bytes 1179656 | tf_op jit(solution)/shard_map/ppermute | solution.py:329
  169.7 2.7 collective-permute-done.14.late2_ref.rest_4_
  172.4 1.9 collective-permute-start.15
  174.4 2.5 collective-permute-done.3.rest_3_
  176.8 2.1 collective-permute-start.5
  178.9 1.7 copy.34.gain_ref
  180.7 1.0 copy.35.seg_col_ref
  181.8 1.0 copy-done.5
  182.8 1.0 copy-done.7
  183.8 1.0 copy-done.9
  184.8 4.2 %norm.1 = (bf16[6144,256]{1,0:T(8,128)(2,1)S(1)}, bf16[6144,256]{1,0:T(8,128)(2,1)S(1)}, f32[2,256]{1,0:T(2,128)S(1)}) custom-call(s32[5]{0:T(128)S(1)} %stack.44.where_ref, f32[6144,1]{1,0:T(8,128)S(1)} %copy.34.gain_ref, bf16[2,384,256]{2,1,0:T(8,128)(2,1)S(1)} %copy-done.9, bf16[2,384,256]{2,1,0:T(8,128)(2,1)S(1)} %copy-done.5, ...), custom_call_target="tpu_custom_call" | custom-call | flops 20000000 | bytes 10000000 | tf_op jit(solution)/shard_map/norm/pallas_call | solution.py:335
  189.1 1.7 copy-done.2
  190.8 1.7 copy-done.3
  192.5 0.6 copy-done.11
  193.1 9.2 %first.1.part_ref = f32[256,768]{1,0:T(8,128)} custom-call(s32[5]{0:T(128)} %copy-done.10, bf16[6144,256]{1,0:T(8,128)(2,1)} %copy-done.2, bf16[4,1,192,768]{3,2,1,0:T(8,128)(2,1)} %bitcast.45, bf16[4,4,192,768]{3,2,1,0:T(8,128)(2,1)} %bitcast.43, bf16[3,192,768]{2,1,0:T(8,128)(2,1)} %copy-done.13, bf16[3,192,768]{2,1,0:T(8,128)(2,1)} %copy-done.14, ...), custom_call_target="tpu_custom_call" | custom-call | flops 2200000000 | bytes 12000000 | tf_op jit(solution)/shard_map/first/pallas_call | solution.py:352
  202.3 22.2 %core.1 = (bf16[256,256]{1,0:T(8,128)(2,1)}, bf16[1536,256]{1,0:T(8,128)(2,1)}, bf16[1552,256]{1,0:T(8,128)(2,1)}, bf16[1536,256]{1,0:T(8,128)(2,1)}, bf16[1552,256]{1,0:T(8,128)(2,1)}) custom-call(s32[5]{0:T(128)} %copy-done.10, f32[6144,1]{1,0:T(8,128)} %copy-done.1, f32[2,256]{1,0:T(2,128)} %copy-done.11, s32[1,256]{1,0:T(1,128)} %bitcast.66, ...), custom_call_target="tpu_custom_call" | custom-call | flops 3000000000 | bytes 20000000 | tf_op jit(solution)/shard_map/core/pallas_call | solution.py:369
  224.5 2.4 collective-permute-start.17
  226.9 1.9 collective-permute-start.16
  228.8 0.7 slice_convert_fusion.4
  229.7 1.4 add_convert_fusion
  231.1 1.0 pad_maximum_fusion.3
  232.1 6.7 %all-to-all-start.2 = ((bf16[4,400,256]{2,1,0:T(8,128)(2,1)}), bf16[4,400,256]{2,1,0:T(8,128)(2,1)S(1)}, u32[]{:S(2)}, u32[]{:S(2)}) async-start(bf16[4,400,256]{2,1,0:T(8,128)(2,1)} %pad_maximum_fusion.3), calls=%async_computation.2 | async-start | bytes 1638400 | tf_op jit(solution)/shard_map/all_to_all | solution.py:396
  238.8 0.8 dynamic_slice.3
  239.6 1.1 add_convert_fusion.1
  240.6 10.3 %all-to-all-done.2 = bf16[4,400,256]{2,1,0:T(8,128)(2,1)S(1)} async-done(((bf16[4,400,256]{2,1,0:T(8,128)(2,1)}), bf16[4,400,256]{2,1,0:T(8,128)(2,1)S(1)}, u32[]{:S(2)}, u32[]{:S(2)}) %all-to-all-start.2) | async-done | bytes 819232 | tf_op jit(solution)/shard_map/all_to_all | solution.py:396
  250.9 4.9 %all-to-all-start.1 = ((bf16[4,384,256]{2,1,0:T(8,128)(2,1)}), bf16[4,384,256]{2,1,0:T(8,128)(2,1)S(1)}, u32[]{:S(2)}, u32[]{:S(2)}) async-start(bf16[4,384,256]{2,1,0:T(8,128)(2,1)} %bitcast.27), calls=%async_computation.1 | async-start | bytes 1572864 | tf_op jit(solution)/shard_map/all_to_all | solution.py:399
  256.0 0.2 concatenate.43
  256.3 8.3 %collective-permute-start.18 = (bf16[400,256]{1,0:T(8,128)(2,1)S(1)}, bf16[400,256]{1,0:T(8,128)(2,1)S(1)}, u32[]{:S(2)}, u32[]{:S(2)}) collective-permute-start(bf16[400,256]{1,0:T(8,128)(2,1)S(1)} %concatenate.43), channel_id=1, source_target_pairs={{0,2},{2,0},{1,3},{3,1},{4,6},{6,4},{5,7},{7,5},{8,10},{10,8},{9,1... | collective-permute-start | bytes 614408 | tf_op jit(solution)/shard_map/ppermute | solution.py:402
  264.6 2.3 all-to-all-done.1
  266.9 19.5 %collective-permute-done.18 = bf16[400,256]{1,0:T(8,128)(2,1)S(1)} collective-permute-done((bf16[400,256]{1,0:T(8,128)(2,1)S(1)}, bf16[400,256]{1,0:T(8,128)(2,1)S(1)}, u32[]{:S(2)}, u32[]{:S(2)}) %collective-permute-start.18) | collective-permute-done | bytes 204832 | tf_op jit(solution)/shard_map/ppermute | solution.py:402
  286.6 0.8 copy.37
  (87 shorter events, 1.9 us)
Async XLA Ops:
  7.2 1.0 copy-start
  8.1 16.8 %copy-start.17 = (bf16[192,256]{1,0:T(8,128)(2,1)S(1)}, bf16[192,256]{1,0:T(8,128)(2,1)}, u32[]{:S(2)}) copy-start(bf16[192,256]{1,0:T(8,128)(2,1)} %param.14) | copy-start | bytes 294916
  8.2 16.8 %copy-start.18 = (bf16[192,256]{1,0:T(8,128)(2,1)S(1)}, bf16[192,256]{1,0:T(8,128)(2,1)}, u32[]{:S(2)}) copy-start(bf16[192,256]{1,0:T(8,128)(2,1)} %param.15) | copy-start | bytes 294916
  8.5 16.5 %copy-start.19 = (bf16[192,256]{1,0:T(8,128)(2,1)S(1)}, bf16[192,256]{1,0:T(8,128)(2,1)}, u32[]{:S(2)}) copy-start(bf16[192,256]{1,0:T(8,128)(2,1)} %param.16) | copy-start | bytes 294916
  9.6 57.0 %all-to-all-start = ((bf16[32,56,128]{2,1,0:T(8,128)(2,1)}), bf16[32,56,128]{2,1,0:T(8,128)(2,1)S(1)}, u32[]{:S(2)}, u32[]{:S(2)}) async-start(bf16[32,56,128]{2,1,0:T(8,128)(2,1)} %fusion.2), calls=%async_computation | async-start | bytes 917504 | tf_op jit(solution)/shard_map/all_to_all | solution.py:306
  24.9 168.2 %all-gather.3.cloned.1.call-start = ((), (), s32[]{:S(2)}) async-start(), calls=%async_computation.3 | async-start | bytes 1474560 | tf_op jit(solution)/shard_map/all_gather | solution.py:319
  25.0 0.7 copy-start.16
  25.8 167.3 %all-gather.5.cloned.1.call-start = ((), (), s32[]{:S(2)}) async-start(), calls=%async_computation.4 | async-start | bytes 5898240 | tf_op jit(solution)/shard_map/all_gather | solution.py:319
  25.8 42.0 %collective-permute-start.6 = (bf16[192,768]{1,0:T(8,128)(2,1)}, bf16[192,768]{1,0:T(8,128)(2,1)S(1)}, u32[]{:S(2)}, u32[]{:S(2)}) collective-permute-start(bf16[192,768]{1,0:T(8,128)(2,1)} %copy-done.16), channel_id=1, source_target_pairs={{0,128},{128,256},{256,384},{384,448},{448,320},{320,192},{192,64}... | collective-permute-start | bytes 884744 | tf_op jit(solution)/shard_map/ppermute | solution.py:310
  28.0 59.1 %collective-permute-start.8 = (bf16[192,768]{1,0:T(8,128)(2,1)}, bf16[192,768]{1,0:T(8,128)(2,1)S(1)}, u32[]{:S(2)}, u32[]{:S(2)}) collective-permute-start(bf16[192,768]{1,0:T(8,128)(2,1)} %copy-done.16), channel_id=1, source_target_pairs={{0,256},{128,384},{256,448},{384,320},{448,192},{320,64},{192,0},{... | collective-permute-start | bytes 884744 | tf_op jit(solution)/shard_map/ppermute | solution.py:312
  34.7 52.4 %collective-permute-start.9 = (bf16[192,768]{1,0:T(8,128)(2,1)}, bf16[192,768]{1,0:T(8,128)(2,1)S(1)}, u32[]{:S(2)}, u32[]{:S(2)}) collective-permute-start(bf16[192,768]{1,0:T(8,128)(2,1)} %copy-done.16), channel_id=1, source_target_pairs={{256,0},{384,128},{448,256},{320,384},{192,448},{64,320},{0,192},{... | collective-permute-start | bytes 884744 | tf_op jit(solution)/shard_map/ppermute | solution.py:313
  37.7 49.3 %collective-permute-start.7 = (bf16[192,768]{1,0:T(8,128)(2,1)}, bf16[192,768]{1,0:T(8,128)(2,1)S(1)}, u32[]{:S(2)}, u32[]{:S(2)}) collective-permute-start(bf16[192,768]{1,0:T(8,128)(2,1)} %copy-done.16), channel_id=1, source_target_pairs={{128,0},{256,128},{384,256},{448,384},{320,448},{192,320},{64,192}... | collective-permute-start | bytes 884744 | tf_op jit(solution)/shard_map/ppermute | solution.py:311
  88.4 27.2 %collective-permute-start.10 = (bf16[192,768]{1,0:T(8,128)(2,1)S(1)}, bf16[192,768]{1,0:T(8,128)(2,1)S(1)}, u32[]{:S(2)}, u32[]{:S(2)}) collective-permute-start(bf16[192,768]{1,0:T(8,128)(2,1)S(1)} %broadcast_add_fusion.1), channel_id=1, source_target_pairs={{0,128},{128,256},{256,384},{384,448},{448,320},{320,192},{192,64}... | collective-permute-start | bytes 884744 | tf_op jit(solution)/shard_map/ppermute | solution.py:314
  91.3 23.1 %collective-permute-start = (bf16[384,256]{1,0:T(8,128)(2,1)S(1)}, bf16[384,256]{1,0:T(8,128)(2,1)S(1)}, u32[]{:S(2)}, u32[]{:S(2)}) collective-permute-start(bf16[384,256]{1,0:T(8,128)(2,1)S(1)} %get-tuple-element.39), channel_id=1, source_target_pairs={{0,2},{2,0},{1,3},{3,1},{4,6},{6,4},{5,7},{7,5},{8,10},{10,8},{9,1... | collective-permute-start | bytes 589832 | tf_op jit(solution)/shard_map/ppermute | solution.py:308
  99.5 21.8 %collective-permute-start.11 = (bf16[192,768]{1,0:T(8,128)(2,1)S(1)}, bf16[192,768]{1,0:T(8,128)(2,1)S(1)}, u32[]{:S(2)}, u32[]{:S(2)}) collective-permute-start(bf16[192,768]{1,0:T(8,128)(2,1)S(1)} %collective-permute-done.9), channel_id=1, source_target_pairs={{128,0},{256,128},{384,256},{448,384},{320,448},{192,320},{64,192}... | collective-permute-start | bytes 884744 | tf_op jit(solution)/shard_map/ppermute | solution.py:315
  115.6 23.5 %collective-permute-start.12 = (bf16[192,768]{1,0:T(8,128)(2,1)S(1)}, bf16[192,768]{1,0:T(8,128)(2,1)S(1)}, u32[]{:S(2)}, u32[]{:S(2)}) collective-permute-start(bf16[192,768]{1,0:T(8,128)(2,1)S(1)} %broadcast_add_fusion), channel_id=1, source_target_pairs={{0,128},{128,256},{256,384},{384,448},{448,320},{320,192},{192,64}... | collective-permute-start | bytes 884744 | tf_op jit(solution)/shard_map/ppermute | solution.py:316
  139.2 16.9 %copy-start.13 = (bf16[3,192,768]{2,1,0:T(8,128)(2,1)}, bf16[3,192,768]{2,1,0:T(8,128)(2,1)S(1)}, u32[]{:S(2)}) copy-start(bf16[3,192,768]{2,1,0:T(8,128)(2,1)S(1)} %pad_maximum_fusion.2.late0_ref.rest_2_) | copy-start | bytes 2654212
  139.3 16.9 %collective-permute-start.13 = (bf16[3,192,768]{2,1,0:T(8,128)(2,1)S(1)}, bf16[3,192,768]{2,1,0:T(8,128)(2,1)S(1)}, u32[]{:S(2)}, u32[]{:S(2)}) collective-permute-start(bf16[3,192,768]{2,1,0:T(8,128)(2,1)S(1)} %pad_maximum_fusion.2.late0_ref.rest_2_), channel_id=1, source_target_pairs={{0,16},{1,49},{16,32},{17,1},{32,48},{33,17},{48,0},{49,33},{2,18}... | collective-permute-start | bytes 2654216 | tf_op jit(solution)/shard_map/ppermute | solution.py:325
  143.0 9.7 %collective-permute-start.1 = (bf16[2,384,256]{2,1,0:T(8,128)(2,1)S(1)}, bf16[2,384,256]{2,1,0:T(8,128)(2,1)S(1)}, u32[]{:S(2)}, u32[]{:S(2)}) collective-permute-start(bf16[2,384,256]{2,1,0:T(8,128)(2,1)S(1)} %pad_maximum_fusion.4.rest_0_), channel_id=1, source_target_pairs={{0,4},{1,13},{4,8},{5,1},{8,12},{9,5},{12,0},{13,9},{2,6},{3,15},{... | collective-permute-start | bytes 1179656 | tf_op jit(solution)/shard_map/ppermute | solution.py:329
  146.5 0.8 copy-start.8
  152.7 9.7 %collective-permute-start.2 = (bf16[2,384,256]{2,1,0:T(8,128)(2,1)S(1)}, bf16[2,384,256]{2,1,0:T(8,128)(2,1)S(1)}, u32[]{:S(2)}, u32[]{:S(2)}) collective-permute-start(bf16[2,384,256]{2,1,0:T(8,128)(2,1)S(1)} %collective-permute-done.1.rest_1_), channel_id=1, source_target_pairs={{0,4},{1,13},{4,8},{5,1},{8,12},{9,5},{12,0},{13,9},{2,6},{3,15},{... | collective-permute-start | bytes 1179656 | tf_op jit(solution)/shard_map/ppermute | solution.py:329
  156.2 20.7 %copy-start.14 = (bf16[3,192,768]{2,1,0:T(8,128)(2,1)}, bf16[3,192,768]{2,1,0:T(8,128)(2,1)S(1)}, u32[]{:S(2)}) copy-start(bf16[3,192,768]{2,1,0:T(8,128)(2,1)S(1)} %collective-permute-done.13.late1_ref.rest_3_) | copy-start | bytes 2654212
  156.2 16.3 %collective-permute-start.14 = (bf16[3,192,768]{2,1,0:T(8,128)(2,1)S(1)}, bf16[3,192,768]{2,1,0:T(8,128)(2,1)}, u32[]{:S(2)}, u32[]{:S(2)}) collective-permute-start(bf16[3,192,768]{2,1,0:T(8,128)(2,1)S(1)} %collective-permute-done.13.late1_ref.rest_3_), channel_id=1, source_target_pairs={{0,16},{1,49},{16,32},{17,1},{32,48},{33,17},{48,0},{49,33},{2,18}... | collective-permute-start | bytes 2654216 | tf_op jit(solution)/shard_map/ppermute | solution.py:325
  162.3 3.9 %copy-start.6 = (bf16[2,384,256]{2,1,0:T(8,128)(2,1)}, bf16[2,384,256]{2,1,0:T(8,128)(2,1)S(1)}, u32[]{:S(2)}) copy-start(bf16[2,384,256]{2,1,0:T(8,128)(2,1)S(1)} %collective-permute-done.2.rest_2_) | copy-start | bytes 1179652
  163.5 0.8 copy-start.4
  164.3 17.6 %collective-permute-start.4 = (bf16[6,384,256]{2,1,0:T(8,128)(2,1)}, bf16[6,384,256]{2,1,0:T(8,128)(2,1)}, u32[]{:S(2)}, u32[]{:S(2)}) collective-permute-start(bf16[6,384,256]{2,1,0:T(8,128)(2,1)} %pad_maximum_fusion), channel_id=1, source_target_pairs={{0,1},{1,0},{2,3},{3,2},{4,5},{5,4},{6,7},{7,6},{8,9},{9,8},{10,11... | collective-permute-start | bytes 3538952 | tf_op jit(solution)/shard_map/ppermute | solution.py:330
  166.2 10.6 %collective-permute-start.3 = (bf16[2,384,256]{2,1,0:T(8,128)(2,1)S(1)}, bf16[2,384,256]{2,1,0:T(8,128)(2,1)}, u32[]{:S(2)}, u32[]{:S(2)}) collective-permute-start(bf16[2,384,256]{2,1,0:T(8,128)(2,1)S(1)} %collective-permute-done.2.rest_2_), channel_id=1, source_target_pairs={{0,4},{1,13},{4,8},{5,1},{8,12},{9,5},{12,0},{13,9},{2,6},{3,15},{... | collective-permute-start | bytes 1179656 | tf_op jit(solution)/shard_map/ppermute | solution.py:329
  172.4 29.8 %collective-permute-start.15 = (bf16[3,192,768]{2,1,0:T(8,128)(2,1)}, bf16[3,192,768]{2,1,0:T(8,128)(2,1)}, u32[]{:S(2)}, u32[]{:S(2)}) collective-permute-start(bf16[3,192,768]{2,1,0:T(8,128)(2,1)} %collective-permute-done.14.late2_ref.rest_4_), channel_id=1, source_target_pairs={{0,16},{1,49},{16,32},{17,1},{32,48},{33,17},{48,0},{49,33},{2,18}... | collective-permute-start | bytes 2654216 | tf_op jit(solution)/shard_map/ppermute | solution.py:325
  176.8 5.0 %collective-permute-start.5 = (bf16[2,384,256]{2,1,0:T(8,128)(2,1)}, bf16[2,384,256]{2,1,0:T(8,128)(2,1)}, u32[]{:S(2)}, u32[]{:S(2)}) collective-permute-start(bf16[2,384,256]{2,1,0:T(8,128)(2,1)} %collective-permute-done.3.rest_3_), channel_id=1, source_target_pairs={{0,1},{1,0},{2,3},{3,2},{4,5},{5,4},{6,7},{7,6},{8,9},{9,8},{10,11... | collective-permute-start | bytes 1179656 | tf_op jit(solution)/shard_map/ppermute | solution.py:331
  178.9 1.8 copy-start.20
  180.7 8.4 %copy-start.1 = (f32[6144,1]{1,0:T(8,128)}, f32[6144,1]{1,0:T(8,128)S(1)}, u32[]{:S(2)}) copy-start(f32[6144,1]{1,0:T(8,128)S(1)} %copy.34.gain_ref) | copy-start | bytes 73732
  181.8 7.3 %copy-start.10 = (s32[5]{0:T(128)}, s32[5]{0:T(128)S(1)}, u32[]{:S(2)}) copy-start(s32[5]{0:T(128)S(1)} %stack.44.where_ref) | copy-start | bytes 64
  181.8 1.0 copy-start.5
  182.8 1.0 copy-start.7
  183.8 1.0 copy-start.9
  189.1 1.7 copy-start.2
  190.8 1.7 copy-start.3
  192.5 0.6 copy-start.11
  224.5 5.1 %collective-permute-start.17 = (bf16[1552,256]{1,0:T(8,128)(2,1)}, bf16[1552,256]{1,0:T(8,128)(2,1)S(1)}, u32[]{:S(2)}, u32[]{:S(2)}) collective-permute-start(bf16[1552,256]{1,0:T(8,128)(2,1)} %get-tuple-element.17), channel_id=1, source_target_pairs={{0,1},{1,0},{2,3},{3,2},{4,5},{5,4},{6,7},{7,6},{8,9},{9,8},{10,11... | collective-permute-start | bytes 2383880 | tf_op jit(solution)/shard_map/ppermute | solution.py:392
  226.9 12.7 %collective-permute-start.16 = (bf16[1536,256]{1,0:T(8,128)(2,1)}, bf16[1536,256]{1,0:T(8,128)(2,1)S(1)}, u32[]{:S(2)}, u32[]{:S(2)}) collective-permute-start(bf16[1536,256]{1,0:T(8,128)(2,1)} %get-tuple-element.15), channel_id=1, source_target_pairs={{0,1},{1,0},{2,3},{3,2},{4,5},{5,4},{6,7},{7,6},{8,9},{9,8},{10,11... | collective-permute-start | bytes 2359304 | tf_op jit(solution)/shard_map/ppermute | solution.py:397
  231.1 8.4 %copy-start.15 = (bf16[1536,256]{1,0:T(8,128)(2,1)S(1)}, bf16[1536,256]{1,0:T(8,128)(2,1)}, u32[]{:S(2)}) copy-start(bf16[1536,256]{1,0:T(8,128)(2,1)} %get-tuple-element.14) | copy-start | bytes 2359300
  232.1 18.8 %all-to-all-start.2 = ((bf16[4,400,256]{2,1,0:T(8,128)(2,1)}), bf16[4,400,256]{2,1,0:T(8,128)(2,1)S(1)}, u32[]{:S(2)}, u32[]{:S(2)}) async-start(bf16[4,400,256]{2,1,0:T(8,128)(2,1)} %pad_maximum_fusion.3), calls=%async_computation.2 | async-start | bytes 1638400 | tf_op jit(solution)/shard_map/all_to_all | solution.py:396
  240.6 23.9 %copy-start.12 = (f32[2,256]{1,0:T(2,128)S(1)}, f32[2,256]{1,0:T(2,128)}, u32[]{:S(2)}) copy-start(f32[2,256]{1,0:T(2,128)} %copy-done.11) | copy-start | bytes 6148
  250.9 15.9 %all-to-all-start.1 = ((bf16[4,384,256]{2,1,0:T(8,128)(2,1)}), bf16[4,384,256]{2,1,0:T(8,128)(2,1)S(1)}, u32[]{:S(2)}, u32[]{:S(2)}) async-start(bf16[4,384,256]{2,1,0:T(8,128)(2,1)} %bitcast.27), calls=%async_computation.1 | async-start | bytes 1572864 | tf_op jit(solution)/shard_map/all_to_all | solution.py:399
  256.3 30.2 %collective-permute-start.18 = (bf16[400,256]{1,0:T(8,128)(2,1)S(1)}, bf16[400,256]{1,0:T(8,128)(2,1)S(1)}, u32[]{:S(2)}, u32[]{:S(2)}) collective-permute-start(bf16[400,256]{1,0:T(8,128)(2,1)S(1)} %concatenate.43), channel_id=1, source_target_pairs={{0,2},{2,0},{1,3},{3,1},{4,6},{6,4},{5,7},{7,5},{8,10},{10,8},{9,1... | collective-permute-start | bytes 614408 | tf_op jit(solution)/shard_map/ppermute | solution.py:402
Sparse Core Ops, SparseCore 0:
  27.8 30.8 all-gather.2
  88.3 57.4 all-gather.4

commit v3 on v2

--- a/solution.py
+++ b/solution.py
@@ -22,7 +22,6 @@
 FOLD = [0, 2, 4, 6, 7, 5, 3, 1]
 Z_RING = [(FOLD[i], FOLD[(i + 1) % NZ]) for i in range(NZ)]
 Z_BACK = [(b, a) for a, b in Z_RING]
-Z_TWO = [(FOLD[i], FOLD[(i + 2) % NZ]) for i in range(NZ)]
 EARLY = (0, 1, -1, 2, -2)
 FIRST = 1
 LATE = (3, -3, 4)
@@ -306,26 +305,28 @@
     got = lax.all_to_all(packets, ("zl", "x"), split_axis=0, concat_axis=0, tiled=True)
     mine = unpack(got)
     partner = lax.ppermute(mine, "zh", shift(NH, 1))
+    g = [jnp.stack([mine, partner])]
+    g.append(y_ring(g[0]))
+    wait_for = {2: got, 3: partner, 4: g[1]}
     z = {0: weight}
-    z[1] = lax.ppermute(weight, "zl", Z_RING)
-    z[-1] = lax.ppermute(weight, "zl", Z_BACK)
-    z[2] = lax.ppermute(weight, "zl", Z_TWO)
-    z[-2] = lax.ppermute(weight, "zl", [(b, a) for a, b in Z_TWO])
-    z[3] = lax.ppermute(after(z[2], got), "zl", Z_RING)
-    z[-3] = lax.ppermute(z[-2], "zl", Z_BACK)
-    z[4] = lax.ppermute(after(z[3], partner), "zl", Z_RING)
+    for step in (1, 2, 3, 4):
+        block = z[step - 1]
+        if step in wait_for:
+            block = after(block, wait_for[step])
+        z[step] = lax.ppermute(block, "zl", Z_RING)
+        if step < 4:
+            z[-step] = lax.ppermute(z[1 - step], "zl", Z_BACK)
     early = []
     for steps in (EARLY[:FIRST], EARLY[FIRST:]):
         joined = lax.all_gather(
-            jnp.concatenate([after(z[n], got) if n == 1 else z[n] for n in steps]),
+            jnp.concatenate([after(z[n], partner) if n == -1 else z[n] for n in steps]),
             "x", axis=0, tiled=True)
         early.append(joined.reshape((NX, len(steps)) + weight.shape))
     late = [jnp.stack([z[n] for n in LATE])]
     for _ in range(NX - 1):
         late.append(x_ring(late[-1]))
 
-    g = [jnp.stack([mine, partner])]
-    for _ in range(NY - 1):
+    for _ in range(NY - 2):
         g.append(y_ring(g[-1]))
     most = lax.ppermute(jnp.concatenate(g[:3]), "c", shift(NC, 1))
     last = lax.ppermute(g[3], "c", shift(NC, 1))
@@ -379,7 +380,7 @@
             pltpu.VMEM((LEN, 3 * width), BF),
             pltpu.SemaphoreType.DMA((3 * NX + len(LATE) + 1,)),
         ],
-        compiler_params=pltpu.CompilerParams(vmem_limit_bytes=54 << 20),
+        compiler_params=pltpu.CompilerParams(vmem_limit_bytes=36 << 20),
         cost_estimate=pl.CostEstimate(
             flops=3_000_000_000, bytes_accessed=20_000_000, transcendentals=131072),
         name="core",

time: 296 us -> 296 us (level)
  the two profiles are of different devices: /device:TPU:40 before, /device:TPU:14 now
where the time goes in v3:
time: 296 us; the launch traced here: 294 us
  waiting for transfers between devices  115 us (39%)
  starting transfers between devices  101 us (34%)
  Pallas kernels  32.9 us (11%)
  local copies, waits for them, and re-layouts  18 us (6%)
  between operations  16.9 us (6%)
  other arithmetic  8.2 us (3%)
    ppermute x3, waiting for transfers between devices, per_device(): late.append(x_ring(late[-1]))  33.5 us
    ppermute x3, waiting for transfers between devices, per_device(): z[-step] = lax.ppermute(z[1 - step], 'zl', Z_BACK)  26.3 us
    ppermute x4, waiting for transfers between devices, per_device(): z[step] = lax.ppermute(block, 'zl', Z_RING)  23.8 us
    ppermute x4, starting transfers between devices, per_device(): z[step] = lax.ppermute(block, 'zl', Z_RING)  23.1 us
    ppermute x1, waiting for transfers between devices, per_device(): lax.ppermute(jnp.concatenate([leave, split_sums(*sums)], axis=0), 'zh', s...  18.6 us
    pallas_call x1, Pallas kernels, per_device(): pl.pallas_call(main_kernel, out_shape=(jax.ShapeDtypeStruct((LEN, width),...  18.6 us
    all_to_all x1, starting transfers between devices, per_device(): lax.all_to_all(packets, ('zl', 'x'), split_axis=0, concat_axis=0, tiled=T...  15.6 us
    unnamed x73, local copies, waits for them, and re-layouts  13.7 us
  transfers between devices with their start and end apart: 24, of which 12 were waited for; matrix products, arithmetic and copies ran while one was open for 4% of the time, Pallas kernels for 5%

profile of v3, /device:TPU:14, one launch (start us, length us, event | category | flops | bytes accessed | tf_op | source)
XLA Modules:
  0.0 294.2 jit_solution(17492600589038063822)
XLA Ops:
  7.2 0.7 and_select_fusion.1
  8.2 0.3 convolution_convert_fusion
  8.8 0.8 fusion.2
  9.6 15.6 %all-to-all-start = ((bf16[32,56,128]{2,1,0:T(8,128)(2,1)}), bf16[32,56,128]{2,1,0:T(8,128)(2,1)S(1)}, u32[]{:S(2)}, u32[]{:S(2)}) async-start(bf16[32,56,128]{2,1,0:T(8,128)(2,1)} %fusion.2), calls=%async_computation | async-start | bytes 917504 | tf_op jit(solution)/shard_map/all_to_all | solution.py:305
  25.4 3.4 %collective-permute-start.7 = (bf16[192,768]{1,0:T(8,128)(2,1)S(1)}, bf16[192,768]{1,0:T(8,128)(2,1)S(1)}, u32[]{:S(2)}, u32[]{:S(2)}) collective-permute-start(bf16[192,768]{1,0:T(8,128)(2,1)S(1)} %constant_dynamic-update-slice_fusion), channel_id=1, source_target_pairs={{128,0},{256,128},{384,256},{448,384},{320,448},{192,320},{64,192}... | collective-permute-start | bytes 884744 | tf_op jit(solution)/shard_map/ppermute | solution.py:318
  28.8 3.4 %collective-permute-start.6 = (bf16[192,768]{1,0:T(8,128)(2,1)S(1)}, bf16[192,768]{1,0:T(8,128)(2,1)S(1)}, u32[]{:S(2)}, u32[]{:S(2)}) collective-permute-start(bf16[192,768]{1,0:T(8,128)(2,1)S(1)} %constant_dynamic-update-slice_fusion), channel_id=1, source_target_pairs={{0,128},{128,256},{256,384},{384,448},{448,320},{320,192},{192,64}... | collective-permute-start | bytes 884744 | tf_op jit(solution)/shard_map/ppermute | solution.py:316
  32.3 23.0 %collective-permute-done.7 = bf16[192,768]{1,0:T(8,128)(2,1)S(1)} collective-permute-done((bf16[192,768]{1,0:T(8,128)(2,1)S(1)}, bf16[192,768]{1,0:T(8,128)(2,1)S(1)}, u32[]{:S(2)}, u32[]{:S(2)}) %collective-permute-start.7) | collective-permute-done | bytes 294944 | tf_op jit(solution)/shard_map/ppermute | solution.py:318
  55.2 1.9 collective-permute-start.9
  57.3 0.3 convolution_convert_fusion.3
  57.6 0.3 convolution_convert_fusion.2
  58.0 0.3 convolution_convert_fusion.1
  58.6 0.3 copy-done.29
  58.9 8.2 %collective-permute-start = (bf16[384,256]{1,0:T(8,128)(2,1)S(1)}, bf16[384,256]{1,0:T(8,128)(2,1)S(1)}, u32[]{:S(2)}, u32[]{:S(2)}) collective-permute-start(bf16[384,256]{1,0:T(8,128)(2,1)S(1)} %get-tuple-element.37), channel_id=1, source_target_pairs={{0,2},{2,0},{1,3},{3,1},{4,6},{6,4},{5,7},{7,5},{8,10},{10,8},{9,1... | collective-permute-start | bytes 589832 | tf_op jit(solution)/shard_map/ppermute | solution.py:307
  67.1 0.5 slice.185
  68.3 10.4 %collective-permute-start.8 = (bf16[192,768]{1,0:T(8,128)(2,1)S(1)}, bf16[192,768]{1,0:T(8,128)(2,1)S(1)}, u32[]{:S(2)}, u32[]{:S(2)}) collective-permute-start(bf16[192,768]{1,0:T(8,128)(2,1)S(1)} %broadcast_add_fusion.1), channel_id=1, source_target_pairs={{0,128},{128,256},{256,384},{384,448},{448,320},{320,192},{192,64}... | collective-permute-start | bytes 884744 | tf_op jit(solution)/shard_map/ppermute | solution.py:316
  78.8 0.5 slice.184
  80.0 15.6 %collective-permute-done.8 = bf16[192,768]{1,0:T(8,128)(2,1)S(1)} collective-permute-done((bf16[192,768]{1,0:T(8,128)(2,1)S(1)}, bf16[192,768]{1,0:T(8,128)(2,1)S(1)}, u32[]{:S(2)}, u32[]{:S(2)}) %collective-permute-start.8) | collective-permute-done | bytes 294944 | tf_op jit(solution)/shard_map/ppermute | solution.py:316
  95.6 1.1 pad_maximum_fusion.1
  96.8 3.5 %collective-permute-start.1 = (bf16[2,384,256]{2,1,0:T(8,128)(2,1)S(1)}, bf16[2,384,256]{2,1,0:T(8,128)(2,1)S(1)}, u32[]{:S(2)}, u32[]{:S(2)}) collective-permute-start(bf16[2,384,256]{2,1,0:T(8,128)(2,1)S(1)} %pad_maximum_fusion.4.rest_0_), channel_id=1, source_target_pairs={{0,4},{1,13},{4,8},{5,1},{8,12},{9,5},{12,0},{13,9},{2,6},{3,15},{... | collective-permute-start | bytes 1179656 | tf_op jit(solution)/shard_map/ppermute | solution.py:309
  100.3 3.9 %collective-permute-start.10 = (bf16[192,768]{1,0:T(8,128)(2,1)S(1)}, bf16[192,768]{1,0:T(8,128)(2,1)S(1)}, u32[]{:S(2)}, u32[]{:S(2)}) collective-permute-start(bf16[192,768]{1,0:T(8,128)(2,1)S(1)} %broadcast_add_fusion.2), channel_id=1, source_target_pairs={{0,128},{128,256},{256,384},{384,448},{448,320},{320,192},{192,64}... | collective-permute-start | bytes 884744 | tf_op jit(solution)/shard_map/ppermute | solution.py:316
  104.3 1.9 collective-permute-start.11
  106.5 0.5 slice.186
  107.7 3.9 %collective-permute-done.10 = bf16[192,768]{1,0:T(8,128)(2,1)S(1)} collective-permute-done((bf16[192,768]{1,0:T(8,128)(2,1)S(1)}, bf16[192,768]{1,0:T(8,128)(2,1)S(1)}, u32[]{:S(2)}, u32[]{:S(2)}) %collective-permute-start.10) | collective-permute-done | bytes 294944 | tf_op jit(solution)/shard_map/ppermute | solution.py:316
  111.6 5.4 %collective-permute-start.12 = (bf16[192,768]{1,0:T(8,128)(2,1)S(1)}, bf16[192,768]{1,0:T(8,128)(2,1)S(1)}, u32[]{:S(2)}, u32[]{:S(2)}) collective-permute-start(bf16[192,768]{1,0:T(8,128)(2,1)S(1)} %broadcast_add_fusion), channel_id=1, source_target_pairs={{0,128},{128,256},{256,384},{384,448},{448,320},{320,192},{192,64}... | collective-permute-start | bytes 884744 | tf_op jit(solution)/shard_map/ppermute | solution.py:316
  117.0 3.4 %collective-permute-done.11 = bf16[192,768]{1,0:T(8,128)(2,1)S(1)} collective-permute-done((bf16[192,768]{1,0:T(8,128)(2,1)S(1)}, bf16[192,768]{1,0:T(8,128)(2,1)S(1)}, u32[]{:S(2)}, u32[]{:S(2)}) %collective-permute-start.11) | collective-permute-done | bytes 294944 | tf_op jit(solution)/shard_map/ppermute | solution.py:318
  120.4 4.3 %collective-permute-done.12 = bf16[192,768]{1,0:T(8,128)(2,1)S(1)} collective-permute-done((bf16[192,768]{1,0:T(8,128)(2,1)S(1)}, bf16[192,768]{1,0:T(8,128)(2,1)S(1)}, u32[]{:S(2)}, u32[]{:S(2)}) %collective-permute-start.12) | collective-permute-done | bytes 294944 | tf_op jit(solution)/shard_map/ppermute | solution.py:316
  124.8 0.9 copy-done.3
  125.7 2.2 collective-permute-start.13
  127.9 3.5 %collective-permute-start.2 = (bf16[2,384,256]{2,1,0:T(8,128)(2,1)S(1)}, bf16[2,384,256]{2,1,0:T(8,128)(2,1)S(1)}, u32[]{:S(2)}, u32[]{:S(2)}) collective-permute-start(bf16[2,384,256]{2,1,0:T(8,128)(2,1)S(1)} %collective-permute-done.1.rest_1_), channel_id=1, source_target_pairs={{0,4},{1,13},{4,8},{5,1},{8,12},{9,5},{12,0},{13,9},{2,6},{3,15},{... | collective-permute-start | bytes 1179656 | tf_op jit(solution)/shard_map/ppermute | solution.py:330
  131.4 28.3 %collective-permute-done.13.late1_ref.rest_3_ = bf16[3,192,768]{2,1,0:T(8,128)(2,1)S(1)} collective-permute-done((bf16[3,192,768]{2,1,0:T(8,128)(2,1)S(1)}, bf16[3,192,768]{2,1,0:T(8,128)(2,1)S(1)}, u32[]{:S(2)}, u32[]{:S(2)}) %collective-permute-start.13) | collective-permute-done | bytes 884768 | tf_op jit(solution)/shard_map/ppermute | solution.py:327
  159.7 0.9 copy-done.6
  160.6 3.2 %collective-permute-start.14 = (bf16[3,192,768]{2,1,0:T(8,128)(2,1)S(1)}, bf16[3,192,768]{2,1,0:T(8,128)(2,1)}, u32[]{:S(2)}, u32[]{:S(2)}) collective-permute-start(bf16[3,192,768]{2,1,0:T(8,128)(2,1)S(1)} %collective-permute-done.13.late1_ref.rest_3_), channel_id=1, source_target_pairs={{0,16},{1,49},{16,32},{17,1},{32,48},{33,17},{48,0},{49,33},{2,18}... | collective-permute-start | bytes 2654216 | tf_op jit(solution)/shard_map/ppermute | solution.py:327
  163.9 1.2 pad_maximum_fusion
  165.1 1.9 collective-permute-start.4
  167.0 3.5 %collective-permute-start.3 = (bf16[2,384,256]{2,1,0:T(8,128)(2,1)S(1)}, bf16[2,384,256]{2,1,0:T(8,128)(2,1)}, u32[]{:S(2)}, u32[]{:S(2)}) collective-permute-start(bf16[2,384,256]{2,1,0:T(8,128)(2,1)S(1)} %collective-permute-done.2.rest_2_), channel_id=1, source_target_pairs={{0,4},{1,13},{4,8},{5,1},{8,12},{9,5},{12,0},{13,9},{2,6},{3,15},{... | collective-permute-start | bytes 1179656 | tf_op jit(solution)/shard_map/ppermute | solution.py:330
  170.5 5.2 %collective-permute-done.14.late2_ref.rest_4_ = bf16[3,192,768]{2,1,0:T(8,128)(2,1)} collective-permute-done((bf16[3,192,768]{2,1,0:T(8,128)(2,1)S(1)}, bf16[3,192,768]{2,1,0:T(8,128)(2,1)}, u32[]{:S(2)}, u32[]{:S(2)}) %collective-permute-start.14) | collective-permute-done | bytes 884768 | tf_op jit(solution)/shard_map/ppermute | solution.py:327
  175.7 4.4 %collective-permute-start.15 = (bf16[3,192,768]{2,1,0:T(8,128)(2,1)}, bf16[3,192,768]{2,1,0:T(8,128)(2,1)}, u32[]{:S(2)}, u32[]{:S(2)}) collective-permute-start(bf16[3,192,768]{2,1,0:T(8,128)(2,1)} %collective-permute-done.14.late2_ref.rest_4_), channel_id=1, source_target_pairs={{0,16},{1,49},{16,32},{17,1},{32,48},{33,17},{48,0},{49,33},{2,18}... | collective-permute-start | bytes 2654216 | tf_op jit(solution)/shard_map/ppermute | solution.py:327
  180.1 2.1 collective-permute-start.5
  182.3 1.1 copy.25.gain_ref
  183.6 0.5 collective-permute-done.5.rest_5_
  184.1 1.0 copy-done.12
  185.1 1.0 copy-done.14
  186.1 1.0 copy-done.16
  187.1 4.2 %norm.1 = (bf16[6144,256]{1,0:T(8,128)(2,1)S(1)}, bf16[6144,256]{1,0:T(8,128)(2,1)S(1)}, f32[2,256]{1,0:T(2,128)S(1)}) custom-call(s32[5]{0:T(128)S(1)} %stack.44.where_ref, f32[6144,1]{1,0:T(8,128)S(1)} %copy.25.gain_ref, bf16[2,384,256]{2,1,0:T(8,128)(2,1)S(1)} %copy-done.16, bf16[2,384,256]{2,1,0:T(8,128)(2,1)S(1)} %copy-done.12, ...), custom_call_target="tpu_custom_call" | custom-call | flops 20000000 | bytes 10000000 | tf_op jit(solution)/shard_map/norm/pallas_call | solution.py:336
  191.4 1.7 copy-done.1
  193.0 1.7 copy-done.9
  194.8 10.1 %first.1.part_ref = f32[256,768]{1,0:T(8,128)} custom-call(s32[5]{0:T(128)} %copy-done.21, bf16[6144,256]{1,0:T(8,128)(2,1)} %copy-done.1, bf16[4,1,192,768]{3,2,1,0:T(8,128)(2,1)} %bitcast.44, bf16[4,4,192,768]{3,2,1,0:T(8,128)(2,1)} %bitcast.50, bf16[3,192,768]{2,1,0:T(8,128)(2,1)} %copy-done.3, bf16[3,192,768]{2,1,0:T(8,128)(2,1)} %copy-done.6, ...), custom_call_target="tpu_custom_call" | custom-call | flops 2200000000 | bytes 12000000 | tf_op jit(solution)/shard_map/first/pallas_call | solution.py:353
  205.0 1.1 copy-done.8
  206.2 1.9 copy-done.10
  208.1 18.6 %core.1 = (bf16[256,256]{1,0:T(8,128)(2,1)}, bf16[1536,256]{1,0:T(8,128)(2,1)S(1)}, bf16[1552,256]{1,0:T(8,128)(2,1)S(1)}, bf16[1536,256]{1,0:T(8,128)(2,1)}, bf16[1552,256]{1,0:T(8,128)(2,1)S(1)}) custom-call(s32[5]{0:T(128)S(1)} %copy-done.22, f32[6144,1]{1,0:T(8,128)S(1)} %copy.25.gain_ref, f32[2,256]{1,0:T(2,128)S(1)} %get-tuple-element.10.stat_ref, ...), custom_call_target="tpu_custom_call" | custom-call | flops 3000000000 | bytes 20000000 | tf_op jit(solution)/shard_map/core/pallas_call | solution.py:370
  226.6 0.9 copy-done.18
  227.5 2.0 collective-permute-start.17
  229.5 2.3 collective-permute-start.16
  232.1 1.3 add_convert_fusion
  233.4 1.0 pad_maximum_fusion.3
  234.4 6.0 %all-to-all-start.2 = ((bf16[4,400,256]{2,1,0:T(8,128)(2,1)}), bf16[4,400,256]{2,1,0:T(8,128)(2,1)S(1)}, u32[]{:S(2)}, u32[]{:S(2)}) async-start(bf16[4,400,256]{2,1,0:T(8,128)(2,1)} %pad_maximum_fusion.3), calls=%async_computation.2 | async-start | bytes 1638400 | tf_op jit(solution)/shard_map/all_to_all | solution.py:397
  240.4 0.8 dynamic_slice.3
  241.2 1.1 add_convert_fusion.1
  242.3 9.9 %all-to-all-done.2 = bf16[4,400,256]{2,1,0:T(8,128)(2,1)S(1)} async-done(((bf16[4,400,256]{2,1,0:T(8,128)(2,1)}), bf16[4,400,256]{2,1,0:T(8,128)(2,1)S(1)}, u32[]{:S(2)}, u32[]{:S(2)}) %all-to-all-start.2) | async-done | bytes 819232 | tf_op jit(solution)/shard_map/all_to_all | solution.py:397
  252.2 4.9 %all-to-all-start.1 = ((bf16[4,384,256]{2,1,0:T(8,128)(2,1)}), bf16[4,384,256]{2,1,0:T(8,128)(2,1)S(1)}, u32[]{:S(2)}, u32[]{:S(2)}) async-start(bf16[4,384,256]{2,1,0:T(8,128)(2,1)} %bitcast.28), calls=%async_computation.1 | async-start | bytes 1572864 | tf_op jit(solution)/shard_map/all_to_all | solution.py:400
  257.5 7.7 %collective-permute-start.18 = (bf16[400,256]{1,0:T(8,128)(2,1)S(1)}, bf16[400,256]{1,0:T(8,128)(2,1)S(1)}, u32[]{:S(2)}, u32[]{:S(2)}) collective-permute-start(bf16[400,256]{1,0:T(8,128)(2,1)S(1)} %concatenate.43), channel_id=1, source_target_pairs={{0,2},{2,0},{1,3},{3,1},{4,6},{6,4},{5,7},{7,5},{8,10},{10,8},{9,1... | collective-permute-start | bytes 614408 | tf_op jit(solution)/shard_map/ppermute | solution.py:403
  265.3 2.4 all-to-all-done.1
  267.8 18.6 %collective-permute-done.18 = bf16[400,256]{1,0:T(8,128)(2,1)S(1)} collective-permute-done((bf16[400,256]{1,0:T(8,128)(2,1)S(1)}, bf16[400,256]{1,0:T(8,128)(2,1)S(1)}, u32[]{:S(2)}, u32[]{:S(2)}) %collective-permute-start.18) | collective-permute-done | bytes 204832 | tf_op jit(solution)/shard_map/ppermute | solution.py:403
  286.6 0.8 copy.28
  (117 shorter events, 2.9 us)
Async XLA Ops:
  7.2 1.0 copy-start
  8.1 17.2 %copy-start.31 = (bf16[192,256]{1,0:T(8,128)(2,1)S(1)}, bf16[192,256]{1,0:T(8,128)(2,1)}, u32[]{:S(2)}) copy-start(bf16[192,256]{1,0:T(8,128)(2,1)} %param.14) | copy-start | bytes 294916
  8.2 17.2 %copy-start.32 = (bf16[192,256]{1,0:T(8,128)(2,1)S(1)}, bf16[192,256]{1,0:T(8,128)(2,1)}, u32[]{:S(2)}) copy-start(bf16[192,256]{1,0:T(8,128)(2,1)} %param.15) | copy-start | bytes 294916
  8.5 16.9 %copy-start.33 = (bf16[192,256]{1,0:T(8,128)(2,1)S(1)}, bf16[192,256]{1,0:T(8,128)(2,1)}, u32[]{:S(2)}) copy-start(bf16[192,256]{1,0:T(8,128)(2,1)} %param.16) | copy-start | bytes 294916
  9.6 47.5 %all-to-all-start = ((bf16[32,56,128]{2,1,0:T(8,128)(2,1)}), bf16[32,56,128]{2,1,0:T(8,128)(2,1)S(1)}, u32[]{:S(2)}, u32[]{:S(2)}) async-start(bf16[32,56,128]{2,1,0:T(8,128)(2,1)} %fusion.2), calls=%async_computation | async-start | bytes 917504 | tf_op jit(solution)/shard_map/all_to_all | solution.py:305
  25.3 169.5 %all-gather.3.cloned.1.call-start = ((), (), s32[]{:S(2)}) async-start(), calls=%async_computation.3 | async-start | bytes 1474560 | tf_op jit(solution)/shard_map/all_gather | solution.py:321
  25.4 6.8 %copy-start.26 = (bf16[192,768]{1,0:T(8,128)(2,1)}, bf16[192,768]{1,0:T(8,128)(2,1)S(1)}, u32[]{:S(2)}) copy-start(bf16[192,768]{1,0:T(8,128)(2,1)S(1)} %constant_dynamic-update-slice_fusion) | copy-start | bytes 884740
  25.4 29.8 %collective-permute-start.7 = (bf16[192,768]{1,0:T(8,128)(2,1)S(1)}, bf16[192,768]{1,0:T(8,128)(2,1)S(1)}, u32[]{:S(2)}, u32[]{:S(2)}) collective-permute-start(bf16[192,768]{1,0:T(8,128)(2,1)S(1)} %constant_dynamic-update-slice_fusion), channel_id=1, source_target_pairs={{128,0},{256,128},{384,256},{448,384},{320,448},{192,320},{64,192}... | collective-permute-start | bytes 884744 | tf_op jit(solution)/shard_map/ppermute | solution.py:318
  28.8 39.5 %collective-permute-start.6 = (bf16[192,768]{1,0:T(8,128)(2,1)S(1)}, bf16[192,768]{1,0:T(8,128)(2,1)S(1)}, u32[]{:S(2)}, u32[]{:S(2)}) collective-permute-start(bf16[192,768]{1,0:T(8,128)(2,1)S(1)} %constant_dynamic-update-slice_fusion), channel_id=1, source_target_pairs={{0,128},{128,256},{256,384},{384,448},{448,320},{320,192},{192,64}... | collective-permute-start | bytes 884744 | tf_op jit(solution)/shard_map/ppermute | solution.py:316
  32.2 162.6 %all-gather.5.cloned.1.call-start = ((), (), s32[]{:S(2)}) async-start(), calls=%async_computation.4 | async-start | bytes 5898240 | tf_op jit(solution)/shard_map/all_gather | solution.py:321
  55.2 24.8 %collective-permute-start.9 = (bf16[192,768]{1,0:T(8,128)(2,1)S(1)}, bf16[192,768]{1,0:T(8,128)(2,1)S(1)}, u32[]{:S(2)}, u32[]{:S(2)}) collective-permute-start(bf16[192,768]{1,0:T(8,128)(2,1)S(1)} %collective-permute-done.7), channel_id=1, source_target_pairs={{128,0},{256,128},{384,256},{448,384},{320,448},{192,320},{64,192}... | collective-permute-start | bytes 884744 | tf_op jit(solution)/shard_map/ppermute | solution.py:318
  58.0 0.6 copy-start.27
  58.3 0.6 copy-start.29
  58.9 19.9 %collective-permute-start = (bf16[384,256]{1,0:T(8,128)(2,1)S(1)}, bf16[384,256]{1,0:T(8,128)(2,1)S(1)}, u32[]{:S(2)}, u32[]{:S(2)}) collective-permute-start(bf16[384,256]{1,0:T(8,128)(2,1)S(1)} %get-tuple-element.37), channel_id=1, source_target_pairs={{0,2},{2,0},{1,3},{3,1},{4,6},{6,4},{5,7},{7,5},{8,10},{10,8},{9,1... | collective-permute-start | bytes 589832 | tf_op jit(solution)/shard_map/ppermute | solution.py:307
  68.3 27.3 %collective-permute-start.8 = (bf16[192,768]{1,0:T(8,128)(2,1)S(1)}, bf16[192,768]{1,0:T(8,128)(2,1)S(1)}, u32[]{:S(2)}, u32[]{:S(2)}) collective-permute-start(bf16[192,768]{1,0:T(8,128)(2,1)S(1)} %broadcast_add_fusion.1), channel_id=1, source_target_pairs={{0,128},{128,256},{256,384},{384,448},{448,320},{320,192},{192,64}... | collective-permute-start | bytes 884744 | tf_op jit(solution)/shard_map/ppermute | solution.py:316
  96.8 27.9 %copy-start.15 = (bf16[2,384,256]{2,1,0:T(8,128)(2,1)}, bf16[2,384,256]{2,1,0:T(8,128)(2,1)S(1)}, u32[]{:S(2)}) copy-start(bf16[2,384,256]{2,1,0:T(8,128)(2,1)S(1)} %pad_maximum_fusion.4.rest_0_) | copy-start | bytes 1179652
  96.8 9.7 %collective-permute-start.1 = (bf16[2,384,256]{2,1,0:T(8,128)(2,1)S(1)}, bf16[2,384,256]{2,1,0:T(8,128)(2,1)S(1)}, u32[]{:S(2)}, u32[]{:S(2)}) collective-permute-start(bf16[2,384,256]{2,1,0:T(8,128)(2,1)S(1)} %pad_maximum_fusion.4.rest_0_), channel_id=1, source_target_pairs={{0,4},{1,13},{4,8},{5,1},{8,12},{9,5},{12,0},{13,9},{2,6},{3,15},{... | collective-permute-start | bytes 1179656 | tf_op jit(solution)/shard_map/ppermute | solution.py:309
  100.3 11.2 %collective-permute-start.10 = (bf16[192,768]{1,0:T(8,128)(2,1)S(1)}, bf16[192,768]{1,0:T(8,128)(2,1)S(1)}, u32[]{:S(2)}, u32[]{:S(2)}) collective-permute-start(bf16[192,768]{1,0:T(8,128)(2,1)S(1)} %broadcast_add_fusion.2), channel_id=1, source_target_pairs={{0,128},{128,256},{256,384},{384,448},{448,320},{320,192},{192,64}... | collective-permute-start | bytes 884744 | tf_op jit(solution)/shard_map/ppermute | solution.py:316
  104.3 16.1 %collective-permute-start.11 = (bf16[192,768]{1,0:T(8,128)(2,1)S(1)}, bf16[192,768]{1,0:T(8,128)(2,1)S(1)}, u32[]{:S(2)}, u32[]{:S(2)}) collective-permute-start(bf16[192,768]{1,0:T(8,128)(2,1)S(1)} %collective-permute-done.9), channel_id=1, source_target_pairs={{128,0},{256,128},{384,256},{448,384},{320,448},{192,320},{64,192}... | collective-permute-start | bytes 884744 | tf_op jit(solution)/shard_map/ppermute | solution.py:318
  106.5 58.6 %copy-start.11 = (bf16[2,384,256]{2,1,0:T(8,128)(2,1)}, bf16[2,384,256]{2,1,0:T(8,128)(2,1)S(1)}, u32[]{:S(2)}) copy-start(bf16[2,384,256]{2,1,0:T(8,128)(2,1)S(1)} %collective-permute-done.1.rest_1_) | copy-start | bytes 1179652
  111.6 13.1 %collective-permute-start.12 = (bf16[192,768]{1,0:T(8,128)(2,1)S(1)}, bf16[192,768]{1,0:T(8,128)(2,1)S(1)}, u32[]{:S(2)}, u32[]{:S(2)}) collective-permute-start(bf16[192,768]{1,0:T(8,128)(2,1)S(1)} %broadcast_add_fusion), channel_id=1, source_target_pairs={{0,128},{128,256},{256,384},{384,448},{448,320},{320,192},{192,64}... | collective-permute-start | bytes 884744 | tf_op jit(solution)/shard_map/ppermute | solution.py:316
  124.8 0.9 copy-start.3
  125.7 56.5 %copy-start.34 = (f32[6144]{0:T(1024)S(1)}, f32[6144]{0:T(1024)}, u32[]{:S(2)}) copy-start(f32[6144]{0:T(1024)} %param.13) | copy-start | bytes 73732
  125.7 34.0 %collective-permute-start.13 = (bf16[3,192,768]{2,1,0:T(8,128)(2,1)S(1)}, bf16[3,192,768]{2,1,0:T(8,128)(2,1)S(1)}, u32[]{:S(2)}, u32[]{:S(2)}) collective-permute-start(bf16[3,192,768]{2,1,0:T(8,128)(2,1)S(1)} %pad_maximum_fusion.2.late0_ref.rest_2_), channel_id=1, source_target_pairs={{0,16},{1,49},{16,32},{17,1},{32,48},{33,17},{48,0},{49,33},{2,18}... | collective-permute-start | bytes 2654216 | tf_op jit(solution)/shard_map/ppermute | solution.py:327
  127.9 36.0 %collective-permute-start.2 = (bf16[2,384,256]{2,1,0:T(8,128)(2,1)S(1)}, bf16[2,384,256]{2,1,0:T(8,128)(2,1)S(1)}, u32[]{:S(2)}, u32[]{:S(2)}) collective-permute-start(bf16[2,384,256]{2,1,0:T(8,128)(2,1)S(1)} %collective-permute-done.1.rest_1_), channel_id=1, source_target_pairs={{0,4},{1,13},{4,8},{5,1},{8,12},{9,5},{12,0},{13,9},{2,6},{3,15},{... | collective-permute-start | bytes 1179656 | tf_op jit(solution)/shard_map/ppermute | solution.py:330
  159.7 0.9 copy-start.6
  160.6 15.0 %collective-permute-start.14 = (bf16[3,192,768]{2,1,0:T(8,128)(2,1)S(1)}, bf16[3,192,768]{2,1,0:T(8,128)(2,1)}, u32[]{:S(2)}, u32[]{:S(2)}) collective-permute-start(bf16[3,192,768]{2,1,0:T(8,128)(2,1)S(1)} %collective-permute-done.13.late1_ref.rest_3_), channel_id=1, source_target_pairs={{0,16},{1,49},{16,32},{17,1},{32,48},{33,17},{48,0},{49,33},{2,18}... | collective-permute-start | bytes 2654216 | tf_op jit(solution)/shard_map/ppermute | solution.py:327
  163.9 11.8 %copy-start.13 = (bf16[2,384,256]{2,1,0:T(8,128)(2,1)}, bf16[2,384,256]{2,1,0:T(8,128)(2,1)S(1)}, u32[]{:S(2)}) copy-start(bf16[2,384,256]{2,1,0:T(8,128)(2,1)S(1)} %collective-permute-done.2.rest_2_) | copy-start | bytes 1179652
  165.1 19.0 %collective-permute-start.4 = (bf16[6,384,256]{2,1,0:T(8,128)(2,1)}, bf16[6,384,256]{2,1,0:T(8,128)(2,1)}, u32[]{:S(2)}, u32[]{:S(2)}) collective-permute-start(bf16[6,384,256]{2,1,0:T(8,128)(2,1)} %pad_maximum_fusion), channel_id=1, source_target_pairs={{0,1},{1,0},{2,3},{3,2},{4,5},{5,4},{6,7},{7,6},{8,9},{9,8},{10,11... | collective-permute-start | bytes 3538952 | tf_op jit(solution)/shard_map/ppermute | solution.py:331
  167.0 13.2 %collective-permute-start.3 = (bf16[2,384,256]{2,1,0:T(8,128)(2,1)S(1)}, bf16[2,384,256]{2,1,0:T(8,128)(2,1)}, u32[]{:S(2)}, u32[]{:S(2)}) collective-permute-start(bf16[2,384,256]{2,1,0:T(8,128)(2,1)S(1)} %collective-permute-done.2.rest_2_), channel_id=1, source_target_pairs={{0,4},{1,13},{4,8},{5,1},{8,12},{9,5},{12,0},{13,9},{2,6},{3,15},{... | collective-permute-start | bytes 1179656 | tf_op jit(solution)/shard_map/ppermute | solution.py:330
  175.7 29.3 %collective-permute-start.15 = (bf16[3,192,768]{2,1,0:T(8,128)(2,1)}, bf16[3,192,768]{2,1,0:T(8,128)(2,1)}, u32[]{:S(2)}, u32[]{:S(2)}) collective-permute-start(bf16[3,192,768]{2,1,0:T(8,128)(2,1)} %collective-permute-done.14.late2_ref.rest_4_), channel_id=1, source_target_pairs={{0,16},{1,49},{16,32},{17,1},{32,48},{33,17},{48,0},{49,33},{2,18}... | collective-permute-start | bytes 2654216 | tf_op jit(solution)/shard_map/ppermute | solution.py:327
  180.1 4.0 %collective-permute-start.5 = (bf16[2,384,256]{2,1,0:T(8,128)(2,1)}, bf16[2,384,256]{2,1,0:T(8,128)(2,1)}, u32[]{:S(2)}, u32[]{:S(2)}) collective-permute-start(bf16[2,384,256]{2,1,0:T(8,128)(2,1)} %collective-permute-done.3.rest_3_), channel_id=1, source_target_pairs={{0,1},{1,0},{2,3},{3,2},{4,5},{5,4},{6,7},{7,6},{8,9},{9,8},{10,11... | collective-permute-start | bytes 1179656 | tf_op jit(solution)/shard_map/ppermute | solution.py:332
  182.3 1.1 copy-start.23
  183.6 7.8 %copy-start.21 = (s32[5]{0:T(128)}, s32[5]{0:T(128)S(1)}, u32[]{:S(2)}) copy-start(s32[5]{0:T(128)S(1)} %stack.44.where_ref) | copy-start | bytes 64
  184.1 1.0 copy-start.12
  185.1 1.0 copy-start.14
  186.1 1.0 copy-start.16
  191.4 1.7 copy-start.1
  193.0 1.7 copy-start.9
  194.8 10.2 %copy-start.2 = (bf16[6144,256]{1,0:T(8,128)(2,1)S(1)}, bf16[6144,256]{1,0:T(8,128)(2,1)}, u32[]{:S(2)}) copy-start(bf16[6144,256]{1,0:T(8,128)(2,1)} %copy-done.1) | copy-start | bytes 9437188
  194.8 10.2 %copy-start.4 = (bf16[3,192,768]{2,1,0:T(8,128)(2,1)S(1)}, bf16[3,192,768]{2,1,0:T(8,128)(2,1)}, u32[]{:S(2)}) copy-start(bf16[3,192,768]{2,1,0:T(8,128)(2,1)} %copy-done.3) | copy-start | bytes 2654212
  194.8 10.2 %copy-start.5 = (bf16[768,768]{1,0:T(8,128)(2,1)S(1)}, bf16[768,768]{1,0:T(8,128)(2,1)}, u32[]{:S(2)}) copy-start(bf16[768,768]{1,0:T(8,128)(2,1)} %all-gather.3.cloned.1.call-done) | copy-start | bytes 3538948
  194.8 10.2 %copy-start.7 = (bf16[3,192,768]{2,1,0:T(8,128)(2,1)S(1)}, bf16[3,192,768]{2,1,0:T(8,128)(2,1)}, u32[]{:S(2)}) copy-start(bf16[3,192,768]{2,1,0:T(8,128)(2,1)} %copy-done.6) | copy-start | bytes 2654212
  194.8 10.2 %copy-start.20 = (bf16[256,256]{1,0:T(8,128)(2,1)S(1)}, bf16[256,256]{1,0:T(8,128)(2,1)}, u32[]{:S(2)}) copy-start(bf16[256,256]{1,0:T(8,128)(2,1)} %cot_ref.1) | copy-start | bytes 393220
  194.8 10.2 %copy-start.22 = (s32[5]{0:T(128)S(1)}, s32[5]{0:T(128)}, u32[]{:S(2)}) copy-start(s32[5]{0:T(128)} %copy-done.21) | copy-start | bytes 64
  194.8 10.2 %copy-start.24 = (f32[256]{0:T(256)S(1)}, f32[256]{0:T(256)}, u32[]{:S(2)}) copy-start(f32[256]{0:T(256)} %param.17) | copy-start | bytes 3076
  194.8 10.2 %copy-start.25 = (f32[256]{0:T(256)S(1)}, f32[256]{0:T(256)}, u32[]{:S(2)}) copy-start(f32[256]{0:T(256)} %param.18) | copy-start | bytes 3076
  205.0 1.1 copy-start.8
  206.2 1.9 copy-start.10
  226.6 0.9 copy-start.18
  227.5 4.3 %copy-start.17 = (bf16[1552,256]{1,0:T(8,128)(2,1)}, bf16[1552,256]{1,0:T(8,128)(2,1)S(1)}, u32[]{:S(2)}) copy-start(bf16[1552,256]{1,0:T(8,128)(2,1)S(1)} %get-tuple-element.16) | copy-start | bytes 2383876
  227.5 4.4 %collective-permute-start.17 = (bf16[1552,256]{1,0:T(8,128)(2,1)S(1)}, bf16[1552,256]{1,0:T(8,128)(2,1)S(1)}, u32[]{:S(2)}, u32[]{:S(2)}) collective-permute-start(bf16[1552,256]{1,0:T(8,128)(2,1)S(1)} %get-tuple-element.17), channel_id=1, source_target_pairs={{0,1},{1,0},{2,3},{3,2},{4,5},{5,4},{6,7},{7,6},{8,9},{9,8},{10,11... | collective-permute-start | bytes 2383880 | tf_op jit(solution)/shard_map/ppermute | solution.py:393
  229.5 11.7 %collective-permute-start.16 = (bf16[1536,256]{1,0:T(8,128)(2,1)}, bf16[1536,256]{1,0:T(8,128)(2,1)S(1)}, u32[]{:S(2)}, u32[]{:S(2)}) collective-permute-start(bf16[1536,256]{1,0:T(8,128)(2,1)} %get-tuple-element.15), channel_id=1, source_target_pairs={{0,1},{1,0},{2,3},{3,2},{4,5},{5,4},{6,7},{7,6},{8,9},{9,8},{10,11... | collective-permute-start | bytes 2359304 | tf_op jit(solution)/shard_map/ppermute | solution.py:398
  233.4 7.7 %copy-start.19 = (bf16[1536,256]{1,0:T(8,128)(2,1)S(1)}, bf16[1536,256]{1,0:T(8,128)(2,1)}, u32[]{:S(2)}) copy-start(bf16[1536,256]{1,0:T(8,128)(2,1)} %copy-done.18) | copy-start | bytes 2359300
  234.4 17.8 %all-to-all-start.2 = ((bf16[4,400,256]{2,1,0:T(8,128)(2,1)}), bf16[4,400,256]{2,1,0:T(8,128)(2,1)S(1)}, u32[]{:S(2)}, u32[]{:S(2)}) async-start(bf16[4,400,256]{2,1,0:T(8,128)(2,1)} %pad_maximum_fusion.3), calls=%async_computation.2 | async-start | bytes 1638400 | tf_op jit(solution)/shard_map/all_to_all | solution.py:397
  252.2 15.5 %all-to-all-start.1 = ((bf16[4,384,256]{2,1,0:T(8,128)(2,1)}), bf16[4,384,256]{2,1,0:T(8,128)(2,1)S(1)}, u32[]{:S(2)}, u32[]{:S(2)}) async-start(bf16[4,384,256]{2,1,0:T(8,128)(2,1)} %bitcast.28), calls=%async_computation.1 | async-start | bytes 1572864 | tf_op jit(solution)/shard_map/all_to_all | solution.py:400
  257.1 29.3 %copy-start.28 = (bf16[128,256]{1,0:T(8,128)(2,1)S(1)}, bf16[128,256]{1,0:T(8,128)(2,1)}, u32[]{:S(2)}) copy-start(bf16[128,256]{1,0:T(8,128)(2,1)} %copy-done.27) | copy-start | bytes 196612
  257.1 29.3 %copy-start.30 = (bf16[128,256]{1,0:T(8,128)(2,1)S(1)}, bf16[128,256]{1,0:T(8,128)(2,1)}, u32[]{:S(2)}) copy-start(bf16[128,256]{1,0:T(8,128)(2,1)} %copy-done.29) | copy-start | bytes 196612
  257.5 28.8 %collective-permute-start.18 = (bf16[400,256]{1,0:T(8,128)(2,1)S(1)}, bf16[400,256]{1,0:T(8,128)(2,1)S(1)}, u32[]{:S(2)}, u32[]{:S(2)}) collective-permute-start(bf16[400,256]{1,0:T(8,128)(2,1)S(1)} %concatenate.43), channel_id=1, source_target_pairs={{0,2},{2,0},{1,3},{3,1},{4,6},{6,4},{5,7},{7,5},{8,10},{10,8},{9,1... | collective-permute-start | bytes 614408 | tf_op jit(solution)/shard_map/ppermute | solution.py:403
Sparse Core Ops, SparseCore 0:
  32.3 29.9 all-gather.2
  96.9 64.4 all-gather.4

commit v4 on v3

--- a/solution.py
+++ b/solution.py
@@ -22,8 +22,7 @@
 FOLD = [0, 2, 4, 6, 7, 5, 3, 1]
 Z_RING = [(FOLD[i], FOLD[(i + 1) % NZ]) for i in range(NZ)]
 Z_BACK = [(b, a) for a, b in Z_RING]
-EARLY = (0, 1, -1, 2, -2)
-FIRST = 1
+EARLY = ((0,), (1, -1), (2, -2))
 LATE = (3, -3, 4)
 TAIL = 16
 
@@ -101,7 +100,7 @@
     c, zl, x = where_ref[2], where_ref[3], where_ref[4]
     position = jnp.where(lax.rem(zl, 2) == 0, zl // 2, 7 - zl // 2)
     found = []
-    for steps in (EARLY[:FIRST], EARLY[FIRST:], LATE):
+    for steps in EARLY + (LATE,):
         for off in range(NX):
             x_from = ring_source(x, c, off, NX) if steps is LATE else off
             for step in steps:
@@ -129,11 +128,11 @@
     return copies
 
 
-def first_kernel(where_ref, normed_ref, early0_ref, early1_ref, late0_ref, late1_ref, late2_ref,
-                 acc_ref, weight_ref, sems):
+def first_kernel(where_ref, normed_ref, *rest):
+    early_refs, late_refs = rest[:len(EARLY)], rest[len(EARLY):len(EARLY) + NX - 1]
+    acc_ref, weight_ref, sems = rest[len(EARLY) + NX - 1:]
     blocks = weight_blocks(where_ref)
-    copies = load_weights(
-        (early0_ref, early1_ref), (late0_ref, late1_ref, late2_ref), weight_ref, sems)
+    copies = load_weights(early_refs, late_refs, weight_ref, sems)
     for copy in copies.values():
         copy.start()
     for slot in range(weight_ref.shape[0]):
@@ -148,7 +147,10 @@
 
 def main_kernel(where_ref, gain_ref, stat_ref, seg_row_ref, seg_col_ref, qgain_ref, kgain_ref,
                 cot_ref, part_ref, normed_ref, packed_hbm, *rest):
-    early_refs, late_refs, rest = rest[:2], rest[2:2 + NX], rest[2 + NX:]
+    n_early = len(EARLY)
+    early_refs, late_refs = rest[:n_early], rest[n_early:n_early + NX]
+    rest = rest[n_early + NX:]
+    n_copies = (n_early + 1) * NX
     attn_ref, keep_a, keep_b, give_a, give_b = rest[:5]
     weight_ref, rows_ref, packed_ref, acc_ref, grad_ref, sems = rest[5:]
     zh, c = where_ref[1], where_ref[2]
@@ -160,10 +162,10 @@
     last_copy.start()
     row_copies = [
         pltpu.make_async_copy(
-            normed_ref.at[block_rows(blocks[final + j]), :], rows_ref.at[j], sems.at[3 * NX + j])
+            normed_ref.at[block_rows(blocks[final + j]), :], rows_ref.at[j], sems.at[n_copies + j])
         for j in range(len(LATE))
     ]
-    packed_copy = pltpu.make_async_copy(packed_hbm, packed_ref, sems.at[3 * NX + len(LATE)])
+    packed_copy = pltpu.make_async_copy(packed_hbm, packed_ref, sems.at[n_copies + len(LATE)])
     for copy in row_copies + list(arrived.values()) + [packed_copy]:
         copy.start()
 
@@ -317,17 +319,16 @@
         if step < 4:
             z[-step] = lax.ppermute(z[1 - step], "zl", Z_BACK)
     early = []
-    for steps in (EARLY[:FIRST], EARLY[FIRST:]):
+    for steps in EARLY:
         joined = lax.all_gather(
-            jnp.concatenate([after(z[n], partner) if n == -1 else z[n] for n in steps]),
+            jnp.concatenate([after(z[n], partner) if n == -2 else z[n] for n in steps]),
             "x", axis=0, tiled=True)
         early.append(joined.reshape((NX, len(steps)) + weight.shape))
-    late = [jnp.stack([z[n] for n in LATE])]
+    for _ in range(NY - 2):
+        g.append(y_ring(g[-1]))
+    late = [jnp.stack([after(z[n], g[3]) if n < 0 else z[n] for n in LATE])]
     for _ in range(NX - 1):
         late.append(x_ring(late[-1]))
-
-    for _ in range(NY - 2):
-        g.append(y_ring(g[-1]))
     most = lax.ppermute(jnp.concatenate(g[:3]), "c", shift(NC, 1))
     last = lax.ppermute(g[3], "c", shift(NC, 1))
 
@@ -349,15 +350,15 @@
 
     width = w_query.shape[1]
     hbm = pl.BlockSpec(memory_space=pl.ANY)
-    n_first = NX * len(EARLY) + (NX - 1) * len(LATE)
+    n_first = NZ * NX - len(LATE)
     part = pl.pallas_call(
         first_kernel,
         out_shape=jax.ShapeDtypeStruct((LEN, 3 * width), F32),
-        in_specs=[smem, vmem] + [hbm] * (NX + 1),
+        in_specs=[smem, vmem] + [hbm] * (len(EARLY) + NX - 1),
         out_specs=vmem,
         scratch_shapes=[
             pltpu.VMEM((n_first,) + weight.shape, BF),
-            pltpu.SemaphoreType.DMA((3 * NX - 1,)),
+            pltpu.SemaphoreType.DMA(((len(EARLY) + 1) * NX - 1,)),
         ],
         compiler_params=pltpu.CompilerParams(vmem_limit_bytes=54 << 20),
         cost_estimate=pl.CostEstimate(
@@ -370,7 +371,7 @@
     context, keep_a, keep_b, give_a, give_b = pl.pallas_call(
         main_kernel,
         out_shape=(jax.ShapeDtypeStruct((LEN, width), BF), half, half_tail, half, half_tail),
-        in_specs=[smem] + [vmem] * 8 + [hbm] * (4 + NX),
+        in_specs=[smem] + [vmem] * 8 + [hbm] * (2 + len(EARLY) + NX),
         out_specs=(vmem,) * 5,
         scratch_shapes=[
             pltpu.VMEM((NZ * NX,) + weight.shape, BF),
@@ -378,7 +379,7 @@
             pltpu.VMEM((D, LEN), BF),
             pltpu.VMEM((LEN, 3 * width), F32),
             pltpu.VMEM((LEN, 3 * width), BF),
-            pltpu.SemaphoreType.DMA((3 * NX + len(LATE) + 1,)),
+            pltpu.SemaphoreType.DMA(((len(EARLY) + 1) * NX + len(LATE) + 1,)),
         ],
         compiler_params=pltpu.CompilerParams(vmem_limit_bytes=36 << 20),
         cost_estimate=pl.CostEstimate(

time: 296 us -> 289 us (0.976)
  the two profiles are of different devices: /device:TPU:14 before, /device:TPU:47 now
where the time goes in v4:
time: 289 us; the launch traced here: 287 us
  waiting for transfers between devices  106 us (37%)
  starting transfers between devices  97.7 us (34%)
  Pallas kernels  33.7 us (12%)
  local copies, waits for them, and re-layouts  21.7 us (8%)
  between operations  17.2 us (6%)
  other arithmetic  8.84 us (3%)
    all_to_all x1, waiting for transfers between devices, per_device(): lax.all_to_all(packets, ('zl', 'x'), split_axis=0, concat_axis=0, tiled=T...  25.1 us
    pallas_call x1, Pallas kernels, per_device(): pl.pallas_call(main_kernel, out_shape=(jax.ShapeDtypeStruct((LEN, width),...  19 us
    ppermute x3, waiting for transfers between devices, per_device(): late.append(x_ring(late[-1]))  18.8 us
    ppermute x1, waiting for transfers between devices, per_device(): lax.ppermute(jnp.concatenate([leave, split_sums(*sums)], axis=0), 'zh', s...  18.5 us
    ppermute x1, waiting for transfers between devices, per_device(): partner = lax.ppermute(mine, 'zh', shift(NH, 1))  17.6 us
    unnamed x67, local copies, waits for them, and re-layouts  15.3 us
    all_to_all x1, starting transfers between devices, per_device(): lax.all_to_all(packets, ('zl', 'x'), split_axis=0, concat_axis=0, tiled=T...  13.1 us
    all_to_all x1, starting transfers between devices, per_device(): y_swap(jnp.concatenate([both.reshape(NY, SHARD, LEN), tail], axis=1))  11.6 us
  transfers between devices with their start and end apart: 25, of which 11 were waited for; matrix products, arithmetic and copies ran while one was open for 5% of the time, Pallas kernels for 5%

profile of v4, /device:TPU:47, one launch (start us, length us, event | category | flops | bytes accessed | tf_op | source)
XLA Modules:
  0.0 287.1 jit_solution(18131566555372521061)
XLA Ops:
  7.2 0.9 constant_dynamic-update-slice_fusion.2
  8.2 0.9 constant_dynamic-update-slice_fusion.1
  9.1 0.9 constant_dynamic-update-slice_fusion
  10.0 0.7 copy-done.26
  10.7 1.9 collective-permute-start.6
  12.6 4.9 %collective-permute-start.7 = (bf16[192,768]{1,0:T(8,128)(2,1)}, bf16[192,768]{1,0:T(8,128)(2,1)S(1)}, u32[]{:S(2)}, u32[]{:S(2)}) collective-permute-start(bf16[192,768]{1,0:T(8,128)(2,1)} %copy-done.26), channel_id=1, source_target_pairs={{128,0},{256,128},{384,256},{448,384},{320,448},{192,320},{64,192}... | collective-permute-start | bytes 884744 | tf_op jit(solution)/shard_map/ppermute | solution.py:320
  17.5 0.7 and_select_fusion.1
  19.1 0.8 fusion.2
  19.9 13.1 %all-to-all-start = ((bf16[32,56,128]{2,1,0:T(8,128)(2,1)}), bf16[32,56,128]{2,1,0:T(8,128)(2,1)S(1)}, u32[]{:S(2)}, u32[]{:S(2)}) async-start(bf16[32,56,128]{2,1,0:T(8,128)(2,1)} %fusion.2), calls=%async_computation | async-start | bytes 917504 | tf_op jit(solution)/shard_map/all_to_all | solution.py:307
  33.1 0.9 pad_maximum_fusion.3
  34.0 4.0 %collective-permute-start.9 = (bf16[192,768]{1,0:T(8,128)(2,1)S(1)}, bf16[192,768]{1,0:T(8,128)(2,1)S(1)}, u32[]{:S(2)}, u32[]{:S(2)}) collective-permute-start(bf16[192,768]{1,0:T(8,128)(2,1)S(1)} %collective-permute-done.7), channel_id=1, source_target_pairs={{128,0},{256,128},{384,256},{448,384},{320,448},{192,320},{64,192}... | collective-permute-start | bytes 884744 | tf_op jit(solution)/shard_map/ppermute | solution.py:320
  38.0 25.1 %all-to-all-done = bf16[32,56,128]{2,1,0:T(8,128)(2,1)S(1)} async-done(((bf16[32,56,128]{2,1,0:T(8,128)(2,1)}), bf16[32,56,128]{2,1,0:T(8,128)(2,1)S(1)}, u32[]{:S(2)}, u32[]{:S(2)}) %all-to-all-start) | async-done | bytes 458784 | tf_op jit(solution)/shard_map/all_to_all | solution.py:307
  64.8 8.7 %collective-permute-start = (bf16[384,256]{1,0:T(8,128)(2,1)S(1)}, bf16[384,256]{1,0:T(8,128)(2,1)S(1)}, u32[]{:S(2)}, u32[]{:S(2)}) collective-permute-start(bf16[384,256]{1,0:T(8,128)(2,1)S(1)} %get-tuple-element.37), channel_id=1, source_target_pairs={{0,2},{2,0},{1,3},{3,1},{4,6},{6,4},{5,7},{7,5},{8,10},{10,8},{9,1... | collective-permute-start | bytes 589832 | tf_op jit(solution)/shard_map/ppermute | solution.py:309
  73.5 0.5 slice.188
  74.7 2.1 collective-permute-start.8
  76.8 17.6 %collective-permute-done = bf16[384,256]{1,0:T(8,128)(2,1)S(1)} collective-permute-done((bf16[384,256]{1,0:T(8,128)(2,1)S(1)}, bf16[384,256]{1,0:T(8,128)(2,1)S(1)}, u32[]{:S(2)}, u32[]{:S(2)}) %collective-permute-start) | collective-permute-done | bytes 196640 | tf_op jit(solution)/shard_map/ppermute | solution.py:309
  94.5 2.1 collective-permute-start.1
  96.6 0.5 slice.189
  97.8 0.9 pad_maximum_fusion.4
  98.7 4.6 %collective-permute-done.1.rest_1_ = bf16[2,384,256]{2,1,0:T(8,128)(2,1)S(1)} collective-permute-done((bf16[2,384,256]{2,1,0:T(8,128)(2,1)S(1)}, bf16[2,384,256]{2,1,0:T(8,128)(2,1)S(1)}, u32[]{:S(2)}, u32[]{:S(2)}) %collective-permute-start.1) | collective-permute-done | bytes 393248 | tf_op jit(solution)/shard_map/ppermute | solution.py:311
  103.3 2.6 collective-permute-start.2
  106.0 1.9 collective-permute-start.10
  107.9 4.2 %collective-permute-done.2.rest_2_ = bf16[2,384,256]{2,1,0:T(8,128)(2,1)S(1)} collective-permute-done((bf16[2,384,256]{2,1,0:T(8,128)(2,1)S(1)}, bf16[2,384,256]{2,1,0:T(8,128)(2,1)S(1)}, u32[]{:S(2)}, u32[]{:S(2)}) %collective-permute-start.2) | collective-permute-done | bytes 393248 | tf_op jit(solution)/shard_map/ppermute | solution.py:328
  112.1 3.5 %collective-permute-start.3 = (bf16[2,384,256]{2,1,0:T(8,128)(2,1)S(1)}, bf16[2,384,256]{2,1,0:T(8,128)(2,1)}, u32[]{:S(2)}, u32[]{:S(2)}) collective-permute-start(bf16[2,384,256]{2,1,0:T(8,128)(2,1)S(1)} %collective-permute-done.2.rest_2_), channel_id=1, source_target_pairs={{0,4},{1,13},{4,8},{5,1},{8,12},{9,5},{12,0},{13,9},{2,6},{3,15},{... | collective-permute-start | bytes 1179656 | tf_op jit(solution)/shard_map/ppermute | solution.py:328
  115.7 1.9 collective-permute-start.11
  117.6 0.5 slice.191
  118.8 3.4 %collective-permute-start.12 = (bf16[192,768]{1,0:T(8,128)(2,1)S(1)}, bf16[192,768]{1,0:T(8,128)(2,1)S(1)}, u32[]{:S(2)}, u32[]{:S(2)}) collective-permute-start(bf16[192,768]{1,0:T(8,128)(2,1)S(1)} %broadcast_add_fusion), channel_id=1, source_target_pairs={{0,128},{128,256},{256,384},{384,448},{448,320},{320,192},{192,64}... | collective-permute-start | bytes 884744 | tf_op jit(solution)/shard_map/ppermute | solution.py:318
  122.2 1.2 slice.190
  124.1 4.0 %collective-permute-done.12 = bf16[192,768]{1,0:T(8,128)(2,1)S(1)} collective-permute-done((bf16[192,768]{1,0:T(8,128)(2,1)S(1)}, bf16[192,768]{1,0:T(8,128)(2,1)S(1)}, u32[]{:S(2)}, u32[]{:S(2)}) %collective-permute-start.12) | collective-permute-done | bytes 294944 | tf_op jit(solution)/shard_map/ppermute | solution.py:318
  128.2 0.9 copy-done.4
  129.2 2.0 collective-permute-start.13
  131.2 14.0 %collective-permute-done.13.rest_4_ = bf16[3,192,768]{2,1,0:T(8,128)(2,1)S(1)} collective-permute-done((bf16[3,192,768]{2,1,0:T(8,128)(2,1)S(1)}, bf16[3,192,768]{2,1,0:T(8,128)(2,1)S(1)}, u32[]{:S(2)}, u32[]{:S(2)}) %collective-permute-start.13) | collective-permute-done | bytes 884768 | tf_op jit(solution)/shard_map/ppermute | solution.py:331
  145.2 3.4 %collective-permute-start.14 = (bf16[3,192,768]{2,1,0:T(8,128)(2,1)S(1)}, bf16[3,192,768]{2,1,0:T(8,128)(2,1)}, u32[]{:S(2)}, u32[]{:S(2)}) collective-permute-start(bf16[3,192,768]{2,1,0:T(8,128)(2,1)S(1)} %collective-permute-done.13.rest_4_), channel_id=1, source_target_pairs={{0,16},{1,49},{16,32},{17,1},{32,48},{33,17},{48,0},{49,33},{2,18}... | collective-permute-start | bytes 2654216 | tf_op jit(solution)/shard_map/ppermute | solution.py:331
  148.7 1.2 pad_maximum_fusion
  149.8 5.8 %collective-permute-start.4 = (bf16[6,384,256]{2,1,0:T(8,128)(2,1)}, bf16[6,384,256]{2,1,0:T(8,128)(2,1)}, u32[]{:S(2)}, u32[]{:S(2)}) collective-permute-start(bf16[6,384,256]{2,1,0:T(8,128)(2,1)} %pad_maximum_fusion), channel_id=1, source_target_pairs={{0,1},{1,0},{2,3},{3,2},{4,5},{5,4},{6,7},{7,6},{8,9},{9,8},{10,11... | collective-permute-start | bytes 3538952 | tf_op jit(solution)/shard_map/ppermute | solution.py:332
  155.6 4.7 %collective-permute-done.14.rest_5_ = bf16[3,192,768]{2,1,0:T(8,128)(2,1)} collective-permute-done((bf16[3,192,768]{2,1,0:T(8,128)(2,1)S(1)}, bf16[3,192,768]{2,1,0:T(8,128)(2,1)}, u32[]{:S(2)}, u32[]{:S(2)}) %collective-permute-start.14) | collective-permute-done | bytes 884768 | tf_op jit(solution)/shard_map/ppermute | solution.py:331
  160.3 2.5 collective-permute-start.15
  162.8 8.0 %collective-permute-start.5 = (bf16[2,384,256]{2,1,0:T(8,128)(2,1)}, bf16[2,384,256]{2,1,0:T(8,128)(2,1)}, u32[]{:S(2)}, u32[]{:S(2)}) collective-permute-start(bf16[2,384,256]{2,1,0:T(8,128)(2,1)} %collective-permute-done.3.rest_3_), channel_id=1, source_target_pairs={{0,1},{1,0},{2,3},{3,2},{4,5},{5,4},{6,7},{7,6},{8,9},{9,8},{10,11... | collective-permute-start | bytes 1179656 | tf_op jit(solution)/shard_map/ppermute | solution.py:333
  170.9 1.1 copy.25.gain_ref
  172.3 1.0 copy-done.12
  173.3 1.0 copy-done.14
  174.3 1.0 copy-done.16
  175.3 4.3 %norm.1 = (bf16[6144,256]{1,0:T(8,128)(2,1)S(1)}, bf16[6144,256]{1,0:T(8,128)(2,1)S(1)}, f32[2,256]{1,0:T(2,128)S(1)}) custom-call(s32[5]{0:T(128)S(1)} %stack.44.where_ref, f32[6144,1]{1,0:T(8,128)S(1)} %copy.25.gain_ref, bf16[2,384,256]{2,1,0:T(8,128)(2,1)S(1)} %copy-done.16, bf16[2,384,256]{2,1,0:T(8,128)(2,1)S(1)} %copy-done.12, ...), custom_call_target="tpu_custom_call" | custom-call | flops 20000000 | bytes 10000000 | tf_op jit(solution)/shard_map/norm/pallas_call | solution.py:337
  179.6 1.6 copy-done.1
  181.3 1.7 copy-done.10
  183.0 10.4 %first.1.part_ref = f32[256,768]{1,0:T(8,128)} custom-call(s32[5]{0:T(128)} %copy-done.21, bf16[6144,256]{1,0:T(8,128)(2,1)} %copy-done.1, bf16[4,1,192,768]{3,2,1,0:T(8,128)(2,1)} %bitcast.51, bf16[4,2,192,768]{3,2,1,0:T(8,128)(2,1)} %bitcast.47, bf16[4,2,192,768]{3,2,1,0:T(8,128)(2,1)} %bitcast.49, bf16[3,192,768]{2,1,0:T(8,128)(2,1)} %copy-done.4, ...), custom_call_target="tpu_custom_call" | custom-call | flops 2200000000 | bytes 12000000 | tf_op jit(solution)/shard_map/first/pallas_call | solution.py:354
  193.6 1.2 copy-done.8
  194.7 1.1 copy-done.9
  195.8 0.9 copy-done.20
  196.7 19.0 %core.1 = (bf16[256,256]{1,0:T(8,128)(2,1)}, bf16[1536,256]{1,0:T(8,128)(2,1)S(1)}, bf16[1552,256]{1,0:T(8,128)(2,1)S(1)}, bf16[1536,256]{1,0:T(8,128)(2,1)}, bf16[1552,256]{1,0:T(8,128)(2,1)S(1)}) custom-call(s32[5]{0:T(128)S(1)} %copy-done.22, f32[6144,1]{1,0:T(8,128)S(1)} %copy.25.gain_ref, f32[2,256]{1,0:T(2,128)S(1)} %get-tuple-element.10.stat_ref, ...), custom_call_target="tpu_custom_call" | custom-call | flops 3000000000 | bytes 20000000 | tf_op jit(solution)/shard_map/core/pallas_call | solution.py:371
  215.7 0.9 copy-done.18
  216.6 2.3 collective-permute-start.17
  218.9 2.0 collective-permute-start.16
  221.2 1.4 add_convert_fusion
  222.6 1.0 pad_maximum_fusion.2
  223.5 11.6 %all-to-all-start.2 = ((bf16[4,400,256]{2,1,0:T(8,128)(2,1)}), bf16[4,400,256]{2,1,0:T(8,128)(2,1)S(1)}, u32[]{:S(2)}, u32[]{:S(2)}) async-start(bf16[4,400,256]{2,1,0:T(8,128)(2,1)} %pad_maximum_fusion.2), calls=%async_computation.2 | async-start | bytes 1638400 | tf_op jit(solution)/shard_map/all_to_all | solution.py:398
  235.1 0.8 dynamic_slice.3
  235.9 1.1 add_convert_fusion.1
  237.0 9.3 %all-to-all-done.2 = bf16[4,400,256]{2,1,0:T(8,128)(2,1)S(1)} async-done(((bf16[4,400,256]{2,1,0:T(8,128)(2,1)}), bf16[4,400,256]{2,1,0:T(8,128)(2,1)S(1)}, u32[]{:S(2)}, u32[]{:S(2)}) %all-to-all-start.2) | async-done | bytes 819232 | tf_op jit(solution)/shard_map/all_to_all | solution.py:398
  246.3 4.6 %all-to-all-start.1 = ((bf16[4,384,256]{2,1,0:T(8,128)(2,1)}), bf16[4,384,256]{2,1,0:T(8,128)(2,1)S(1)}, u32[]{:S(2)}, u32[]{:S(2)}) async-start(bf16[4,384,256]{2,1,0:T(8,128)(2,1)} %bitcast.30), calls=%async_computation.1 | async-start | bytes 1572864 | tf_op jit(solution)/shard_map/all_to_all | solution.py:401
  251.4 5.3 %collective-permute-start.18 = (bf16[400,256]{1,0:T(8,128)(2,1)S(1)}, bf16[400,256]{1,0:T(8,128)(2,1)S(1)}, u32[]{:S(2)}, u32[]{:S(2)}) collective-permute-start(bf16[400,256]{1,0:T(8,128)(2,1)S(1)} %concatenate.47), channel_id=1, source_target_pairs={{0,2},{2,0},{1,3},{3,1},{4,6},{6,4},{5,7},{7,5},{8,10},{10,8},{9,1... | collective-permute-start | bytes 614408 | tf_op jit(solution)/shard_map/ppermute | solution.py:404
  256.8 4.1 %all-to-all-done.1 = bf16[4,384,256]{2,1,0:T(8,128)(2,1)S(1)} async-done(((bf16[4,384,256]{2,1,0:T(8,128)(2,1)}), bf16[4,384,256]{2,1,0:T(8,128)(2,1)S(1)}, u32[]{:S(2)}, u32[]{:S(2)}) %all-to-all-start.1) | async-done | bytes 786464 | tf_op jit(solution)/shard_map/all_to_all | solution.py:401
  261.0 18.5 %collective-permute-done.18 = bf16[400,256]{1,0:T(8,128)(2,1)S(1)} collective-permute-done((bf16[400,256]{1,0:T(8,128)(2,1)S(1)}, bf16[400,256]{1,0:T(8,128)(2,1)S(1)}, u32[]{:S(2)}, u32[]{:S(2)}) %collective-permute-start.18) | collective-permute-done | bytes 204832 | tf_op jit(solution)/shard_map/ppermute | solution.py:404
  279.7 0.8 copy.28
  (117 shorter events, 4.4 us)
Async XLA Ops:
  7.2 11.5 %copy-start = (bf16[256,384]{1,0:T(8,128)(2,1)S(1)}, bf16[256,384]{1,0:T(8,128)(2,1)}, u32[]{:S(2)}) copy-start(bf16[256,384]{1,0:T(8,128)(2,1)} %param.10) | copy-start | bytes 589828
  7.2 175.8 %all-gather.4.cloned.1.call-start = ((), (), s32[]{:S(2)}) async-start(), calls=%async_computation.3 | async-start | bytes 1474560 | tf_op jit(solution)/shard_map/all_gather | solution.py:323
  10.0 0.7 copy-start.26
  10.7 22.3 %collective-permute-start.6 = (bf16[192,768]{1,0:T(8,128)(2,1)}, bf16[192,768]{1,0:T(8,128)(2,1)S(1)}, u32[]{:S(2)}, u32[]{:S(2)}) collective-permute-start(bf16[192,768]{1,0:T(8,128)(2,1)} %copy-done.26), channel_id=1, source_target_pairs={{0,128},{128,256},{256,384},{384,448},{448,320},{320,192},{192,64}... | collective-permute-start | bytes 884744 | tf_op jit(solution)/shard_map/ppermute | solution.py:318
  12.6 20.4 %collective-permute-start.7 = (bf16[192,768]{1,0:T(8,128)(2,1)}, bf16[192,768]{1,0:T(8,128)(2,1)S(1)}, u32[]{:S(2)}, u32[]{:S(2)}) collective-permute-start(bf16[192,768]{1,0:T(8,128)(2,1)} %copy-done.26), channel_id=1, source_target_pairs={{128,0},{256,128},{384,256},{448,384},{320,448},{192,320},{64,192}... | collective-permute-start | bytes 884744 | tf_op jit(solution)/shard_map/ppermute | solution.py:320
  19.9 43.1 %all-to-all-start = ((bf16[32,56,128]{2,1,0:T(8,128)(2,1)}), bf16[32,56,128]{2,1,0:T(8,128)(2,1)S(1)}, u32[]{:S(2)}, u32[]{:S(2)}) async-start(bf16[32,56,128]{2,1,0:T(8,128)(2,1)} %fusion.2), calls=%async_computation | async-start | bytes 917504 | tf_op jit(solution)/shard_map/all_to_all | solution.py:307
  33.0 150.0 %all-gather.6.cloned.1.call-start = ((), (), s32[]{:S(2)}) async-start(), calls=%async_computation.4 | async-start | bytes 2949120 | tf_op jit(solution)/shard_map/all_gather | solution.py:323
  33.9 149.0 %all-gather.8.cloned.1.call-start = ((), (), s32[]{:S(2)}) async-start(), calls=%async_computation.5 | async-start | bytes 2949120 | tf_op jit(solution)/shard_map/all_gather | solution.py:323
  34.0 63.8 %collective-permute-start.9 = (bf16[192,768]{1,0:T(8,128)(2,1)S(1)}, bf16[192,768]{1,0:T(8,128)(2,1)S(1)}, u32[]{:S(2)}, u32[]{:S(2)}) collective-permute-start(bf16[192,768]{1,0:T(8,128)(2,1)S(1)} %collective-permute-done.7), channel_id=1, source_target_pairs={{128,0},{256,128},{384,256},{448,384},{320,448},{192,320},{64,192}... | collective-permute-start | bytes 884744 | tf_op jit(solution)/shard_map/ppermute | solution.py:320
  63.9 0.6 copy-start.27
  64.2 0.6 copy-start.29
  64.8 29.6 %collective-permute-start = (bf16[384,256]{1,0:T(8,128)(2,1)S(1)}, bf16[384,256]{1,0:T(8,128)(2,1)S(1)}, u32[]{:S(2)}, u32[]{:S(2)}) collective-permute-start(bf16[384,256]{1,0:T(8,128)(2,1)S(1)} %get-tuple-element.37), channel_id=1, source_target_pairs={{0,2},{2,0},{1,3},{3,1},{4,6},{6,4},{5,7},{7,5},{8,10},{10,8},{9,1... | collective-permute-start | bytes 589832 | tf_op jit(solution)/shard_map/ppermute | solution.py:309
  74.7 23.1 %collective-permute-start.8 = (bf16[192,768]{1,0:T(8,128)(2,1)S(1)}, bf16[192,768]{1,0:T(8,128)(2,1)S(1)}, u32[]{:S(2)}, u32[]{:S(2)}) collective-permute-start(bf16[192,768]{1,0:T(8,128)(2,1)S(1)} %broadcast_add_fusion.3), channel_id=1, source_target_pairs={{0,128},{128,256},{256,384},{384,448},{448,320},{320,192},{192,64}... | collective-permute-start | bytes 884744 | tf_op jit(solution)/shard_map/ppermute | solution.py:318
  94.5 4.2 %copy-start.15 = (bf16[2,384,256]{2,1,0:T(8,128)(2,1)}, bf16[2,384,256]{2,1,0:T(8,128)(2,1)S(1)}, u32[]{:S(2)}) copy-start(bf16[2,384,256]{2,1,0:T(8,128)(2,1)S(1)} %pad_maximum_fusion.5.rest_0_) | copy-start | bytes 1179652
  94.5 8.8 %collective-permute-start.1 = (bf16[2,384,256]{2,1,0:T(8,128)(2,1)S(1)}, bf16[2,384,256]{2,1,0:T(8,128)(2,1)S(1)}, u32[]{:S(2)}, u32[]{:S(2)}) collective-permute-start(bf16[2,384,256]{2,1,0:T(8,128)(2,1)S(1)} %pad_maximum_fusion.5.rest_0_), channel_id=1, source_target_pairs={{0,4},{1,13},{4,8},{5,1},{8,12},{9,5},{12,0},{13,9},{2,6},{3,15},{... | collective-permute-start | bytes 1179656 | tf_op jit(solution)/shard_map/ppermute | solution.py:311
  103.3 45.3 %copy-start.11 = (bf16[2,384,256]{2,1,0:T(8,128)(2,1)}, bf16[2,384,256]{2,1,0:T(8,128)(2,1)S(1)}, u32[]{:S(2)}) copy-start(bf16[2,384,256]{2,1,0:T(8,128)(2,1)S(1)} %collective-permute-done.1.rest_1_) | copy-start | bytes 1179652
  103.3 8.8 %collective-permute-start.2 = (bf16[2,384,256]{2,1,0:T(8,128)(2,1)S(1)}, bf16[2,384,256]{2,1,0:T(8,128)(2,1)S(1)}, u32[]{:S(2)}, u32[]{:S(2)}) collective-permute-start(bf16[2,384,256]{2,1,0:T(8,128)(2,1)S(1)} %collective-permute-done.1.rest_1_), channel_id=1, source_target_pairs={{0,4},{1,13},{4,8},{5,1},{8,12},{9,5},{12,0},{13,9},{2,6},{3,15},{... | collective-permute-start | bytes 1179656 | tf_op jit(solution)/shard_map/ppermute | solution.py:328
  106.0 12.8 %collective-permute-start.10 = (bf16[192,768]{1,0:T(8,128)(2,1)S(1)}, bf16[192,768]{1,0:T(8,128)(2,1)S(1)}, u32[]{:S(2)}, u32[]{:S(2)}) collective-permute-start(bf16[192,768]{1,0:T(8,128)(2,1)S(1)} %broadcast_add_fusion.1), channel_id=1, source_target_pairs={{0,128},{128,256},{256,384},{384,448},{448,320},{320,192},{192,64}... | collective-permute-start | bytes 884744 | tf_op jit(solution)/shard_map/ppermute | solution.py:318
  112.1 36.5 %copy-start.13 = (bf16[2,384,256]{2,1,0:T(8,128)(2,1)}, bf16[2,384,256]{2,1,0:T(8,128)(2,1)S(1)}, u32[]{:S(2)}) copy-start(bf16[2,384,256]{2,1,0:T(8,128)(2,1)S(1)} %collective-permute-done.2.rest_2_) | copy-start | bytes 1179652
  112.1 10.1 %collective-permute-start.3 = (bf16[2,384,256]{2,1,0:T(8,128)(2,1)S(1)}, bf16[2,384,256]{2,1,0:T(8,128)(2,1)}, u32[]{:S(2)}, u32[]{:S(2)}) collective-permute-start(bf16[2,384,256]{2,1,0:T(8,128)(2,1)S(1)} %collective-permute-done.2.rest_2_), channel_id=1, source_target_pairs={{0,4},{1,13},{4,8},{5,1},{8,12},{9,5},{12,0},{13,9},{2,6},{3,15},{... | collective-permute-start | bytes 1179656 | tf_op jit(solution)/shard_map/ppermute | solution.py:328
  115.7 8.4 %collective-permute-start.11 = (bf16[192,768]{1,0:T(8,128)(2,1)S(1)}, bf16[192,768]{1,0:T(8,128)(2,1)S(1)}, u32[]{:S(2)}, u32[]{:S(2)}) collective-permute-start(bf16[192,768]{1,0:T(8,128)(2,1)S(1)} %collective-permute-done.9), channel_id=1, source_target_pairs={{128,0},{256,128},{384,256},{448,384},{320,448},{192,320},{64,192}... | collective-permute-start | bytes 884744 | tf_op jit(solution)/shard_map/ppermute | solution.py:320
  118.8 9.3 %collective-permute-start.12 = (bf16[192,768]{1,0:T(8,128)(2,1)S(1)}, bf16[192,768]{1,0:T(8,128)(2,1)S(1)}, u32[]{:S(2)}, u32[]{:S(2)}) collective-permute-start(bf16[192,768]{1,0:T(8,128)(2,1)S(1)} %broadcast_add_fusion), channel_id=1, source_target_pairs={{0,128},{128,256},{256,384},{384,448},{448,320},{320,192},{192,64}... | collective-permute-start | bytes 884744 | tf_op jit(solution)/shard_map/ppermute | solution.py:318
  128.2 1.0 copy-start.4
  129.2 41.7 %copy-start.31 = (f32[6144]{0:T(1024)S(1)}, f32[6144]{0:T(1024)}, u32[]{:S(2)}) copy-start(f32[6144]{0:T(1024)} %param.13) | copy-start | bytes 73732
  129.2 16.1 %collective-permute-start.13 = (bf16[3,192,768]{2,1,0:T(8,128)(2,1)S(1)}, bf16[3,192,768]{2,1,0:T(8,128)(2,1)S(1)}, u32[]{:S(2)}, u32[]{:S(2)}) collective-permute-start(bf16[3,192,768]{2,1,0:T(8,128)(2,1)S(1)} %pad_maximum_fusion.1.rest_3_), channel_id=1, source_target_pairs={{0,16},{1,49},{16,32},{17,1},{32,48},{33,17},{48,0},{49,33},{2,18}... | collective-permute-start | bytes 2654216 | tf_op jit(solution)/shard_map/ppermute | solution.py:331
  145.2 4.6 %copy-start.7 = (bf16[3,192,768]{2,1,0:T(8,128)(2,1)}, bf16[3,192,768]{2,1,0:T(8,128)(2,1)S(1)}, u32[]{:S(2)}) copy-start(bf16[3,192,768]{2,1,0:T(8,128)(2,1)S(1)} %collective-permute-done.13.rest_4_) | copy-start | bytes 2654212
  145.2 15.1 %collective-permute-start.14 = (bf16[3,192,768]{2,1,0:T(8,128)(2,1)S(1)}, bf16[3,192,768]{2,1,0:T(8,128)(2,1)}, u32[]{:S(2)}, u32[]{:S(2)}) collective-permute-start(bf16[3,192,768]{2,1,0:T(8,128)(2,1)S(1)} %collective-permute-done.13.rest_4_), channel_id=1, source_target_pairs={{0,16},{1,49},{16,32},{17,1},{32,48},{33,17},{48,0},{49,33},{2,18}... | collective-permute-start | bytes 2654216 | tf_op jit(solution)/shard_map/ppermute | solution.py:331
  149.8 22.5 %collective-permute-start.4 = (bf16[6,384,256]{2,1,0:T(8,128)(2,1)}, bf16[6,384,256]{2,1,0:T(8,128)(2,1)}, u32[]{:S(2)}, u32[]{:S(2)}) collective-permute-start(bf16[6,384,256]{2,1,0:T(8,128)(2,1)} %pad_maximum_fusion), channel_id=1, source_target_pairs={{0,1},{1,0},{2,3},{3,2},{4,5},{5,4},{6,7},{7,6},{8,9},{9,8},{10,11... | collective-permute-start | bytes 3538952 | tf_op jit(solution)/shard_map/ppermute | solution.py:332
  160.3 33.1 %collective-permute-start.15 = (bf16[3,192,768]{2,1,0:T(8,128)(2,1)}, bf16[3,192,768]{2,1,0:T(8,128)(2,1)}, u32[]{:S(2)}, u32[]{:S(2)}) collective-permute-start(bf16[3,192,768]{2,1,0:T(8,128)(2,1)} %collective-permute-done.14.rest_5_), channel_id=1, source_target_pairs={{0,16},{1,49},{16,32},{17,1},{32,48},{33,17},{48,0},{49,33},{2,18}... | collective-permute-start | bytes 2654216 | tf_op jit(solution)/shard_map/ppermute | solution.py:331
  162.8 9.5 %collective-permute-start.5 = (bf16[2,384,256]{2,1,0:T(8,128)(2,1)}, bf16[2,384,256]{2,1,0:T(8,128)(2,1)}, u32[]{:S(2)}, u32[]{:S(2)}) collective-permute-start(bf16[2,384,256]{2,1,0:T(8,128)(2,1)} %collective-permute-done.3.rest_3_), channel_id=1, source_target_pairs={{0,1},{1,0},{2,3},{3,2},{4,5},{5,4},{6,7},{7,6},{8,9},{9,8},{10,11... | collective-permute-start | bytes 1179656 | tf_op jit(solution)/shard_map/ppermute | solution.py:333
  170.9 1.1 copy-start.23
  172.2 7.5 %copy-start.21 = (s32[5]{0:T(128)}, s32[5]{0:T(128)S(1)}, u32[]{:S(2)}) copy-start(s32[5]{0:T(128)S(1)} %stack.44.where_ref) | copy-start | bytes 64
  172.3 1.0 copy-start.12
  173.3 1.0 copy-start.14
  174.3 1.0 copy-start.16
  179.6 1.6 copy-start.1
  181.3 1.7 copy-start.10
  182.9 10.5 %copy-start.2 = (bf16[1536,768]{1,0:T(8,128)(2,1)S(1)}, bf16[1536,768]{1,0:T(8,128)(2,1)}, u32[]{:S(2)}) copy-start(bf16[1536,768]{1,0:T(8,128)(2,1)} %all-gather.6.cloned.1.call-done) | copy-start | bytes 7077892
  183.0 10.5 %copy-start.3 = (bf16[1536,768]{1,0:T(8,128)(2,1)S(1)}, bf16[1536,768]{1,0:T(8,128)(2,1)}, u32[]{:S(2)}) copy-start(bf16[1536,768]{1,0:T(8,128)(2,1)} %all-gather.8.cloned.1.call-done) | copy-start | bytes 7077892
  183.0 10.5 %copy-start.5 = (bf16[3,192,768]{2,1,0:T(8,128)(2,1)S(1)}, bf16[3,192,768]{2,1,0:T(8,128)(2,1)}, u32[]{:S(2)}) copy-start(bf16[3,192,768]{2,1,0:T(8,128)(2,1)} %copy-done.4) | copy-start | bytes 2654212
  183.0 10.5 %copy-start.6 = (bf16[768,768]{1,0:T(8,128)(2,1)S(1)}, bf16[768,768]{1,0:T(8,128)(2,1)}, u32[]{:S(2)}) copy-start(bf16[768,768]{1,0:T(8,128)(2,1)} %all-gather.4.cloned.1.call-done) | copy-start | bytes 3538948
  183.0 10.5 %copy-start.22 = (s32[5]{0:T(128)S(1)}, s32[5]{0:T(128)}, u32[]{:S(2)}) copy-start(s32[5]{0:T(128)} %copy-done.21) | copy-start | bytes 64
  183.0 10.5 %copy-start.24 = (f32[256]{0:T(256)S(1)}, f32[256]{0:T(256)}, u32[]{:S(2)}) copy-start(f32[256]{0:T(256)} %param.17) | copy-start | bytes 3076
  183.0 10.5 %copy-start.25 = (f32[256]{0:T(256)S(1)}, f32[256]{0:T(256)}, u32[]{:S(2)}) copy-start(f32[256]{0:T(256)} %param.18) | copy-start | bytes 3076
  193.5 1.2 copy-start.8
  194.7 1.1 copy-start.9
  195.8 0.9 copy-start.20
  215.7 0.9 copy-start.18
  216.6 4.3 %copy-start.17 = (bf16[1552,256]{1,0:T(8,128)(2,1)}, bf16[1552,256]{1,0:T(8,128)(2,1)S(1)}, u32[]{:S(2)}) copy-start(bf16[1552,256]{1,0:T(8,128)(2,1)S(1)} %get-tuple-element.16) | copy-start | bytes 2383876
  216.6 4.4 %collective-permute-start.17 = (bf16[1552,256]{1,0:T(8,128)(2,1)S(1)}, bf16[1552,256]{1,0:T(8,128)(2,1)S(1)}, u32[]{:S(2)}, u32[]{:S(2)}) collective-permute-start(bf16[1552,256]{1,0:T(8,128)(2,1)S(1)} %get-tuple-element.17), channel_id=1, source_target_pairs={{0,1},{1,0},{2,3},{3,2},{4,5},{5,4},{6,7},{7,6},{8,9},{9,8},{10,11... | collective-permute-start | bytes 2383880 | tf_op jit(solution)/shard_map/ppermute | solution.py:394
  218.9 17.0 %collective-permute-start.16 = (bf16[1536,256]{1,0:T(8,128)(2,1)}, bf16[1536,256]{1,0:T(8,128)(2,1)S(1)}, u32[]{:S(2)}, u32[]{:S(2)}) collective-permute-start(bf16[1536,256]{1,0:T(8,128)(2,1)} %get-tuple-element.15), channel_id=1, source_target_pairs={{0,1},{1,0},{2,3},{3,2},{4,5},{5,4},{6,7},{7,6},{8,9},{9,8},{10,11... | collective-permute-start | bytes 2359304 | tf_op jit(solution)/shard_map/ppermute | solution.py:399
  223.5 12.4 %copy-start.19 = (bf16[1536,256]{1,0:T(8,128)(2,1)S(1)}, bf16[1536,256]{1,0:T(8,128)(2,1)}, u32[]{:S(2)}) copy-start(bf16[1536,256]{1,0:T(8,128)(2,1)} %copy-done.18) | copy-start | bytes 2359300
  223.5 22.8 %all-to-all-start.2 = ((bf16[4,400,256]{2,1,0:T(8,128)(2,1)}), bf16[4,400,256]{2,1,0:T(8,128)(2,1)S(1)}, u32[]{:S(2)}, u32[]{:S(2)}) async-start(bf16[4,400,256]{2,1,0:T(8,128)(2,1)} %pad_maximum_fusion.2), calls=%async_computation.2 | async-start | bytes 1638400 | tf_op jit(solution)/shard_map/all_to_all | solution.py:398
  246.3 14.6 %all-to-all-start.1 = ((bf16[4,384,256]{2,1,0:T(8,128)(2,1)}), bf16[4,384,256]{2,1,0:T(8,128)(2,1)S(1)}, u32[]{:S(2)}, u32[]{:S(2)}) async-start(bf16[4,384,256]{2,1,0:T(8,128)(2,1)} %bitcast.30), calls=%async_computation.1 | async-start | bytes 1572864 | tf_op jit(solution)/shard_map/all_to_all | solution.py:401
  251.0 28.5 %copy-start.28 = (bf16[128,256]{1,0:T(8,128)(2,1)S(1)}, bf16[128,256]{1,0:T(8,128)(2,1)}, u32[]{:S(2)}) copy-start(bf16[128,256]{1,0:T(8,128)(2,1)} %copy-done.27) | copy-start | bytes 196612
  251.1 28.5 %copy-start.30 = (bf16[128,256]{1,0:T(8,128)(2,1)S(1)}, bf16[128,256]{1,0:T(8,128)(2,1)}, u32[]{:S(2)}) copy-start(bf16[128,256]{1,0:T(8,128)(2,1)} %copy-done.29) | copy-start | bytes 196612
  251.4 28.1 %collective-permute-start.18 = (bf16[400,256]{1,0:T(8,128)(2,1)S(1)}, bf16[400,256]{1,0:T(8,128)(2,1)S(1)}, u32[]{:S(2)}, u32[]{:S(2)}) collective-permute-start(bf16[400,256]{1,0:T(8,128)(2,1)S(1)} %concatenate.47), channel_id=1, source_target_pairs={{0,2},{2,0},{1,3},{3,1},{4,6},{6,4},{5,7},{7,5},{8,10},{10,8},{9,1... | collective-permute-start | bytes 614408 | tf_op jit(solution)/shard_map/ppermute | solution.py:404
Sparse Core Ops, SparseCore 0:
  10.8 37.2 all-gather.3
  50.2 39.4 all-gather.5
  98.8 37.6 all-gather.7

commit v5 on v4

--- a/solution.py
+++ b/solution.py
@@ -326,11 +326,12 @@
         early.append(joined.reshape((NX, len(steps)) + weight.shape))
     for _ in range(NY - 2):
         g.append(y_ring(g[-1]))
-    late = [jnp.stack([after(z[n], g[3]) if n < 0 else z[n] for n in LATE])]
-    for _ in range(NX - 1):
-        late.append(x_ring(late[-1]))
     most = lax.ppermute(jnp.concatenate(g[:3]), "c", shift(NC, 1))
     last = lax.ppermute(g[3], "c", shift(NC, 1))
+
+    held = after(after(z[-3], most), last)
+    late = [jnp.stack([held if n == -3 else z[n] for n in LATE])]
+    late.append(x_ring(late[0]))
 
     vmem = pl.BlockSpec(memory_space=pltpu.VMEM)
     smem = pl.BlockSpec(memory_space=pltpu.SMEM)
@@ -347,6 +348,9 @@
         cost_estimate=pl.CostEstimate(flops=20_000_000, bytes_accessed=10_000_000, transcendentals=0),
         name="norm",
     )(where, gain_column, *g, most, last)
+
+    late.append(x_ring(after(late[1], normed)))
+    late.append(x_ring(late[2]))
 
     width = w_query.shape[1]
     hbm = pl.BlockSpec(memory_space=pl.ANY)

time: 289 us -> 301 us (1.042)
  the two profiles are of different devices: /device:TPU:47 before, /device:TPU:136 now
where the time goes in v5:
time: 301 us; the launch traced here: 299 us
  waiting for transfers between devices  121 us (40%)
  starting transfers between devices  91.4 us (30%)
  Pallas kernels  32.2 us (11%)
  local copies, waits for them, and re-layouts  22.8 us (8%)
  between operations  18.5 us (6%)
  other arithmetic  11.9 us (4%)
    ppermute x3, waiting for transfers between devices, per_device(): z[-step] = lax.ppermute(z[1 - step], 'zl', Z_BACK)  28.3 us
    ppermute x1, waiting for transfers between devices, per_device(): lax.ppermute(jnp.concatenate([leave, split_sums(*sums)], axis=0), 'zh', s...  18.9 us
    ppermute x4, starting transfers between devices, per_device(): z[step] = lax.ppermute(block, 'zl', Z_RING)  18.9 us
    pallas_call x1, Pallas kernels, per_device(): pl.pallas_call(main_kernel, out_shape=(jax.ShapeDtypeStruct((LEN, width),...  18.6 us
    ppermute x1, waiting for transfers between devices, per_device(): partner = lax.ppermute(mine, 'zh', shift(NH, 1))  16.3 us
    unnamed x73, local copies, waits for them, and re-layouts  15.9 us
    ppermute x1, waiting for transfers between devices, per_device(): late.append(x_ring(after(late[1], normed)))  14.3 us
    all_to_all x1, starting transfers between devices, per_device(): lax.all_to_all(packets, ('zl', 'x'), split_axis=0, concat_axis=0, tiled=T...  13.9 us
  transfers between devices with their start and end apart: 25, of which 13 were waited for; matrix products, arithmetic and copies ran while one was open for 6% of the time, Pallas kernels for 5%

profile of v5, /device:TPU:136, one launch (start us, length us, event | category | flops | bytes accessed | tf_op | source)
XLA Modules:
  0.0 299.1 jit_solution(12291779173442099541)
XLA Ops:
  7.2 0.9 constant_dynamic-update-slice_fusion.2
  8.2 0.9 constant_dynamic-update-slice_fusion.1
  9.1 0.9 constant_dynamic-update-slice_fusion
  12.3 0.8 fusion.2
  13.1 13.9 %all-to-all-start = ((bf16[32,56,128]{2,1,0:T(8,128)(2,1)}), bf16[32,56,128]{2,1,0:T(8,128)(2,1)S(1)}, u32[]{:S(2)}, u32[]{:S(2)}) async-start(bf16[32,56,128]{2,1,0:T(8,128)(2,1)} %fusion.2), calls=%async_computation | async-start | bytes 917504 | tf_op jit(solution)/shard_map/all_to_all | solution.py:307
  27.0 2.5 collective-permute-start.7
  29.5 4.3 %collective-permute-start.6 = (bf16[192,768]{1,0:T(8,128)(2,1)S(1)}, bf16[192,768]{1,0:T(8,128)(2,1)S(1)}, u32[]{:S(2)}, u32[]{:S(2)}) collective-permute-start(bf16[192,768]{1,0:T(8,128)(2,1)S(1)} %copy-done.29), channel_id=1, source_target_pairs={{0,128},{128,256},{256,384},{384,448},{448,320},{320,192},{192,64}... | collective-permute-start | bytes 884744 | tf_op jit(solution)/shard_map/ppermute | solution.py:318
  33.8 25.3 %collective-permute-done.7 = bf16[192,768]{1,0:T(8,128)(2,1)} collective-permute-done((bf16[192,768]{1,0:T(8,128)(2,1)S(1)}, bf16[192,768]{1,0:T(8,128)(2,1)}, u32[]{:S(2)}, u32[]{:S(2)}) %collective-permute-start.7) | collective-permute-done | bytes 294944 | tf_op jit(solution)/shard_map/ppermute | solution.py:320
  59.1 1.8 pad_maximum_fusion.3
  62.2 8.2 %collective-permute-start = (bf16[384,256]{1,0:T(8,128)(2,1)S(1)}, bf16[384,256]{1,0:T(8,128)(2,1)S(1)}, u32[]{:S(2)}, u32[]{:S(2)}) collective-permute-start(bf16[384,256]{1,0:T(8,128)(2,1)S(1)} %get-tuple-element.37), channel_id=1, source_target_pairs={{0,2},{2,0},{1,3},{3,1},{4,6},{6,4},{5,7},{7,5},{8,10},{10,8},{9,1... | collective-permute-start | bytes 589832 | tf_op jit(solution)/shard_map/ppermute | solution.py:309
  70.4 16.3 %collective-permute-done = bf16[384,256]{1,0:T(8,128)(2,1)S(1)} collective-permute-done((bf16[384,256]{1,0:T(8,128)(2,1)S(1)}, bf16[384,256]{1,0:T(8,128)(2,1)S(1)}, u32[]{:S(2)}, u32[]{:S(2)}) %collective-permute-start) | collective-permute-done | bytes 196640 | tf_op jit(solution)/shard_map/ppermute | solution.py:309
  86.8 3.5 %collective-permute-start.1 = (bf16[2,384,256]{2,1,0:T(8,128)(2,1)S(1)}, bf16[2,384,256]{2,1,0:T(8,128)(2,1)S(1)}, u32[]{:S(2)}, u32[]{:S(2)}) collective-permute-start(bf16[2,384,256]{2,1,0:T(8,128)(2,1)S(1)} %pad_maximum_fusion.5.rest_0_), channel_id=1, source_target_pairs={{0,4},{1,13},{4,8},{5,1},{8,12},{9,5},{12,0},{13,9},{2,6},{3,15},{... | collective-permute-start | bytes 1179656 | tf_op jit(solution)/shard_map/ppermute | solution.py:311
  90.3 6.2 %collective-permute-done.1.rest_1_ = bf16[2,384,256]{2,1,0:T(8,128)(2,1)S(1)} collective-permute-done((bf16[2,384,256]{2,1,0:T(8,128)(2,1)S(1)}, bf16[2,384,256]{2,1,0:T(8,128)(2,1)S(1)}, u32[]{:S(2)}, u32[]{:S(2)}) %collective-permute-start.1) | collective-permute-done | bytes 393248 | tf_op jit(solution)/shard_map/ppermute | solution.py:311
  96.5 3.5 %collective-permute-start.2 = (bf16[2,384,256]{2,1,0:T(8,128)(2,1)S(1)}, bf16[2,384,256]{2,1,0:T(8,128)(2,1)S(1)}, u32[]{:S(2)}, u32[]{:S(2)}) collective-permute-start(bf16[2,384,256]{2,1,0:T(8,128)(2,1)S(1)} %collective-permute-done.1.rest_1_), channel_id=1, source_target_pairs={{0,4},{1,13},{4,8},{5,1},{8,12},{9,5},{12,0},{13,9},{2,6},{3,15},{... | collective-permute-start | bytes 1179656 | tf_op jit(solution)/shard_map/ppermute | solution.py:328
  101.2 5.7 %collective-permute-start.8 = (bf16[192,768]{1,0:T(8,128)(2,1)S(1)}, bf16[192,768]{1,0:T(8,128)(2,1)S(1)}, u32[]{:S(2)}, u32[]{:S(2)}) collective-permute-start(bf16[192,768]{1,0:T(8,128)(2,1)S(1)} %broadcast_add_fusion.4), channel_id=1, source_target_pairs={{0,128},{128,256},{256,384},{384,448},{448,320},{320,192},{192,64}... | collective-permute-start | bytes 884744 | tf_op jit(solution)/shard_map/ppermute | solution.py:318
  106.9 1.2 pad_maximum_fusion
  108.1 1.9 collective-permute-start.4
  110.0 2.2 collective-permute-start.9
  113.5 4.6 %collective-permute-start.10 = (bf16[192,768]{1,0:T(8,128)(2,1)S(1)}, bf16[192,768]{1,0:T(8,128)(2,1)S(1)}, u32[]{:S(2)}, u32[]{:S(2)}) collective-permute-start(bf16[192,768]{1,0:T(8,128)(2,1)S(1)} %broadcast_add_fusion.2), channel_id=1, source_target_pairs={{0,128},{128,256},{256,384},{384,448},{448,320},{320,192},{192,64}... | collective-permute-start | bytes 884744 | tf_op jit(solution)/shard_map/ppermute | solution.py:318
  118.1 3.5 %collective-permute-start.3 = (bf16[2,384,256]{2,1,0:T(8,128)(2,1)S(1)}, bf16[2,384,256]{2,1,0:T(8,128)(2,1)S(1)}, u32[]{:S(2)}, u32[]{:S(2)}) collective-permute-start(bf16[2,384,256]{2,1,0:T(8,128)(2,1)S(1)} %collective-permute-done.2.rest_2_), channel_id=1, source_target_pairs={{0,4},{1,13},{4,8},{5,1},{8,12},{9,5},{12,0},{13,9},{2,6},{3,15},{... | collective-permute-start | bytes 1179656 | tf_op jit(solution)/shard_map/ppermute | solution.py:328
  121.6 1.3 collective-permute-done.9
  123.0 0.9 pad_maximum_fusion.4
  123.8 4.8 %collective-permute-done.3.rest_3_ = bf16[2,384,256]{2,1,0:T(8,128)(2,1)S(1)} collective-permute-done((bf16[2,384,256]{2,1,0:T(8,128)(2,1)S(1)}, bf16[2,384,256]{2,1,0:T(8,128)(2,1)S(1)}, u32[]{:S(2)}, u32[]{:S(2)}) %collective-permute-start.3) | collective-permute-done | bytes 393248 | tf_op jit(solution)/shard_map/ppermute | solution.py:328
  128.7 1.9 collective-permute-start.5
  130.6 2.5 collective-permute-start.11
  134.3 4.3 %collective-permute-start.12 = (bf16[192,768]{1,0:T(8,128)(2,1)S(1)}, bf16[192,768]{1,0:T(8,128)(2,1)S(1)}, u32[]{:S(2)}, u32[]{:S(2)}) collective-permute-start(bf16[192,768]{1,0:T(8,128)(2,1)S(1)} %broadcast_add_fusion.1), channel_id=1, source_target_pairs={{0,128},{128,256},{256,384},{384,448},{448,320},{320,192},{192,64}... | collective-permute-start | bytes 884744 | tf_op jit(solution)/shard_map/ppermute | solution.py:318
  141.1 1.7 collective-permute-done.11
  142.8 8.3 %collective-permute-done.12 = bf16[192,768]{1,0:T(8,128)(2,1)S(1)} collective-permute-done((bf16[192,768]{1,0:T(8,128)(2,1)S(1)}, bf16[192,768]{1,0:T(8,128)(2,1)S(1)}, u32[]{:S(2)}, u32[]{:S(2)}) %collective-permute-start.12) | collective-permute-done | bytes 294944 | tf_op jit(solution)/shard_map/ppermute | solution.py:318
  151.1 1.0 pad_maximum_fusion.1.rest_3_
  152.2 2.6 collective-permute-start.13
  154.8 1.1 copy.25.gain_ref
  156.0 1.0 copy-done.8
  157.0 1.0 copy-done.10
  158.0 1.0 copy-done.12
  159.0 1.3 copy-done.14
  160.3 1.0 copy-done.19
  161.3 1.0 copy-done.21
  162.3 3.3 %norm.1 = (bf16[6144,256]{1,0:T(8,128)(2,1)S(1)}, bf16[6144,256]{1,0:T(8,128)(2,1)S(1)}, f32[2,256]{1,0:T(2,128)S(1)}) custom-call(s32[5]{0:T(128)S(1)} %stack.44.where_ref, f32[6144,1]{1,0:T(8,128)S(1)} %copy.25.gain_ref, bf16[2,384,256]{2,1,0:T(8,128)(2,1)S(1)} %copy-done.12, bf16[2,384,256]{2,1,0:T(8,128)(2,1)S(1)} %copy-done.8, ...), custom_call_target="tpu_custom_call" | custom-call | flops 20000000 | bytes 10000000 | tf_op jit(solution)/shard_map/norm/pallas_call | solution.py:338
  165.6 1.7 copy-done.6
  167.3 1.6 copy-done.1
  170.1 8.7 %collective-permute-done.13.rest_4_ = bf16[3,192,768]{2,1,0:T(8,128)(2,1)} collective-permute-done((bf16[3,192,768]{2,1,0:T(8,128)(2,1)}, bf16[3,192,768]{2,1,0:T(8,128)(2,1)}, u32[]{:S(2)}, u32[]{:S(2)}) %collective-permute-start.13) | collective-permute-done | bytes 884768 | tf_op jit(solution)/shard_map/ppermute | solution.py:334
  178.8 1.2 broadcast_add_fusion
  180.0 1.9 collective-permute-start.14
  182.0 14.3 %collective-permute-done.14.rest_5_ = bf16[3,192,768]{2,1,0:T(8,128)(2,1)} collective-permute-done((bf16[3,192,768]{2,1,0:T(8,128)(2,1)S(1)}, bf16[3,192,768]{2,1,0:T(8,128)(2,1)}, u32[]{:S(2)}, u32[]{:S(2)}) %collective-permute-start.14) | collective-permute-done | bytes 884768 | tf_op jit(solution)/shard_map/ppermute | solution.py:352
  196.3 2.1 collective-permute-start.15
  198.7 10.3 %first.1.part_ref = f32[256,768]{1,0:T(8,128)} custom-call(s32[5]{0:T(128)} %copy-done.23, bf16[6144,256]{1,0:T(8,128)(2,1)} %copy-done.1, bf16[4,1,192,768]{3,2,1,0:T(8,128)(2,1)} %bitcast.53, bf16[4,2,192,768]{3,2,1,0:T(8,128)(2,1)} %bitcast.49, bf16[4,2,192,768]{3,2,1,0:T(8,128)(2,1)} %bitcast.51, bf16[3,192,768]{2,1,0:T(8,128)(2,1)} %pad_maximum_fusion.1.rest_3_, ...), custom_call_target="tpu_custom_call" | custom-call | flops 2200000000 | bytes 12000000 | tf_op jit(solution)/shard_map/first/pallas_call | solution.py:358
  209.0 3.8 %collective-permute-done.15.rest_6_ = bf16[3,192,768]{2,1,0:T(8,128)(2,1)} collective-permute-done((bf16[3,192,768]{2,1,0:T(8,128)(2,1)}, bf16[3,192,768]{2,1,0:T(8,128)(2,1)}, u32[]{:S(2)}, u32[]{:S(2)}) %collective-permute-start.15) | collective-permute-done | bytes 884768 | tf_op jit(solution)/shard_map/ppermute | solution.py:353
  212.8 1.1 copy-done.5
  213.9 0.9 copy-done.22
  214.8 18.6 %core.1 = (bf16[256,256]{1,0:T(8,128)(2,1)}, bf16[1536,256]{1,0:T(8,128)(2,1)S(1)}, bf16[1552,256]{1,0:T(8,128)(2,1)S(1)}, bf16[1536,256]{1,0:T(8,128)(2,1)}, bf16[1552,256]{1,0:T(8,128)(2,1)S(1)}) custom-call(s32[5]{0:T(128)S(1)} %copy-done.24, f32[6144,1]{1,0:T(8,128)S(1)} %copy.25.gain_ref, f32[2,256]{1,0:T(2,128)S(1)} %get-tuple-element.10.stat_ref, ...), custom_call_target="tpu_custom_call" | custom-call | flops 3000000000 | bytes 20000000 | tf_op jit(solution)/shard_map/core/pallas_call | solution.py:375
  233.4 0.9 copy-done.16
  234.3 1.9 collective-permute-start.17
  236.2 2.4 collective-permute-start.16
  238.9 1.3 add_convert_fusion
  240.2 1.0 pad_maximum_fusion.2
  241.2 5.0 %all-to-all-start.2 = ((bf16[4,400,256]{2,1,0:T(8,128)(2,1)}), bf16[4,400,256]{2,1,0:T(8,128)(2,1)S(1)}, u32[]{:S(2)}, u32[]{:S(2)}) async-start(bf16[4,400,256]{2,1,0:T(8,128)(2,1)} %pad_maximum_fusion.2), calls=%async_computation.2 | async-start | bytes 1638400 | tf_op jit(solution)/shard_map/all_to_all | solution.py:402
  246.2 0.8 dynamic_slice.3
  246.9 1.1 add_convert_fusion.1
  248.0 9.5 %all-to-all-done.2 = bf16[4,400,256]{2,1,0:T(8,128)(2,1)S(1)} async-done(((bf16[4,400,256]{2,1,0:T(8,128)(2,1)}), bf16[4,400,256]{2,1,0:T(8,128)(2,1)S(1)}, u32[]{:S(2)}, u32[]{:S(2)}) %all-to-all-start.2) | async-done | bytes 819232 | tf_op jit(solution)/shard_map/all_to_all | solution.py:402
  257.5 4.9 %all-to-all-start.1 = ((bf16[4,384,256]{2,1,0:T(8,128)(2,1)}), bf16[4,384,256]{2,1,0:T(8,128)(2,1)S(1)}, u32[]{:S(2)}, u32[]{:S(2)}) async-start(bf16[4,384,256]{2,1,0:T(8,128)(2,1)} %bitcast.32), calls=%async_computation.1 | async-start | bytes 1572864 | tf_op jit(solution)/shard_map/all_to_all | solution.py:405
  262.9 8.0 %collective-permute-start.18 = (bf16[400,256]{1,0:T(8,128)(2,1)S(1)}, bf16[400,256]{1,0:T(8,128)(2,1)S(1)}, u32[]{:S(2)}, u32[]{:S(2)}) collective-permute-start(bf16[400,256]{1,0:T(8,128)(2,1)S(1)} %concatenate.47), channel_id=1, source_target_pairs={{0,2},{2,0},{1,3},{3,1},{4,6},{6,4},{5,7},{7,5},{8,10},{10,8},{9,1... | collective-permute-start | bytes 614408 | tf_op jit(solution)/shard_map/ppermute | solution.py:408
  271.0 1.6 all-to-all-done.1
  272.7 18.9 %collective-permute-done.18 = bf16[400,256]{1,0:T(8,128)(2,1)S(1)} collective-permute-done((bf16[400,256]{1,0:T(8,128)(2,1)S(1)}, bf16[400,256]{1,0:T(8,128)(2,1)S(1)}, u32[]{:S(2)}, u32[]{:S(2)}) %collective-permute-start.18) | collective-permute-done | bytes 204832 | tf_op jit(solution)/shard_map/ppermute | solution.py:408
  291.8 0.8 copy.28
  (126 shorter events, 8.3 us)
Async XLA Ops:
  7.2 4.5 %copy-start = (bf16[256,384]{1,0:T(8,128)(2,1)S(1)}, bf16[256,384]{1,0:T(8,128)(2,1)}, u32[]{:S(2)}) copy-start(bf16[256,384]{1,0:T(8,128)(2,1)} %param.10) | copy-start | bytes 589828
  7.2 191.4 %all-gather.4.cloned.1.call-start = ((), (), s32[]{:S(2)}) async-start(), calls=%async_computation.3 | async-start | bytes 1474560 | tf_op jit(solution)/shard_map/all_gather | solution.py:323
  10.0 0.7 copy-start.28
  12.2 14.9 %copy-start.29 = (bf16[192,768]{1,0:T(8,128)(2,1)S(1)}, bf16[192,768]{1,0:T(8,128)(2,1)}, u32[]{:S(2)}) copy-start(bf16[192,768]{1,0:T(8,128)(2,1)} %copy-done.28) | copy-start | bytes 884740
  13.1 47.9 %all-to-all-start = ((bf16[32,56,128]{2,1,0:T(8,128)(2,1)}), bf16[32,56,128]{2,1,0:T(8,128)(2,1)S(1)}, u32[]{:S(2)}, u32[]{:S(2)}) async-start(bf16[32,56,128]{2,1,0:T(8,128)(2,1)} %fusion.2), calls=%async_computation | async-start | bytes 917504 | tf_op jit(solution)/shard_map/all_to_all | solution.py:307
  27.0 171.6 %all-gather.6.cloned.1.call-start = ((), (), s32[]{:S(2)}) async-start(), calls=%async_computation.4 | async-start | bytes 2949120 | tf_op jit(solution)/shard_map/all_gather | solution.py:323
  27.0 32.0 %collective-permute-start.7 = (bf16[192,768]{1,0:T(8,128)(2,1)S(1)}, bf16[192,768]{1,0:T(8,128)(2,1)}, u32[]{:S(2)}, u32[]{:S(2)}) collective-permute-start(bf16[192,768]{1,0:T(8,128)(2,1)S(1)} %copy-done.29), channel_id=1, source_target_pairs={{128,0},{256,128},{384,256},{448,384},{320,448},{192,320},{64,192}... | collective-permute-start | bytes 884744 | tf_op jit(solution)/shard_map/ppermute | solution.py:320
  29.5 29.6 %collective-permute-start.6 = (bf16[192,768]{1,0:T(8,128)(2,1)S(1)}, bf16[192,768]{1,0:T(8,128)(2,1)S(1)}, u32[]{:S(2)}, u32[]{:S(2)}) collective-permute-start(bf16[192,768]{1,0:T(8,128)(2,1)S(1)} %copy-done.29), channel_id=1, source_target_pairs={{0,128},{128,256},{256,384},{384,448},{448,320},{320,192},{192,64}... | collective-permute-start | bytes 884744 | tf_op jit(solution)/shard_map/ppermute | solution.py:318
  60.9 137.7 %all-gather.8.cloned.1.call-start = ((), (), s32[]{:S(2)}) async-start(), calls=%async_computation.5 | async-start | bytes 2949120 | tf_op jit(solution)/shard_map/all_gather | solution.py:323
  61.8 45.1 %copy-start.30 = (bf16[128,256]{1,0:T(8,128)(2,1)}, bf16[128,256]{1,0:T(8,128)(2,1)S(1)}, u32[]{:S(2)}) copy-start(bf16[128,256]{1,0:T(8,128)(2,1)S(1)} %convolution_convert_fusion.2) | copy-start | bytes 196612
  62.1 44.8 %copy-start.32 = (bf16[128,256]{1,0:T(8,128)(2,1)}, bf16[128,256]{1,0:T(8,128)(2,1)S(1)}, u32[]{:S(2)}) copy-start(bf16[128,256]{1,0:T(8,128)(2,1)S(1)} %convolution_convert_fusion.1) | copy-start | bytes 196612
  62.2 24.6 %collective-permute-start = (bf16[384,256]{1,0:T(8,128)(2,1)S(1)}, bf16[384,256]{1,0:T(8,128)(2,1)S(1)}, u32[]{:S(2)}, u32[]{:S(2)}) collective-permute-start(bf16[384,256]{1,0:T(8,128)(2,1)S(1)} %get-tuple-element.37), channel_id=1, source_target_pairs={{0,2},{2,0},{1,3},{3,1},{4,6},{6,4},{5,7},{7,5},{8,10},{10,8},{9,1... | collective-permute-start | bytes 589832 | tf_op jit(solution)/shard_map/ppermute | solution.py:309
  86.8 14.4 %copy-start.11 = (bf16[2,384,256]{2,1,0:T(8,128)(2,1)}, bf16[2,384,256]{2,1,0:T(8,128)(2,1)S(1)}, u32[]{:S(2)}) copy-start(bf16[2,384,256]{2,1,0:T(8,128)(2,1)S(1)} %pad_maximum_fusion.5.rest_0_) | copy-start | bytes 1179652
  86.8 9.7 %collective-permute-start.1 = (bf16[2,384,256]{2,1,0:T(8,128)(2,1)S(1)}, bf16[2,384,256]{2,1,0:T(8,128)(2,1)S(1)}, u32[]{:S(2)}, u32[]{:S(2)}) collective-permute-start(bf16[2,384,256]{2,1,0:T(8,128)(2,1)S(1)} %pad_maximum_fusion.5.rest_0_), channel_id=1, source_target_pairs={{0,4},{1,13},{4,8},{5,1},{8,12},{9,5},{12,0},{13,9},{2,6},{3,15},{... | collective-permute-start | bytes 1179656 | tf_op jit(solution)/shard_map/ppermute | solution.py:311
  96.5 36.6 %copy-start.7 = (bf16[2,384,256]{2,1,0:T(8,128)(2,1)}, bf16[2,384,256]{2,1,0:T(8,128)(2,1)S(1)}, u32[]{:S(2)}) copy-start(bf16[2,384,256]{2,1,0:T(8,128)(2,1)S(1)} %collective-permute-done.1.rest_1_) | copy-start | bytes 1179652
  96.5 10.4 %collective-permute-start.2 = (bf16[2,384,256]{2,1,0:T(8,128)(2,1)S(1)}, bf16[2,384,256]{2,1,0:T(8,128)(2,1)S(1)}, u32[]{:S(2)}, u32[]{:S(2)}) collective-permute-start(bf16[2,384,256]{2,1,0:T(8,128)(2,1)S(1)} %collective-permute-done.1.rest_1_), channel_id=1, source_target_pairs={{0,4},{1,13},{4,8},{5,1},{8,12},{9,5},{12,0},{13,9},{2,6},{3,15},{... | collective-permute-start | bytes 1179656 | tf_op jit(solution)/shard_map/ppermute | solution.py:328
  101.2 12.3 %collective-permute-start.8 = (bf16[192,768]{1,0:T(8,128)(2,1)S(1)}, bf16[192,768]{1,0:T(8,128)(2,1)S(1)}, u32[]{:S(2)}, u32[]{:S(2)}) collective-permute-start(bf16[192,768]{1,0:T(8,128)(2,1)S(1)} %broadcast_add_fusion.4), channel_id=1, source_target_pairs={{0,128},{128,256},{256,384},{384,448},{448,320},{320,192},{192,64}... | collective-permute-start | bytes 884744 | tf_op jit(solution)/shard_map/ppermute | solution.py:318
  106.9 11.2 %copy-start.9 = (bf16[2,384,256]{2,1,0:T(8,128)(2,1)}, bf16[2,384,256]{2,1,0:T(8,128)(2,1)S(1)}, u32[]{:S(2)}) copy-start(bf16[2,384,256]{2,1,0:T(8,128)(2,1)S(1)} %collective-permute-done.2.rest_2_) | copy-start | bytes 1179652
  108.1 31.7 %collective-permute-start.4 = (bf16[6,384,256]{2,1,0:T(8,128)(2,1)}, bf16[6,384,256]{2,1,0:T(8,128)(2,1)S(1)}, u32[]{:S(2)}, u32[]{:S(2)}) collective-permute-start(bf16[6,384,256]{2,1,0:T(8,128)(2,1)} %pad_maximum_fusion), channel_id=1, source_target_pairs={{0,1},{1,0},{2,3},{3,2},{4,5},{5,4},{6,7},{7,6},{8,9},{9,8},{10,11... | collective-permute-start | bytes 3538952 | tf_op jit(solution)/shard_map/ppermute | solution.py:329
  110.0 12.9 %collective-permute-start.9 = (bf16[192,768]{1,0:T(8,128)(2,1)}, bf16[192,768]{1,0:T(8,128)(2,1)S(1)}, u32[]{:S(2)}, u32[]{:S(2)}) collective-permute-start(bf16[192,768]{1,0:T(8,128)(2,1)} %collective-permute-done.7), channel_id=1, source_target_pairs={{128,0},{256,128},{384,256},{448,384},{320,448},{192,320},{64,192}... | collective-permute-start | bytes 884744 | tf_op jit(solution)/shard_map/ppermute | solution.py:320
  113.5 20.8 %collective-permute-start.10 = (bf16[192,768]{1,0:T(8,128)(2,1)S(1)}, bf16[192,768]{1,0:T(8,128)(2,1)S(1)}, u32[]{:S(2)}, u32[]{:S(2)}) collective-permute-start(bf16[192,768]{1,0:T(8,128)(2,1)S(1)} %broadcast_add_fusion.2), channel_id=1, source_target_pairs={{0,128},{128,256},{256,384},{384,448},{448,320},{320,192},{192,64}... | collective-permute-start | bytes 884744 | tf_op jit(solution)/shard_map/ppermute | solution.py:318
  118.1 10.5 %collective-permute-start.3 = (bf16[2,384,256]{2,1,0:T(8,128)(2,1)S(1)}, bf16[2,384,256]{2,1,0:T(8,128)(2,1)S(1)}, u32[]{:S(2)}, u32[]{:S(2)}) collective-permute-start(bf16[2,384,256]{2,1,0:T(8,128)(2,1)S(1)} %collective-permute-done.2.rest_2_), channel_id=1, source_target_pairs={{0,4},{1,13},{4,8},{5,1},{8,12},{9,5},{12,0},{13,9},{2,6},{3,15},{... | collective-permute-start | bytes 1179656 | tf_op jit(solution)/shard_map/ppermute | solution.py:328
  128.7 23.5 %copy-start.18 = (bf16[2,384,256]{2,1,0:T(8,128)(2,1)}, bf16[2,384,256]{2,1,0:T(8,128)(2,1)S(1)}, u32[]{:S(2)}) copy-start(bf16[2,384,256]{2,1,0:T(8,128)(2,1)S(1)} %collective-permute-done.3.rest_3_) | copy-start | bytes 1179652
  128.7 9.9 %collective-permute-start.5 = (bf16[2,384,256]{2,1,0:T(8,128)(2,1)S(1)}, bf16[2,384,256]{2,1,0:T(8,128)(2,1)S(1)}, u32[]{:S(2)}, u32[]{:S(2)}) collective-permute-start(bf16[2,384,256]{2,1,0:T(8,128)(2,1)S(1)} %collective-permute-done.3.rest_3_), channel_id=1, source_target_pairs={{0,1},{1,0},{2,3},{3,2},{4,5},{5,4},{6,7},{7,6},{8,9},{9,8},{10,11... | collective-permute-start | bytes 1179656 | tf_op jit(solution)/shard_map/ppermute | solution.py:330
  130.6 12.2 %collective-permute-start.11 = (bf16[192,768]{1,0:T(8,128)(2,1)S(1)}, bf16[192,768]{1,0:T(8,128)(2,1)S(1)}, u32[]{:S(2)}, u32[]{:S(2)}) collective-permute-start(bf16[192,768]{1,0:T(8,128)(2,1)S(1)} %collective-permute-done.9), channel_id=1, source_target_pairs={{128,0},{256,128},{384,256},{448,384},{320,448},{192,320},{64,192}... | collective-permute-start | bytes 884744 | tf_op jit(solution)/shard_map/ppermute | solution.py:320
  134.3 16.9 %collective-permute-start.12 = (bf16[192,768]{1,0:T(8,128)(2,1)S(1)}, bf16[192,768]{1,0:T(8,128)(2,1)S(1)}, u32[]{:S(2)}, u32[]{:S(2)}) collective-permute-start(bf16[192,768]{1,0:T(8,128)(2,1)S(1)} %broadcast_add_fusion.1), channel_id=1, source_target_pairs={{0,128},{128,256},{256,384},{384,448},{448,320},{320,192},{192,64}... | collective-permute-start | bytes 884744 | tf_op jit(solution)/shard_map/ppermute | solution.py:318
  138.6 13.6 %copy-start.20 = (bf16[2,384,256]{2,1,0:T(8,128)(2,1)}, bf16[2,384,256]{2,1,0:T(8,128)(2,1)S(1)}, u32[]{:S(2)}) copy-start(bf16[2,384,256]{2,1,0:T(8,128)(2,1)S(1)} %collective-permute-done.5.rest_5_) | copy-start | bytes 1179652
  139.8 12.4 %copy-start.13 = (bf16[6,384,256]{2,1,0:T(8,128)(2,1)}, bf16[6,384,256]{2,1,0:T(8,128)(2,1)S(1)}, u32[]{:S(2)}) copy-start(bf16[6,384,256]{2,1,0:T(8,128)(2,1)S(1)} %collective-permute-done.4.rest_4_) | copy-start | bytes 3538948
  142.8 12.1 %copy-start.34 = (f32[6144]{0:T(1024)S(1)}, f32[6144]{0:T(1024)}, u32[]{:S(2)}) copy-start(f32[6144]{0:T(1024)} %param.13) | copy-start | bytes 73732
  152.2 26.6 %collective-permute-start.13 = (bf16[3,192,768]{2,1,0:T(8,128)(2,1)}, bf16[3,192,768]{2,1,0:T(8,128)(2,1)}, u32[]{:S(2)}, u32[]{:S(2)}) collective-permute-start(bf16[3,192,768]{2,1,0:T(8,128)(2,1)} %pad_maximum_fusion.1.rest_3_), channel_id=1, source_target_pairs={{0,16},{1,49},{16,32},{17,1},{32,48},{33,17},{48,0},{49,33},{2,18}... | collective-permute-start | bytes 2654216 | tf_op jit(solution)/shard_map/ppermute | solution.py:334
  156.0 1.0 copy-start.8
  157.0 1.0 copy-start.10
  158.0 1.0 copy-start.12
  159.0 1.3 copy-start.14
  160.3 1.0 copy-start.19
  161.3 1.0 copy-start.21
  162.3 3.3 %copy-start.23 = (s32[5]{0:T(128)}, s32[5]{0:T(128)S(1)}, u32[]{:S(2)}) copy-start(s32[5]{0:T(128)S(1)} %stack.44.where_ref) | copy-start | bytes 64
  165.6 1.7 copy-start.6
  167.3 1.6 copy-start.1
  167.3 31.1 %copy-start.25 = (s32[256]{0:T(256)S(1)}, s32[256]{0:T(256)}, u32[]{:S(2)}) copy-start(s32[256]{0:T(256)} %param.12) | copy-start | bytes 3076
  180.0 16.3 %collective-permute-start.14 = (bf16[3,192,768]{2,1,0:T(8,128)(2,1)S(1)}, bf16[3,192,768]{2,1,0:T(8,128)(2,1)}, u32[]{:S(2)}, u32[]{:S(2)}) collective-permute-start(bf16[3,192,768]{2,1,0:T(8,128)(2,1)S(1)} %broadcast_add_fusion), channel_id=1, source_target_pairs={{0,16},{1,49},{16,32},{17,1},{32,48},{33,17},{48,0},{49,33},{2,18}... | collective-permute-start | bytes 2654216 | tf_op jit(solution)/shard_map/ppermute | solution.py:352
  196.3 16.5 %collective-permute-start.15 = (bf16[3,192,768]{2,1,0:T(8,128)(2,1)}, bf16[3,192,768]{2,1,0:T(8,128)(2,1)}, u32[]{:S(2)}, u32[]{:S(2)}) collective-permute-start(bf16[3,192,768]{2,1,0:T(8,128)(2,1)} %collective-permute-done.14.rest_5_), channel_id=1, source_target_pairs={{0,16},{1,49},{16,32},{17,1},{32,48},{33,17},{48,0},{49,33},{2,18}... | collective-permute-start | bytes 2654216 | tf_op jit(solution)/shard_map/ppermute | solution.py:353
  198.6 14.1 %copy-start.2 = (bf16[1536,768]{1,0:T(8,128)(2,1)S(1)}, bf16[1536,768]{1,0:T(8,128)(2,1)}, u32[]{:S(2)}) copy-start(bf16[1536,768]{1,0:T(8,128)(2,1)} %all-gather.6.cloned.1.call-done) | copy-start | bytes 7077892
  198.6 14.1 %copy-start.3 = (bf16[1536,768]{1,0:T(8,128)(2,1)S(1)}, bf16[1536,768]{1,0:T(8,128)(2,1)}, u32[]{:S(2)}) copy-start(bf16[1536,768]{1,0:T(8,128)(2,1)} %all-gather.8.cloned.1.call-done) | copy-start | bytes 7077892
  198.6 14.1 %copy-start.4 = (bf16[768,768]{1,0:T(8,128)(2,1)S(1)}, bf16[768,768]{1,0:T(8,128)(2,1)}, u32[]{:S(2)}) copy-start(bf16[768,768]{1,0:T(8,128)(2,1)} %all-gather.4.cloned.1.call-done) | copy-start | bytes 3538948
  198.7 14.1 %copy-start.24 = (s32[5]{0:T(128)S(1)}, s32[5]{0:T(128)}, u32[]{:S(2)}) copy-start(s32[5]{0:T(128)} %copy-done.23) | copy-start | bytes 64
  198.7 14.1 %copy-start.26 = (f32[256]{0:T(256)S(1)}, f32[256]{0:T(256)}, u32[]{:S(2)}) copy-start(f32[256]{0:T(256)} %param.17) | copy-start | bytes 3076
  198.7 14.1 %copy-start.27 = (f32[256]{0:T(256)S(1)}, f32[256]{0:T(256)}, u32[]{:S(2)}) copy-start(f32[256]{0:T(256)} %param.18) | copy-start | bytes 3076
  212.8 1.1 copy-start.5
  213.9 0.9 copy-start.22
  233.4 0.9 copy-start.16
  234.3 4.3 %copy-start.15 = (bf16[1552,256]{1,0:T(8,128)(2,1)}, bf16[1552,256]{1,0:T(8,128)(2,1)S(1)}, u32[]{:S(2)}) copy-start(bf16[1552,256]{1,0:T(8,128)(2,1)S(1)} %get-tuple-element.16) | copy-start | bytes 2383876
  234.3 4.4 %collective-permute-start.17 = (bf16[1552,256]{1,0:T(8,128)(2,1)S(1)}, bf16[1552,256]{1,0:T(8,128)(2,1)S(1)}, u32[]{:S(2)}, u32[]{:S(2)}) collective-permute-start(bf16[1552,256]{1,0:T(8,128)(2,1)S(1)} %get-tuple-element.17), channel_id=1, source_target_pairs={{0,1},{1,0},{2,3},{3,2},{4,5},{5,4},{6,7},{7,6},{8,9},{9,8},{10,11... | collective-permute-start | bytes 2383880 | tf_op jit(solution)/shard_map/ppermute | solution.py:398
  236.2 10.7 %collective-permute-start.16 = (bf16[1536,256]{1,0:T(8,128)(2,1)}, bf16[1536,256]{1,0:T(8,128)(2,1)S(1)}, u32[]{:S(2)}, u32[]{:S(2)}) collective-permute-start(bf16[1536,256]{1,0:T(8,128)(2,1)} %get-tuple-element.15), channel_id=1, source_target_pairs={{0,1},{1,0},{2,3},{3,2},{4,5},{5,4},{6,7},{7,6},{8,9},{9,8},{10,11... | collective-permute-start | bytes 2359304 | tf_op jit(solution)/shard_map/ppermute | solution.py:403
  241.2 5.7 %copy-start.17 = (bf16[1536,256]{1,0:T(8,128)(2,1)S(1)}, bf16[1536,256]{1,0:T(8,128)(2,1)}, u32[]{:S(2)}) copy-start(bf16[1536,256]{1,0:T(8,128)(2,1)} %copy-done.16) | copy-start | bytes 2359300
  241.2 16.3 %all-to-all-start.2 = ((bf16[4,400,256]{2,1,0:T(8,128)(2,1)}), bf16[4,400,256]{2,1,0:T(8,128)(2,1)S(1)}, u32[]{:S(2)}, u32[]{:S(2)}) async-start(bf16[4,400,256]{2,1,0:T(8,128)(2,1)} %pad_maximum_fusion.2), calls=%async_computation.2 | async-start | bytes 1638400 | tf_op jit(solution)/shard_map/all_to_all | solution.py:402
  257.5 15.0 %all-to-all-start.1 = ((bf16[4,384,256]{2,1,0:T(8,128)(2,1)}), bf16[4,384,256]{2,1,0:T(8,128)(2,1)S(1)}, u32[]{:S(2)}, u32[]{:S(2)}) async-start(bf16[4,384,256]{2,1,0:T(8,128)(2,1)} %bitcast.32), calls=%async_computation.1 | async-start | bytes 1572864 | tf_op jit(solution)/shard_map/all_to_all | solution.py:405
  262.5 29.1 %copy-start.31 = (bf16[128,256]{1,0:T(8,128)(2,1)S(1)}, bf16[128,256]{1,0:T(8,128)(2,1)}, u32[]{:S(2)}) copy-start(bf16[128,256]{1,0:T(8,128)(2,1)} %copy-done.30) | copy-start | bytes 196612
  262.5 29.1 %copy-start.33 = (bf16[128,256]{1,0:T(8,128)(2,1)S(1)}, bf16[128,256]{1,0:T(8,128)(2,1)}, u32[]{:S(2)}) copy-start(bf16[128,256]{1,0:T(8,128)(2,1)} %copy-done.32) | copy-start | bytes 196612
  262.9 28.7 %collective-permute-start.18 = (bf16[400,256]{1,0:T(8,128)(2,1)S(1)}, bf16[400,256]{1,0:T(8,128)(2,1)S(1)}, u32[]{:S(2)}, u32[]{:S(2)}) collective-permute-start(bf16[400,256]{1,0:T(8,128)(2,1)S(1)} %concatenate.47), channel_id=1, source_target_pairs={{0,2},{2,0},{1,3},{3,1},{4,6},{6,4},{5,7},{7,5},{8,10},{10,8},{9,1... | collective-permute-start | bytes 614408 | tf_op jit(solution)/shard_map/ppermute | solution.py:408
Sparse Core Ops, SparseCore 0:
  10.8 36.4 all-gather.3
  61.0 41.9 all-gather.5
  124.0 50.8 all-gather.7

commit v6 on v4

--- a/solution.py
+++ b/solution.py
@@ -306,17 +306,19 @@
     y_ring = functools.partial(lax.ppermute, axis_name=("y", "c"), perm=core_ring(NY))
     got = lax.all_to_all(packets, ("zl", "x"), split_axis=0, concat_axis=0, tiled=True)
     mine = unpack(got)
-    partner = lax.ppermute(mine, "zh", shift(NH, 1))
+    z = {0: weight}
+    for step in (1, 2):
+        z[-step] = lax.ppermute(z[1 - step], "zl", Z_BACK)
+    partner = lax.ppermute(after(mine, z[-2]), "zh", shift(NH, 1))
     g = [jnp.stack([mine, partner])]
     g.append(y_ring(g[0]))
     wait_for = {2: got, 3: partner, 4: g[1]}
-    z = {0: weight}
     for step in (1, 2, 3, 4):
         block = z[step - 1]
         if step in wait_for:
             block = after(block, wait_for[step])
         z[step] = lax.ppermute(block, "zl", Z_RING)
-        if step < 4:
+        if step == 3:
             z[-step] = lax.ppermute(z[1 - step], "zl", Z_BACK)
     early = []
     for steps in EARLY:
@@ -327,7 +329,7 @@
     for _ in range(NY - 2):
         g.append(y_ring(g[-1]))
     late = [jnp.stack([after(z[n], g[3]) if n < 0 else z[n] for n in LATE])]
-    for _ in range(NX - 1):
+    for _ in range(NX - 2):
         late.append(x_ring(late[-1]))
     most = lax.ppermute(jnp.concatenate(g[:3]), "c", shift(NC, 1))
     last = lax.ppermute(g[3], "c", shift(NC, 1))
@@ -347,6 +349,8 @@
         cost_estimate=pl.CostEstimate(flops=20_000_000, bytes_accessed=10_000_000, transcendentals=0),
         name="norm",
     )(where, gain_column, *g, most, last)
+
+    late.append(x_ring(after(late[2], normed)))
 
     width = w_query.shape[1]
     hbm = pl.BlockSpec(memory_space=pl.ANY)

time: 289 us -> 291 us (level)
  the two profiles are of different devices: /device:TPU:47 before, /device:TPU:136 now
where the time goes in v6:
time: 291 us; the launch traced here: 289 us
  waiting for transfers between devices  112 us (38%)
  starting transfers between devices  93.3 us (32%)
  Pallas kernels  33.2 us (11%)
  local copies, waits for them, and re-layouts  20.1 us (7%)
  between operations  18.6 us (6%)
  other arithmetic  10.9 us (4%)
    ppermute x3, waiting for transfers between devices, per_device(): z[-step] = lax.ppermute(z[1 - step], 'zl', Z_BACK)  29.9 us
    ppermute x1, waiting for transfers between devices, per_device(): lax.ppermute(jnp.concatenate([leave, split_sums(*sums)], axis=0), 'zh', s...  18.9 us
    pallas_call x1, Pallas kernels, per_device(): pl.pallas_call(main_kernel, out_shape=(jax.ShapeDtypeStruct((LEN, width),...  18.6 us
    ppermute x2, waiting for transfers between devices, per_device(): late.append(x_ring(late[-1]))  17.9 us
    all_to_all x1, starting transfers between devices, per_device(): lax.all_to_all(packets, ('zl', 'x'), split_axis=0, concat_axis=0, tiled=T...  13.9 us
    ppermute x3, starting transfers between devices, per_device(): z[-step] = lax.ppermute(z[1 - step], 'zl', Z_BACK)  13.7 us
    ppermute x4, starting transfers between devices, per_device(): z[step] = lax.ppermute(block, 'zl', Z_RING)  13.4 us
    ppermute x1, waiting for transfers between devices, per_device(): partner = lax.ppermute(after(mine, z[-2]), 'zh', shift(NH, 1))  13.1 us
  transfers between devices with their start and end apart: 25, of which 12 were waited for; matrix products, arithmetic and copies ran while one was open for 6% of the time, Pallas kernels for 5%

profile of v6, /device:TPU:136, one launch (start us, length us, event | category | flops | bytes accessed | tf_op | source)
XLA Modules:
  0.0 289.2 jit_solution(10439747008103427726)
XLA Ops:
  7.2 0.9 constant_dynamic-update-slice_fusion.2
  8.2 0.9 constant_dynamic-update-slice_fusion.1
  9.1 0.9 constant_dynamic-update-slice_fusion
  10.0 0.7 copy-done.24
  10.7 0.7 and_select_fusion.1
  12.3 0.8 fusion.2
  13.1 13.9 %all-to-all-start = ((bf16[32,56,128]{2,1,0:T(8,128)(2,1)}), bf16[32,56,128]{2,1,0:T(8,128)(2,1)S(1)}, u32[]{:S(2)}, u32[]{:S(2)}) async-start(bf16[32,56,128]{2,1,0:T(8,128)(2,1)} %fusion.2), calls=%async_computation | async-start | bytes 917504 | tf_op jit(solution)/shard_map/all_to_all | solution.py:307
  27.0 2.5 collective-permute-start
  29.5 4.3 %collective-permute-start.8 = (bf16[192,768]{1,0:T(8,128)(2,1)S(1)}, bf16[192,768]{1,0:T(8,128)(2,1)S(1)}, u32[]{:S(2)}, u32[]{:S(2)}) collective-permute-start(bf16[192,768]{1,0:T(8,128)(2,1)S(1)} %copy-done.25), channel_id=1, source_target_pairs={{0,128},{128,256},{256,384},{384,448},{448,320},{320,192},{192,64}... | collective-permute-start | bytes 884744 | tf_op jit(solution)/shard_map/ppermute | solution.py:320
  33.8 25.3 %collective-permute-done = bf16[192,768]{1,0:T(8,128)(2,1)S(1)} collective-permute-done((bf16[192,768]{1,0:T(8,128)(2,1)S(1)}, bf16[192,768]{1,0:T(8,128)(2,1)S(1)}, u32[]{:S(2)}, u32[]{:S(2)}) %collective-permute-start) | collective-permute-done | bytes 294944 | tf_op jit(solution)/shard_map/ppermute | solution.py:311
  59.1 0.9 pad_maximum_fusion.3
  60.0 6.5 %collective-permute-start.1 = (bf16[192,768]{1,0:T(8,128)(2,1)S(1)}, bf16[192,768]{1,0:T(8,128)(2,1)S(1)}, u32[]{:S(2)}, u32[]{:S(2)}) collective-permute-start(bf16[192,768]{1,0:T(8,128)(2,1)S(1)} %collective-permute-done), channel_id=1, source_target_pairs={{128,0},{256,128},{384,256},{448,384},{320,448},{192,320},{64,192}... | collective-permute-start | bytes 884744 | tf_op jit(solution)/shard_map/ppermute | solution.py:311
  66.5 4.6 %collective-permute-done.1 = bf16[192,768]{1,0:T(8,128)(2,1)S(1)} collective-permute-done((bf16[192,768]{1,0:T(8,128)(2,1)S(1)}, bf16[192,768]{1,0:T(8,128)(2,1)S(1)}, u32[]{:S(2)}, u32[]{:S(2)}) %collective-permute-start.1) | collective-permute-done | bytes 294944 | tf_op jit(solution)/shard_map/ppermute | solution.py:311
  73.5 8.2 %collective-permute-start.2 = (bf16[384,256]{1,0:T(8,128)(2,1)S(1)}, bf16[384,256]{1,0:T(8,128)(2,1)S(1)}, u32[]{:S(2)}, u32[]{:S(2)}) collective-permute-start(bf16[384,256]{1,0:T(8,128)(2,1)S(1)} %get-tuple-element.37), channel_id=1, source_target_pairs={{0,2},{2,0},{1,3},{3,1},{4,6},{6,4},{5,7},{7,5},{8,10},{10,8},{9,1... | collective-permute-start | bytes 589832 | tf_op jit(solution)/shard_map/ppermute | solution.py:312
  81.7 0.5 slice.197
  82.9 2.0 collective-permute-start.9
  85.0 13.1 %collective-permute-done.2 = bf16[384,256]{1,0:T(8,128)(2,1)S(1)} collective-permute-done((bf16[384,256]{1,0:T(8,128)(2,1)S(1)}, bf16[384,256]{1,0:T(8,128)(2,1)S(1)}, u32[]{:S(2)}, u32[]{:S(2)}) %collective-permute-start.2) | collective-permute-done | bytes 196640 | tf_op jit(solution)/shard_map/ppermute | solution.py:312
  98.1 3.5 %collective-permute-start.3 = (bf16[2,384,256]{2,1,0:T(8,128)(2,1)S(1)}, bf16[2,384,256]{2,1,0:T(8,128)(2,1)S(1)}, u32[]{:S(2)}, u32[]{:S(2)}) collective-permute-start(bf16[2,384,256]{2,1,0:T(8,128)(2,1)S(1)} %pad_maximum_fusion.5.rest_0_), channel_id=1, source_target_pairs={{0,4},{1,13},{4,8},{5,1},{8,12},{9,5},{12,0},{13,9},{2,6},{3,15},{... | collective-permute-start | bytes 1179656 | tf_op jit(solution)/shard_map/ppermute | solution.py:314
  101.6 0.5 slice.198
  102.8 2.0 collective-permute-done.9
  104.8 4.7 %collective-permute-start.10 = (bf16[192,768]{1,0:T(8,128)(2,1)S(1)}, bf16[192,768]{1,0:T(8,128)(2,1)S(1)}, u32[]{:S(2)}, u32[]{:S(2)}) collective-permute-start(bf16[192,768]{1,0:T(8,128)(2,1)S(1)} %broadcast_add_fusion.2), channel_id=1, source_target_pairs={{0,128},{128,256},{256,384},{384,448},{448,320},{320,192},{192,64}... | collective-permute-start | bytes 884744 | tf_op jit(solution)/shard_map/ppermute | solution.py:320
  109.5 3.2 %collective-permute-start.4 = (bf16[2,384,256]{2,1,0:T(8,128)(2,1)S(1)}, bf16[2,384,256]{2,1,0:T(8,128)(2,1)S(1)}, u32[]{:S(2)}, u32[]{:S(2)}) collective-permute-start(bf16[2,384,256]{2,1,0:T(8,128)(2,1)S(1)} %collective-permute-done.3.rest_1_), channel_id=1, source_target_pairs={{0,4},{1,13},{4,8},{5,1},{8,12},{9,5},{12,0},{13,9},{2,6},{3,15},{... | collective-permute-start | bytes 1179656 | tf_op jit(solution)/shard_map/ppermute | solution.py:330
  112.7 0.9 pad_maximum_fusion.4
  113.6 5.5 %collective-permute-done.4.rest_2_ = bf16[2,384,256]{2,1,0:T(8,128)(2,1)S(1)} collective-permute-done((bf16[2,384,256]{2,1,0:T(8,128)(2,1)S(1)}, bf16[2,384,256]{2,1,0:T(8,128)(2,1)S(1)}, u32[]{:S(2)}, u32[]{:S(2)}) %collective-permute-start.4) | collective-permute-done | bytes 393248 | tf_op jit(solution)/shard_map/ppermute | solution.py:330
  119.2 3.2 %collective-permute-start.5 = (bf16[2,384,256]{2,1,0:T(8,128)(2,1)S(1)}, bf16[2,384,256]{2,1,0:T(8,128)(2,1)}, u32[]{:S(2)}, u32[]{:S(2)}) collective-permute-start(bf16[2,384,256]{2,1,0:T(8,128)(2,1)S(1)} %collective-permute-done.4.rest_2_), channel_id=1, source_target_pairs={{0,4},{1,13},{4,8},{5,1},{8,12},{9,5},{12,0},{13,9},{2,6},{3,15},{... | collective-permute-start | bytes 1179656 | tf_op jit(solution)/shard_map/ppermute | solution.py:330
  122.4 4.7 %collective-permute-start.11 = (bf16[192,768]{1,0:T(8,128)(2,1)S(1)}, bf16[192,768]{1,0:T(8,128)(2,1)S(1)}, u32[]{:S(2)}, u32[]{:S(2)}) collective-permute-start(bf16[192,768]{1,0:T(8,128)(2,1)S(1)} %collective-permute-done.1), channel_id=1, source_target_pairs={{128,0},{256,128},{384,256},{448,384},{320,448},{192,320},{64,192}... | collective-permute-start | bytes 884744 | tf_op jit(solution)/shard_map/ppermute | solution.py:322
  128.3 2.4 collective-permute-start.12
  130.7 1.2 slice.199
  132.6 9.7 %collective-permute-done.12 = bf16[192,768]{1,0:T(8,128)(2,1)S(1)} collective-permute-done((bf16[192,768]{1,0:T(8,128)(2,1)S(1)}, bf16[192,768]{1,0:T(8,128)(2,1)S(1)}, u32[]{:S(2)}, u32[]{:S(2)}) %collective-permute-start.12) | collective-permute-done | bytes 294944 | tf_op jit(solution)/shard_map/ppermute | solution.py:320
  142.5 2.9 %collective-permute-start.13 = (bf16[3,192,768]{2,1,0:T(8,128)(2,1)S(1)}, bf16[3,192,768]{2,1,0:T(8,128)(2,1)}, u32[]{:S(2)}, u32[]{:S(2)}) collective-permute-start(bf16[3,192,768]{2,1,0:T(8,128)(2,1)S(1)} %pad_maximum_fusion.1.rest_3_), channel_id=1, source_target_pairs={{0,16},{1,49},{16,32},{17,1},{32,48},{33,17},{48,0},{49,33},{2,18}... | collective-permute-start | bytes 2654216 | tf_op jit(solution)/shard_map/ppermute | solution.py:333
  145.5 1.2 pad_maximum_fusion
  146.6 1.9 collective-permute-start.6
  148.5 17.9 %collective-permute-done.13.rest_4_ = bf16[3,192,768]{2,1,0:T(8,128)(2,1)} collective-permute-done((bf16[3,192,768]{2,1,0:T(8,128)(2,1)S(1)}, bf16[3,192,768]{2,1,0:T(8,128)(2,1)}, u32[]{:S(2)}, u32[]{:S(2)}) %collective-permute-start.13) | collective-permute-done | bytes 884768 | tf_op jit(solution)/shard_map/ppermute | solution.py:333
  166.4 1.9 collective-permute-start.14
  168.4 2.3 collective-permute-start.7
  170.7 1.1 copy.25.gain_ref
  172.4 1.0 copy-done.10
  173.4 1.0 copy-done.12
  174.4 1.0 copy-done.14
  175.4 4.2 %norm.1 = (bf16[6144,256]{1,0:T(8,128)(2,1)S(1)}, bf16[6144,256]{1,0:T(8,128)(2,1)S(1)}, f32[2,256]{1,0:T(2,128)S(1)}) custom-call(s32[5]{0:T(128)S(1)} %stack.44.where_ref, f32[6144,1]{1,0:T(8,128)S(1)} %copy.25.gain_ref, bf16[2,384,256]{2,1,0:T(8,128)(2,1)S(1)} %copy-done.14, bf16[2,384,256]{2,1,0:T(8,128)(2,1)S(1)} %copy-done.10, ...), custom_call_target="tpu_custom_call" | custom-call | flops 20000000 | bytes 10000000 | tf_op jit(solution)/shard_map/norm/pallas_call | solution.py:339
  179.6 1.7 copy-done.8
  181.3 1.6 copy-done.1
  182.9 0.6 slice.154
  184.2 2.1 broadcast_add_fusion
  186.4 2.8 collective-permute-start.15
  189.5 10.4 %first.1.part_ref = f32[256,768]{1,0:T(8,128)} custom-call(s32[5]{0:T(128)} %copy-done.19, bf16[6144,256]{1,0:T(8,128)(2,1)} %copy-done.1, bf16[4,1,192,768]{3,2,1,0:T(8,128)(2,1)} %bitcast.53, bf16[4,2,192,768]{3,2,1,0:T(8,128)(2,1)} %bitcast.49, bf16[4,2,192,768]{3,2,1,0:T(8,128)(2,1)} %bitcast.51, bf16[3,192,768]{2,1,0:T(8,128)(2,1)} %copy-done.4, ...), custom_call_target="tpu_custom_call" | custom-call | flops 2200000000 | bytes 12000000 | tf_op jit(solution)/shard_map/first/pallas_call | solution.py:358
  199.9 2.9 collective-permute-done.15.rest_6_
  202.9 1.1 copy-done.7
  204.0 0.9 copy-done.18
  204.9 18.6 %core.1 = (bf16[256,256]{1,0:T(8,128)(2,1)}, bf16[1536,256]{1,0:T(8,128)(2,1)S(1)}, bf16[1552,256]{1,0:T(8,128)(2,1)S(1)}, bf16[1536,256]{1,0:T(8,128)(2,1)}, bf16[1552,256]{1,0:T(8,128)(2,1)S(1)}) custom-call(s32[5]{0:T(128)S(1)} %copy-done.20, f32[6144,1]{1,0:T(8,128)S(1)} %copy.25.gain_ref, f32[2,256]{1,0:T(2,128)S(1)} %get-tuple-element.10.stat_ref, ...), custom_call_target="tpu_custom_call" | custom-call | flops 3000000000 | bytes 20000000 | tf_op jit(solution)/shard_map/core/pallas_call | solution.py:375
  223.5 0.9 copy-done.16
  224.3 1.9 collective-permute-start.17
  226.2 2.4 collective-permute-start.16
  228.9 1.3 add_convert_fusion
  230.3 1.0 pad_maximum_fusion.2
  231.2 5.0 %all-to-all-start.2 = ((bf16[4,400,256]{2,1,0:T(8,128)(2,1)}), bf16[4,400,256]{2,1,0:T(8,128)(2,1)S(1)}, u32[]{:S(2)}, u32[]{:S(2)}) async-start(bf16[4,400,256]{2,1,0:T(8,128)(2,1)} %pad_maximum_fusion.2), calls=%async_computation.2 | async-start | bytes 1638400 | tf_op jit(solution)/shard_map/all_to_all | solution.py:402
  236.2 0.8 dynamic_slice.3
  237.0 1.1 add_convert_fusion.1
  238.0 9.5 %all-to-all-done.2 = bf16[4,400,256]{2,1,0:T(8,128)(2,1)S(1)} async-done(((bf16[4,400,256]{2,1,0:T(8,128)(2,1)}), bf16[4,400,256]{2,1,0:T(8,128)(2,1)S(1)}, u32[]{:S(2)}, u32[]{:S(2)}) %all-to-all-start.2) | async-done | bytes 819232 | tf_op jit(solution)/shard_map/all_to_all | solution.py:402
  247.6 4.9 %all-to-all-start.1 = ((bf16[4,384,256]{2,1,0:T(8,128)(2,1)}), bf16[4,384,256]{2,1,0:T(8,128)(2,1)S(1)}, u32[]{:S(2)}, u32[]{:S(2)}) async-start(bf16[4,384,256]{2,1,0:T(8,128)(2,1)} %bitcast.32), calls=%async_computation.1 | async-start | bytes 1572864 | tf_op jit(solution)/shard_map/all_to_all | solution.py:405
  252.9 8.0 %collective-permute-start.18 = (bf16[400,256]{1,0:T(8,128)(2,1)S(1)}, bf16[400,256]{1,0:T(8,128)(2,1)S(1)}, u32[]{:S(2)}, u32[]{:S(2)}) collective-permute-start(bf16[400,256]{1,0:T(8,128)(2,1)S(1)} %concatenate.47), channel_id=1, source_target_pairs={{0,2},{2,0},{1,3},{3,1},{4,6},{6,4},{5,7},{7,5},{8,10},{10,8},{9,1... | collective-permute-start | bytes 614408 | tf_op jit(solution)/shard_map/ppermute | solution.py:408
  261.0 1.6 all-to-all-done.1
  262.7 18.9 %collective-permute-done.18 = bf16[400,256]{1,0:T(8,128)(2,1)S(1)} collective-permute-done((bf16[400,256]{1,0:T(8,128)(2,1)S(1)}, bf16[400,256]{1,0:T(8,128)(2,1)S(1)}, u32[]{:S(2)}, u32[]{:S(2)}) %collective-permute-start.18) | collective-permute-done | bytes 204832 | tf_op jit(solution)/shard_map/ppermute | solution.py:408
  281.8 0.8 copy.28
  (118 shorter events, 5.2 us)
Async XLA Ops:
  7.2 4.7 %copy-start = (bf16[256,384]{1,0:T(8,128)(2,1)S(1)}, bf16[256,384]{1,0:T(8,128)(2,1)}, u32[]{:S(2)}) copy-start(bf16[256,384]{1,0:T(8,128)(2,1)} %param.10) | copy-start | bytes 589828
  7.2 182.2 %all-gather.4.cloned.1.call-start = ((), (), s32[]{:S(2)}) async-start(), calls=%async_computation.3 | async-start | bytes 1474560 | tf_op jit(solution)/shard_map/all_gather | solution.py:325
  10.0 0.7 copy-start.24
  12.2 14.9 %copy-start.25 = (bf16[192,768]{1,0:T(8,128)(2,1)S(1)}, bf16[192,768]{1,0:T(8,128)(2,1)}, u32[]{:S(2)}) copy-start(bf16[192,768]{1,0:T(8,128)(2,1)} %copy-done.24) | copy-start | bytes 884740
  13.1 59.2 %all-to-all-start = ((bf16[32,56,128]{2,1,0:T(8,128)(2,1)}), bf16[32,56,128]{2,1,0:T(8,128)(2,1)S(1)}, u32[]{:S(2)}, u32[]{:S(2)}) async-start(bf16[32,56,128]{2,1,0:T(8,128)(2,1)} %fusion.2), calls=%async_computation | async-start | bytes 917504 | tf_op jit(solution)/shard_map/all_to_all | solution.py:307
  27.0 162.4 %all-gather.6.cloned.1.call-start = ((), (), s32[]{:S(2)}) async-start(), calls=%async_computation.4 | async-start | bytes 2949120 | tf_op jit(solution)/shard_map/all_gather | solution.py:325
  27.0 32.0 %collective-permute-start = (bf16[192,768]{1,0:T(8,128)(2,1)S(1)}, bf16[192,768]{1,0:T(8,128)(2,1)S(1)}, u32[]{:S(2)}, u32[]{:S(2)}) collective-permute-start(bf16[192,768]{1,0:T(8,128)(2,1)S(1)} %copy-done.25), channel_id=1, source_target_pairs={{128,0},{256,128},{384,256},{448,384},{320,448},{192,320},{64,192}... | collective-permute-start | bytes 884744 | tf_op jit(solution)/shard_map/ppermute | solution.py:311
  29.5 29.6 %collective-permute-start.8 = (bf16[192,768]{1,0:T(8,128)(2,1)S(1)}, bf16[192,768]{1,0:T(8,128)(2,1)S(1)}, u32[]{:S(2)}, u32[]{:S(2)}) collective-permute-start(bf16[192,768]{1,0:T(8,128)(2,1)S(1)} %copy-done.25), channel_id=1, source_target_pairs={{0,128},{128,256},{256,384},{384,448},{448,320},{320,192},{192,64}... | collective-permute-start | bytes 884744 | tf_op jit(solution)/shard_map/ppermute | solution.py:320
  60.0 129.4 %all-gather.8.cloned.1.call-start = ((), (), s32[]{:S(2)}) async-start(), calls=%async_computation.5 | async-start | bytes 2949120 | tf_op jit(solution)/shard_map/all_gather | solution.py:325
  60.0 11.1 %collective-permute-start.1 = (bf16[192,768]{1,0:T(8,128)(2,1)S(1)}, bf16[192,768]{1,0:T(8,128)(2,1)S(1)}, u32[]{:S(2)}, u32[]{:S(2)}) collective-permute-start(bf16[192,768]{1,0:T(8,128)(2,1)S(1)} %collective-permute-done), channel_id=1, source_target_pairs={{128,0},{256,128},{384,256},{448,384},{320,448},{192,320},{64,192}... | collective-permute-start | bytes 884744 | tf_op jit(solution)/shard_map/ppermute | solution.py:311
  73.1 9.8 %copy-start.26 = (bf16[128,256]{1,0:T(8,128)(2,1)}, bf16[128,256]{1,0:T(8,128)(2,1)S(1)}, u32[]{:S(2)}) copy-start(bf16[128,256]{1,0:T(8,128)(2,1)S(1)} %convolution_convert_fusion.2) | copy-start | bytes 196612
  73.4 9.5 %copy-start.28 = (bf16[128,256]{1,0:T(8,128)(2,1)}, bf16[128,256]{1,0:T(8,128)(2,1)S(1)}, u32[]{:S(2)}) copy-start(bf16[128,256]{1,0:T(8,128)(2,1)S(1)} %convolution_convert_fusion.1) | copy-start | bytes 196612
  73.5 24.6 %collective-permute-start.2 = (bf16[384,256]{1,0:T(8,128)(2,1)S(1)}, bf16[384,256]{1,0:T(8,128)(2,1)S(1)}, u32[]{:S(2)}, u32[]{:S(2)}) collective-permute-start(bf16[384,256]{1,0:T(8,128)(2,1)S(1)} %get-tuple-element.37), channel_id=1, source_target_pairs={{0,2},{2,0},{1,3},{3,1},{4,6},{6,4},{5,7},{7,5},{8,10},{10,8},{9,1... | collective-permute-start | bytes 589832 | tf_op jit(solution)/shard_map/ppermute | solution.py:312
  82.9 21.9 %collective-permute-start.9 = (bf16[192,768]{1,0:T(8,128)(2,1)S(1)}, bf16[192,768]{1,0:T(8,128)(2,1)S(1)}, u32[]{:S(2)}, u32[]{:S(2)}) collective-permute-start(bf16[192,768]{1,0:T(8,128)(2,1)S(1)} %broadcast_add_fusion.4), channel_id=1, source_target_pairs={{0,128},{128,256},{256,384},{384,448},{448,320},{320,192},{192,64}... | collective-permute-start | bytes 884744 | tf_op jit(solution)/shard_map/ppermute | solution.py:320
  98.1 11.4 %copy-start.13 = (bf16[2,384,256]{2,1,0:T(8,128)(2,1)}, bf16[2,384,256]{2,1,0:T(8,128)(2,1)S(1)}, u32[]{:S(2)}) copy-start(bf16[2,384,256]{2,1,0:T(8,128)(2,1)S(1)} %pad_maximum_fusion.5.rest_0_) | copy-start | bytes 1179652
  98.1 11.4 %collective-permute-start.3 = (bf16[2,384,256]{2,1,0:T(8,128)(2,1)S(1)}, bf16[2,384,256]{2,1,0:T(8,128)(2,1)S(1)}, u32[]{:S(2)}, u32[]{:S(2)}) collective-permute-start(bf16[2,384,256]{2,1,0:T(8,128)(2,1)S(1)} %pad_maximum_fusion.5.rest_0_), channel_id=1, source_target_pairs={{0,4},{1,13},{4,8},{5,1},{8,12},{9,5},{12,0},{13,9},{2,6},{3,15},{... | collective-permute-start | bytes 1179656 | tf_op jit(solution)/shard_map/ppermute | solution.py:314
  104.8 23.5 %collective-permute-start.10 = (bf16[192,768]{1,0:T(8,128)(2,1)S(1)}, bf16[192,768]{1,0:T(8,128)(2,1)S(1)}, u32[]{:S(2)}, u32[]{:S(2)}) collective-permute-start(bf16[192,768]{1,0:T(8,128)(2,1)S(1)} %broadcast_add_fusion.2), channel_id=1, source_target_pairs={{0,128},{128,256},{256,384},{384,448},{448,320},{320,192},{192,64}... | collective-permute-start | bytes 884744 | tf_op jit(solution)/shard_map/ppermute | solution.py:320
  109.5 35.9 %copy-start.9 = (bf16[2,384,256]{2,1,0:T(8,128)(2,1)}, bf16[2,384,256]{2,1,0:T(8,128)(2,1)S(1)}, u32[]{:S(2)}) copy-start(bf16[2,384,256]{2,1,0:T(8,128)(2,1)S(1)} %collective-permute-done.3.rest_1_) | copy-start | bytes 1179652
  109.5 9.7 %collective-permute-start.4 = (bf16[2,384,256]{2,1,0:T(8,128)(2,1)S(1)}, bf16[2,384,256]{2,1,0:T(8,128)(2,1)S(1)}, u32[]{:S(2)}, u32[]{:S(2)}) collective-permute-start(bf16[2,384,256]{2,1,0:T(8,128)(2,1)S(1)} %collective-permute-done.3.rest_1_), channel_id=1, source_target_pairs={{0,4},{1,13},{4,8},{5,1},{8,12},{9,5},{12,0},{13,9},{2,6},{3,15},{... | collective-permute-start | bytes 1179656 | tf_op jit(solution)/shard_map/ppermute | solution.py:330
  119.2 26.3 %copy-start.11 = (bf16[2,384,256]{2,1,0:T(8,128)(2,1)}, bf16[2,384,256]{2,1,0:T(8,128)(2,1)S(1)}, u32[]{:S(2)}) copy-start(bf16[2,384,256]{2,1,0:T(8,128)(2,1)S(1)} %collective-permute-done.4.rest_2_) | copy-start | bytes 1179652
  119.2 11.6 %collective-permute-start.5 = (bf16[2,384,256]{2,1,0:T(8,128)(2,1)S(1)}, bf16[2,384,256]{2,1,0:T(8,128)(2,1)}, u32[]{:S(2)}, u32[]{:S(2)}) collective-permute-start(bf16[2,384,256]{2,1,0:T(8,128)(2,1)S(1)} %collective-permute-done.4.rest_2_), channel_id=1, source_target_pairs={{0,4},{1,13},{4,8},{5,1},{8,12},{9,5},{12,0},{13,9},{2,6},{3,15},{... | collective-permute-start | bytes 1179656 | tf_op jit(solution)/shard_map/ppermute | solution.py:330
  122.4 10.2 %collective-permute-start.11 = (bf16[192,768]{1,0:T(8,128)(2,1)S(1)}, bf16[192,768]{1,0:T(8,128)(2,1)S(1)}, u32[]{:S(2)}, u32[]{:S(2)}) collective-permute-start(bf16[192,768]{1,0:T(8,128)(2,1)S(1)} %collective-permute-done.1), channel_id=1, source_target_pairs={{128,0},{256,128},{384,256},{448,384},{320,448},{192,320},{64,192}... | collective-permute-start | bytes 884744 | tf_op jit(solution)/shard_map/ppermute | solution.py:322
  128.3 14.0 %collective-permute-start.12 = (bf16[192,768]{1,0:T(8,128)(2,1)S(1)}, bf16[192,768]{1,0:T(8,128)(2,1)S(1)}, u32[]{:S(2)}, u32[]{:S(2)}) collective-permute-start(bf16[192,768]{1,0:T(8,128)(2,1)S(1)} %broadcast_add_fusion.1), channel_id=1, source_target_pairs={{0,128},{128,256},{256,384},{384,448},{448,320},{320,192},{192,64}... | collective-permute-start | bytes 884744 | tf_op jit(solution)/shard_map/ppermute | solution.py:320
  142.5 4.1 %copy-start.4 = (bf16[3,192,768]{2,1,0:T(8,128)(2,1)}, bf16[3,192,768]{2,1,0:T(8,128)(2,1)S(1)}, u32[]{:S(2)}) copy-start(bf16[3,192,768]{2,1,0:T(8,128)(2,1)S(1)} %pad_maximum_fusion.1.rest_3_) | copy-start | bytes 2654212
  142.5 28.2 %copy-start.30 = (f32[6144]{0:T(1024)S(1)}, f32[6144]{0:T(1024)}, u32[]{:S(2)}) copy-start(f32[6144]{0:T(1024)} %param.13) | copy-start | bytes 73732
  142.5 23.9 %collective-permute-start.13 = (bf16[3,192,768]{2,1,0:T(8,128)(2,1)S(1)}, bf16[3,192,768]{2,1,0:T(8,128)(2,1)}, u32[]{:S(2)}, u32[]{:S(2)}) collective-permute-start(bf16[3,192,768]{2,1,0:T(8,128)(2,1)S(1)} %pad_maximum_fusion.1.rest_3_), channel_id=1, source_target_pairs={{0,16},{1,49},{16,32},{17,1},{32,48},{33,17},{48,0},{49,33},{2,18}... | collective-permute-start | bytes 2654216 | tf_op jit(solution)/shard_map/ppermute | solution.py:333
  146.6 25.8 %collective-permute-start.6 = (bf16[6,384,256]{2,1,0:T(8,128)(2,1)}, bf16[6,384,256]{2,1,0:T(8,128)(2,1)}, u32[]{:S(2)}, u32[]{:S(2)}) collective-permute-start(bf16[6,384,256]{2,1,0:T(8,128)(2,1)} %pad_maximum_fusion), channel_id=1, source_target_pairs={{0,1},{1,0},{2,3},{3,2},{4,5},{5,4},{6,7},{7,6},{8,9},{9,8},{10,11... | collective-permute-start | bytes 3538952 | tf_op jit(solution)/shard_map/ppermute | solution.py:334
  166.4 17.8 %collective-permute-start.14 = (bf16[3,192,768]{2,1,0:T(8,128)(2,1)}, bf16[3,192,768]{2,1,0:T(8,128)(2,1)}, u32[]{:S(2)}, u32[]{:S(2)}) collective-permute-start(bf16[3,192,768]{2,1,0:T(8,128)(2,1)} %collective-permute-done.13.rest_4_), channel_id=1, source_target_pairs={{0,16},{1,49},{16,32},{17,1},{32,48},{33,17},{48,0},{49,33},{2,18}... | collective-permute-start | bytes 2654216 | tf_op jit(solution)/shard_map/ppermute | solution.py:333
  168.4 4.0 %collective-permute-start.7 = (bf16[2,384,256]{2,1,0:T(8,128)(2,1)}, bf16[2,384,256]{2,1,0:T(8,128)(2,1)}, u32[]{:S(2)}, u32[]{:S(2)}) collective-permute-start(bf16[2,384,256]{2,1,0:T(8,128)(2,1)} %collective-permute-done.5.rest_3_), channel_id=1, source_target_pairs={{0,1},{1,0},{2,3},{3,2},{4,5},{5,4},{6,7},{7,6},{8,9},{9,8},{10,11... | collective-permute-start | bytes 1179656 | tf_op jit(solution)/shard_map/ppermute | solution.py:335
  171.9 7.7 %copy-start.19 = (s32[5]{0:T(128)}, s32[5]{0:T(128)S(1)}, u32[]{:S(2)}) copy-start(s32[5]{0:T(128)S(1)} %stack.44.where_ref) | copy-start | bytes 64
  172.4 1.0 copy-start.10
  173.4 1.0 copy-start.12
  174.4 1.0 copy-start.14
  179.6 1.7 copy-start.8
  181.3 1.6 copy-start.1
  181.3 7.9 %copy-start.21 = (s32[256]{0:T(256)S(1)}, s32[256]{0:T(256)}, u32[]{:S(2)}) copy-start(s32[256]{0:T(256)} %param.12) | copy-start | bytes 3076
  186.4 16.5 %collective-permute-start.15 = (bf16[3,192,768]{2,1,0:T(8,128)(2,1)}, bf16[3,192,768]{2,1,0:T(8,128)(2,1)}, u32[]{:S(2)}, u32[]{:S(2)}) collective-permute-start(bf16[3,192,768]{2,1,0:T(8,128)(2,1)} %broadcast_add_fusion), channel_id=1, source_target_pairs={{0,16},{1,49},{16,32},{17,1},{32,48},{33,17},{48,0},{49,33},{2,18}... | collective-permute-start | bytes 2654216 | tf_op jit(solution)/shard_map/ppermute | solution.py:353
  189.4 13.4 %copy-start.2 = (bf16[1536,768]{1,0:T(8,128)(2,1)S(1)}, bf16[1536,768]{1,0:T(8,128)(2,1)}, u32[]{:S(2)}) copy-start(bf16[1536,768]{1,0:T(8,128)(2,1)} %all-gather.6.cloned.1.call-done) | copy-start | bytes 7077892
  189.4 13.4 %copy-start.3 = (bf16[1536,768]{1,0:T(8,128)(2,1)S(1)}, bf16[1536,768]{1,0:T(8,128)(2,1)}, u32[]{:S(2)}) copy-start(bf16[1536,768]{1,0:T(8,128)(2,1)} %all-gather.8.cloned.1.call-done) | copy-start | bytes 7077892
  189.4 13.4 %copy-start.5 = (bf16[3,192,768]{2,1,0:T(8,128)(2,1)S(1)}, bf16[3,192,768]{2,1,0:T(8,128)(2,1)}, u32[]{:S(2)}) copy-start(bf16[3,192,768]{2,1,0:T(8,128)(2,1)} %copy-done.4) | copy-start | bytes 2654212
  189.4 13.4 %copy-start.6 = (bf16[768,768]{1,0:T(8,128)(2,1)S(1)}, bf16[768,768]{1,0:T(8,128)(2,1)}, u32[]{:S(2)}) copy-start(bf16[768,768]{1,0:T(8,128)(2,1)} %all-gather.4.cloned.1.call-done) | copy-start | bytes 3538948
  189.4 13.4 %copy-start.20 = (s32[5]{0:T(128)S(1)}, s32[5]{0:T(128)}, u32[]{:S(2)}) copy-start(s32[5]{0:T(128)} %copy-done.19) | copy-start | bytes 64
  189.5 13.4 %copy-start.22 = (f32[256]{0:T(256)S(1)}, f32[256]{0:T(256)}, u32[]{:S(2)}) copy-start(f32[256]{0:T(256)} %param.17) | copy-start | bytes 3076
  189.5 13.4 %copy-start.23 = (f32[256]{0:T(256)S(1)}, f32[256]{0:T(256)}, u32[]{:S(2)}) copy-start(f32[256]{0:T(256)} %param.18) | copy-start | bytes 3076
  202.9 1.1 copy-start.7
  204.0 0.9 copy-start.18
  223.5 0.9 copy-start.16
  224.3 4.3 %copy-start.15 = (bf16[1552,256]{1,0:T(8,128)(2,1)}, bf16[1552,256]{1,0:T(8,128)(2,1)S(1)}, u32[]{:S(2)}) copy-start(bf16[1552,256]{1,0:T(8,128)(2,1)S(1)} %get-tuple-element.16) | copy-start | bytes 2383876
  224.3 4.4 %collective-permute-start.17 = (bf16[1552,256]{1,0:T(8,128)(2,1)S(1)}, bf16[1552,256]{1,0:T(8,128)(2,1)S(1)}, u32[]{:S(2)}, u32[]{:S(2)}) collective-permute-start(bf16[1552,256]{1,0:T(8,128)(2,1)S(1)} %get-tuple-element.17), channel_id=1, source_target_pairs={{0,1},{1,0},{2,3},{3,2},{4,5},{5,4},{6,7},{7,6},{8,9},{9,8},{10,11... | collective-permute-start | bytes 2383880 | tf_op jit(solution)/shard_map/ppermute | solution.py:398
  226.2 10.7 %collective-permute-start.16 = (bf16[1536,256]{1,0:T(8,128)(2,1)}, bf16[1536,256]{1,0:T(8,128)(2,1)S(1)}, u32[]{:S(2)}, u32[]{:S(2)}) collective-permute-start(bf16[1536,256]{1,0:T(8,128)(2,1)} %get-tuple-element.15), channel_id=1, source_target_pairs={{0,1},{1,0},{2,3},{3,2},{4,5},{5,4},{6,7},{7,6},{8,9},{9,8},{10,11... | collective-permute-start | bytes 2359304 | tf_op jit(solution)/shard_map/ppermute | solution.py:403
  231.2 5.7 %copy-start.17 = (bf16[1536,256]{1,0:T(8,128)(2,1)S(1)}, bf16[1536,256]{1,0:T(8,128)(2,1)}, u32[]{:S(2)}) copy-start(bf16[1536,256]{1,0:T(8,128)(2,1)} %copy-done.16) | copy-start | bytes 2359300
  231.2 16.3 %all-to-all-start.2 = ((bf16[4,400,256]{2,1,0:T(8,128)(2,1)}), bf16[4,400,256]{2,1,0:T(8,128)(2,1)S(1)}, u32[]{:S(2)}, u32[]{:S(2)}) async-start(bf16[4,400,256]{2,1,0:T(8,128)(2,1)} %pad_maximum_fusion.2), calls=%async_computation.2 | async-start | bytes 1638400 | tf_op jit(solution)/shard_map/all_to_all | solution.py:402
  247.6 15.0 %all-to-all-start.1 = ((bf16[4,384,256]{2,1,0:T(8,128)(2,1)}), bf16[4,384,256]{2,1,0:T(8,128)(2,1)S(1)}, u32[]{:S(2)}, u32[]{:S(2)}) async-start(bf16[4,384,256]{2,1,0:T(8,128)(2,1)} %bitcast.32), calls=%async_computation.1 | async-start | bytes 1572864 | tf_op jit(solution)/shard_map/all_to_all | solution.py:405
  252.5 29.1 %copy-start.27 = (bf16[128,256]{1,0:T(8,128)(2,1)S(1)}, bf16[128,256]{1,0:T(8,128)(2,1)}, u32[]{:S(2)}) copy-start(bf16[128,256]{1,0:T(8,128)(2,1)} %copy-done.26) | copy-start | bytes 196612
  252.6 29.1 %copy-start.29 = (bf16[128,256]{1,0:T(8,128)(2,1)S(1)}, bf16[128,256]{1,0:T(8,128)(2,1)}, u32[]{:S(2)}) copy-start(bf16[128,256]{1,0:T(8,128)(2,1)} %copy-done.28) | copy-start | bytes 196612
  252.9 28.7 %collective-permute-start.18 = (bf16[400,256]{1,0:T(8,128)(2,1)S(1)}, bf16[400,256]{1,0:T(8,128)(2,1)S(1)}, u32[]{:S(2)}, u32[]{:S(2)}) collective-permute-start(bf16[400,256]{1,0:T(8,128)(2,1)S(1)} %concatenate.47), channel_id=1, source_target_pairs={{0,2},{2,0},{1,3},{3,1},{4,6},{6,4},{5,7},{7,5},{8,10},{10,8},{9,1... | collective-permute-start | bytes 614408 | tf_op jit(solution)/shard_map/ppermute | solution.py:408
Sparse Core Ops, SparseCore 0:
  10.8 36.3 all-gather.3
  60.1 41.8 all-gather.5
  113.8 51.3 all-gather.7
